TPU v7x, 32 devices: a whole 2x2x4 slice. The times are simulated.
32 devices in a mesh: shard: 2 (over x), context: 4 (over z), tensor: 4 (over y, core).
Axes of the slice: x: 2, y: 2, z: 4, core: 2. Of those that a mesh axis runs over, the one named last changes fastest.
Arguments:
- tokens_in: bfloat16 [6, 1536, 1024], P('shard', 'context'), may hold values from -70 to 70
- counts: int32 [6], P('shard'), may hold values from 512 to 1536, as said below
- w_qkv: bfloat16 [1024, 3, 1024], P(('shard', 'context'), None, 'tensor'), may hold values from -0.1875 to 0.1875
- b_qv: bfloat16 [2, 16, 64], P(None, 'tensor', ('shard', 'context')), may hold values from -3 to 3
- w_out: bfloat16 [1024, 1024], P('tensor', ('shard', 'context')), may hold values from -0.5 to 0.5
- b_out: bfloat16 [1024], P(('shard', 'context')), may hold values from -3 to 3
- w_up: bfloat16 [1024, 4096], P(('shard', 'context'), 'tensor'), may hold values from -0.1875 to 0.1875
- b_up: bfloat16 [64, 64], P('tensor', ('shard', 'context')), may hold values from -3 to 3
- w_down: bfloat16 [4096, 1024], P('tensor', ('shard', 'context')), may hold values from -0.09375 to 0.09375
- b_down: bfloat16 [1024], P(('shard', 'context')), may hold values from -3 to 3
- norm1_gain: bfloat16 [1024], P(('shard', 'context')), may hold values from 0.25 to 1.75
- norm1_bias: bfloat16 [1024], P(('shard', 'context')), may hold values from -3 to 3
- norm2_gain: bfloat16 [1024], P(('shard', 'context')), may hold values from 0.25 to 1.75
- norm2_bias: bfloat16 [1024], P(('shard', 'context')), may hold values from -3 to 3
- scale1: bfloat16 [1024], P(('shard', 'context')), may hold values from 0.29882812 to 1.5
- scale2: bfloat16 [1024], P(('shard', 'context')), may hold values from 0.29882812 to 1.5
- cotangent: bfloat16 [6, 1536, 1024], P('shard', 'context'), may hold values from -6 to 6
Outputs:
- output: float32 [6, 1536, 1024], P('shard', 'context')
- input_grad: float32 [6, 1536, 1024], P('shard', 'context')
- g_w_qkv: float32 [1024, 3, 1024], P(('shard', 'context'), None, 'tensor')
- g_b_qv: float32 [2, 16, 64], P(None, 'tensor', ('shard', 'context'))
- g_w_out: float32 [1024, 1024], P('tensor', ('shard', 'context'))
- g_b_out: float32 [1024], P(('shard', 'context'))
- g_w_up: float32 [1024, 4096], P(('shard', 'context'), 'tensor')
- g_b_up: float32 [64, 64], P('tensor', ('shard', 'context'))
- g_w_down: float32 [4096, 1024], P('tensor', ('shard', 'context'))
- g_b_down: float32 [1024], P(('shard', 'context'))
- g_norm1_gain: float32 [1024], P(('shard', 'context'))
- g_norm1_bias: float32 [1024], P(('shard', 'context'))
- g_norm2_gain: float32 [1024], P(('shard', 'context'))
- g_norm2_bias: float32 [1024], P(('shard', 'context'))
- g_scale1: float32 [1024], P(('shard', 'context'))
- g_scale2: float32 [1024], P(('shard', 'context'))
Inputs may be any that keep to these rules, and one draw needn't show every extreme that they name: Image i has counts[i] real tokens in its first slots, the rest are padding that is masked as keys; some image fills all 1536 slots.
All inputs are finite; a program needn't handle non-finite values.
Results may differ from a plain program's by a relative error of at most 0.015.
Values may be sent and summed in bfloat16 or wider, within the bound.
No kernel may reach another device: no remote copies, remote signals or barrier semaphores. Data moves between devices by JAX's collectives and lax.ppermute only.
A program may use at most 128 MiB of HBM per device.

v0:
```python
import jax
import jax.numpy as jnp
from jax import lax
from jax.sharding import PartitionSpec as P

HD = 64


eps_norm = 1e-06
masked_score = -1e30
root_half = 0.7071067811865476
inv_root_two_pi = 0.3989422804014327


def layer_norm(values, norm_gain, norm_shift):
    average = jnp.mean(values, axis=-1, keepdims=True)
    centred = values - average
    variance = jnp.mean(centred * centred, axis=-1, keepdims=True)
    inv_std = lax.rsqrt(variance + eps_norm)
    normed = centred * inv_std
    return (normed * norm_gain + norm_shift, normed, inv_std)


def norm_back(grad_in, normed, inv_std):
    first_mean = jnp.mean(grad_in, axis=-1, keepdims=True)
    second_mean = jnp.mean(grad_in * normed, axis=-1, keepdims=True)
    return inv_std * (grad_in - first_mean - normed * second_mean)


def gelu_exact(values):
    return 0.5 * values * (1.0 + lax.erf(values * root_half))


def gelu_slope(values):
    return 0.5 * (1.0 + lax.erf(values * root_half)) + values * inv_root_two_pi * jnp.exp(
        -0.5 * values * values
    )


def split_heads(packed):
    length = packed.shape[0]
    head_count = packed.shape[2] // HD
    return (
        packed[:, 0].reshape(length, head_count, HD),
        packed[:, 1].reshape(length, head_count, HD),
        packed[:, 2].reshape(length, head_count, HD),
    )


def attend_image(packed, image_count):
    queries, key_rows, value_rows = split_heads(packed)
    length, head_count = (queries.shape[0], queries.shape[1])
    block_rows = min(512, length)
    key_valid = jnp.arange(length) < image_count
    score_scale = HD ** (-0.5)

    def attend_one_block(query_block):
        scores = (
            jnp.einsum("qhd,khd->hqk", query_block, key_rows, preferred_element_type=jnp.float32)
            * score_scale
        )
        scores = jnp.where(key_valid[None, None, :], scores, masked_score)
        highest = jnp.max(scores, axis=2, keepdims=True)
        exponent = jnp.exp(scores - highest)
        denominator = jnp.sum(exponent, axis=2, keepdims=True)
        weights_low = (exponent / denominator).astype(jnp.bfloat16)
        mixture = jnp.einsum(
            "hqk,khd->qhd", weights_low, value_rows, preferred_element_type=jnp.float32
        )
        return (mixture.astype(jnp.bfloat16), (highest + jnp.log(denominator))[:, :, 0])

    mixture, log_total = lax.map(
        attend_one_block, queries.reshape(length // block_rows, block_rows, head_count, HD)
    )
    return (mixture.reshape(length, head_count * HD), log_total)


def attend_item(item_inputs):
    return attend_image(item_inputs[0], item_inputs[1])


def backward_image(packed, mixture, mixture_grad, log_total, image_count):
    queries, key_rows, value_rows = split_heads(packed)
    length, head_count = (queries.shape[0], queries.shape[1])
    block_rows = min(512, length)
    blocks = length // block_rows
    key_valid = jnp.arange(length) < image_count
    score_scale = HD ** (-0.5)
    grad_heads = mixture_grad.reshape(length, head_count, HD)
    delta_sum = jnp.sum(
        mixture.reshape(length, head_count, HD).astype(jnp.float32)
        * grad_heads.astype(jnp.float32),
        axis=2,
    )

    def backward_one_block(running, block_in):
        key_grad, value_grad = running
        query_block, grad_block, log_block, delta_block = block_in
        scores = (
            jnp.einsum("qhd,khd->hqk", query_block, key_rows, preferred_element_type=jnp.float32)
            * score_scale
        )
        scores = jnp.where(key_valid[None, None, :], scores, masked_score)
        probs = jnp.exp(scores - log_block[:, :, None])
        probs_low = probs.astype(jnp.bfloat16)
        value_grad = value_grad + jnp.einsum(
            "hqk,qhd->khd", probs_low, grad_block, preferred_element_type=jnp.float32
        )
        weight_grad = jnp.einsum(
            "qhd,khd->hqk", grad_block, value_rows, preferred_element_type=jnp.float32
        )
        score_grad = (probs * (weight_grad - jnp.transpose(delta_block)[:, :, None])).astype(
            jnp.bfloat16
        )
        query_grad = (
            jnp.einsum("hqk,khd->qhd", score_grad, key_rows, preferred_element_type=jnp.float32)
            * score_scale
        ).astype(jnp.bfloat16)
        key_grad = (
            key_grad
            + jnp.einsum(
                "hqk,qhd->khd", score_grad, query_block, preferred_element_type=jnp.float32
            )
            * score_scale
        )
        return ((key_grad, value_grad), query_grad)

    zero_grad = jnp.zeros((length, head_count, HD), jnp.float32)
    block_inputs = (
        queries.reshape(blocks, block_rows, head_count, HD),
        grad_heads.reshape(blocks, block_rows, head_count, HD),
        log_total,
        delta_sum.reshape(blocks, block_rows, head_count),
    )
    (key_grad, value_grad), query_grads = lax.scan(
        backward_one_block, (zero_grad, zero_grad), block_inputs
    )
    return jnp.stack(
        [
            query_grads.reshape(length, head_count * HD),
            key_grad.astype(jnp.bfloat16).reshape(length, head_count * HD),
            value_grad.astype(jnp.bfloat16).reshape(length, head_count * HD),
        ],
        axis=1,
    )


def backward_item(item_inputs):
    return backward_image(
        item_inputs[0], item_inputs[1], item_inputs[2], item_inputs[3], item_inputs[4]
    )


def per_device(
    tokens_in,
    counts,
    w_qkv,
    b_qv,
    w_out,
    b_out,
    w_up,
    b_up,
    w_down,
    b_down,
    norm1_gain,
    norm1_bias,
    norm2_gain,
    norm2_bias,
    scale1,
    scale2,
    cotangent,
):
    images, row_count, model_width = tokens_in.shape
    token_count = images * row_count
    fetched = (
        lax.all_gather(w_qkv, ("shard", "context"), axis=0, tiled=True),
        lax.all_gather(b_qv, ("shard", "context"), axis=2, tiled=True),
        lax.all_gather(w_out, ("shard", "context"), axis=1, tiled=True),
        lax.all_gather(b_out, ("shard", "context"), axis=0, tiled=True),
        lax.all_gather(w_up, ("shard", "context"), axis=0, tiled=True),
        lax.all_gather(b_up, ("shard", "context"), axis=1, tiled=True),
        lax.all_gather(w_down, ("shard", "context"), axis=1, tiled=True),
        lax.all_gather(b_down, ("shard", "context"), axis=0, tiled=True),
        lax.all_gather(norm1_gain, ("shard", "context"), axis=0, tiled=True),
        lax.all_gather(norm1_bias, ("shard", "context"), axis=0, tiled=True),
        lax.all_gather(norm2_gain, ("shard", "context"), axis=0, tiled=True),
        lax.all_gather(norm2_bias, ("shard", "context"), axis=0, tiled=True),
        lax.all_gather(scale1, ("shard", "context"), axis=0, tiled=True),
        lax.all_gather(scale2, ("shard", "context"), axis=0, tiled=True),
    )
    (
        wqkv_all,
        bqv_all,
        wout_all,
        bout_all,
        wup_all,
        bup_all,
        wdown_all,
        bdown_all,
        gain_one,
        bias_one,
        gain_two,
        bias_two,
        layer_scale1,
        layer_scale2,
    ) = fetched
    columns = wqkv_all.shape[2]
    residual_in = tokens_in.astype(jnp.float32).reshape(token_count, model_width)
    norm_out1, normed1, inv_std1 = layer_norm(
        residual_in, gain_one.astype(jnp.float32), bias_one.astype(jnp.float32)
    )
    norm_low1 = norm_out1.astype(jnp.bfloat16)
    bias_rows = bqv_all.astype(jnp.float32).reshape(2, columns)
    qkv_bias = jnp.stack([bias_rows[0], jnp.zeros_like(bias_rows[0]), bias_rows[1]])
    projected = (
        jnp.dot(
            norm_low1,
            wqkv_all.reshape(model_width, 3 * columns),
            preferred_element_type=jnp.float32,
        ).reshape(token_count, 3, columns)
        + qkv_bias
    )
    packed_local = projected.astype(jnp.bfloat16).reshape(images, row_count, 3, columns)
    packed_full = lax.all_to_all(packed_local, "context", split_axis=3, concat_axis=1, tiled=True)
    mixture_full, log_totals = lax.map(attend_item, (packed_full, counts))
    mixture_local = lax.all_to_all(mixture_full, "context", split_axis=1, concat_axis=2, tiled=True)
    attention_low = mixture_local.reshape(token_count, columns)
    proj_sum = lax.psum(
        jnp.dot(attention_low, wout_all, preferred_element_type=jnp.float32).astype(jnp.bfloat16),
        "tensor",
    ).astype(jnp.float32)
    attn_branch = proj_sum + bout_all.astype(jnp.float32)
    middle = residual_in + layer_scale1.astype(jnp.float32) * attn_branch
    norm_out2, normed2, inv_std2 = layer_norm(
        middle, gain_two.astype(jnp.float32), bias_two.astype(jnp.float32)
    )
    norm_low2 = norm_out2.astype(jnp.bfloat16)
    hidden_pre = jnp.dot(norm_low2, wup_all, preferred_element_type=jnp.float32) + bup_all.astype(
        jnp.float32
    ).reshape(-1)
    hidden_act = gelu_exact(hidden_pre).astype(jnp.bfloat16)
    down_sum = lax.psum(
        jnp.dot(hidden_act, wdown_all, preferred_element_type=jnp.float32).astype(jnp.bfloat16),
        "tensor",
    ).astype(jnp.float32)
    mlp_branch = down_sum + bdown_all.astype(jnp.float32)
    result = middle + layer_scale2.astype(jnp.float32) * mlp_branch
    (
        wqkv_back,
        wout_back,
        wup_back,
        wdown_back,
        gain_one_back,
        gain_two_back,
        scale1_back,
        scale2_back,
    ) = (wqkv_all, wout_all, wup_all, wdown_all, gain_one, gain_two, layer_scale1, layer_scale2)
    upstream = cotangent.astype(jnp.float32).reshape(token_count, model_width)
    grad_scale2 = jnp.sum(upstream * mlp_branch, axis=0)
    branch_wide = scale2_back.astype(jnp.float32) * upstream
    grad_bdown = jnp.sum(branch_wide, axis=0)
    branch_grad = branch_wide.astype(jnp.bfloat16)
    grad_wdown = jnp.dot(hidden_act.T, branch_grad, preferred_element_type=jnp.float32)
    pre_grad = (
        jnp.dot(branch_grad, wdown_back.T, preferred_element_type=jnp.float32)
        * gelu_slope(hidden_pre)
    ).astype(jnp.bfloat16)
    grad_wup = jnp.dot(norm_low2.T, pre_grad, preferred_element_type=jnp.float32)
    grad_bup = jnp.sum(pre_grad.astype(jnp.float32), axis=0).reshape(bup_all.shape)
    norm2_grad = lax.psum(
        jnp.dot(pre_grad, wup_back.T, preferred_element_type=jnp.float32).astype(jnp.bfloat16),
        "tensor",
    ).astype(jnp.float32)
    grad_gain2 = jnp.sum(norm2_grad * normed2, axis=0)
    grad_bias2 = jnp.sum(norm2_grad, axis=0)
    middle_grad = upstream + norm_back(
        norm2_grad * gain_two_back.astype(jnp.float32), normed2, inv_std2
    )
    grad_scale1 = jnp.sum(middle_grad * attn_branch, axis=0)
    proj_wide = scale1_back.astype(jnp.float32) * middle_grad
    grad_bout = jnp.sum(proj_wide, axis=0)
    proj_grad = proj_wide.astype(jnp.bfloat16)
    grad_wout = jnp.dot(attention_low.T, proj_grad, preferred_element_type=jnp.float32)
    mixture_grad_local = (
        jnp.dot(proj_grad, wout_back.T, preferred_element_type=jnp.float32)
        .astype(jnp.bfloat16)
        .reshape(images, row_count, columns)
    )
    mixture_grad_full = lax.all_to_all(
        mixture_grad_local, "context", split_axis=2, concat_axis=1, tiled=True
    )
    qkv_grad_full = lax.map(
        backward_item, (packed_full, mixture_full, mixture_grad_full, log_totals, counts)
    )
    qkv_grad_local = lax.all_to_all(
        qkv_grad_full, "context", split_axis=1, concat_axis=3, tiled=True
    )
    qkv_grad = qkv_grad_local.reshape(token_count, 3 * columns)
    grad_wqkv = jnp.dot(norm_low1.T, qkv_grad, preferred_element_type=jnp.float32).reshape(
        model_width, 3, columns
    )
    summed_qkv = jnp.sum(
        qkv_grad_local.reshape(token_count, 3, columns).astype(jnp.float32), axis=0
    )
    grad_bqv = jnp.stack([summed_qkv[0], summed_qkv[2]]).reshape(bqv_all.shape)
    norm1_grad = lax.psum(
        jnp.dot(
            qkv_grad,
            wqkv_back.reshape(model_width, 3 * columns).T,
            preferred_element_type=jnp.float32,
        ).astype(jnp.bfloat16),
        "tensor",
    ).astype(jnp.float32)
    grad_gain1 = jnp.sum(norm1_grad * normed1, axis=0)
    grad_bias1 = jnp.sum(norm1_grad, axis=0)
    input_grad = middle_grad + norm_back(
        norm1_grad * gain_one_back.astype(jnp.float32), normed1, inv_std1
    )
    shares = (
        lax.psum_scatter(grad_wqkv, ("shard", "context"), scatter_dimension=0, tiled=True),
        lax.psum_scatter(grad_bqv, ("shard", "context"), scatter_dimension=2, tiled=True),
        lax.psum_scatter(grad_wout, ("shard", "context"), scatter_dimension=1, tiled=True),
        lax.psum_scatter(grad_bout, ("shard", "context"), scatter_dimension=0, tiled=True),
        lax.psum_scatter(grad_wup, ("shard", "context"), scatter_dimension=0, tiled=True),
        lax.psum_scatter(grad_bup, ("shard", "context"), scatter_dimension=1, tiled=True),
        lax.psum_scatter(grad_wdown, ("shard", "context"), scatter_dimension=1, tiled=True),
        lax.psum_scatter(grad_bdown, ("shard", "context"), scatter_dimension=0, tiled=True),
        lax.psum_scatter(grad_gain1, ("shard", "context"), scatter_dimension=0, tiled=True),
        lax.psum_scatter(grad_bias1, ("shard", "context"), scatter_dimension=0, tiled=True),
        lax.psum_scatter(grad_gain2, ("shard", "context"), scatter_dimension=0, tiled=True),
        lax.psum_scatter(grad_bias2, ("shard", "context"), scatter_dimension=0, tiled=True),
        lax.psum_scatter(grad_scale1, ("shard", "context"), scatter_dimension=0, tiled=True),
        lax.psum_scatter(grad_scale2, ("shard", "context"), scatter_dimension=0, tiled=True),
    )
    return (
        result.reshape(images, row_count, model_width),
        input_grad.reshape(images, row_count, model_width),
        shares[0],
        shares[1],
        shares[2],
        shares[3],
        shares[4],
        shares[5],
        shares[6],
        shares[7],
        shares[8],
        shares[9],
        shares[10],
        shares[11],
        shares[12],
        shares[13],
    )


def solution(mesh):
    in_specs = (
        P("shard", "context", None),
        P("shard"),
        P(("shard", "context"), None, "tensor"),
        P(None, "tensor", ("shard", "context")),
        P("tensor", ("shard", "context")),
        P(("shard", "context")),
        P(("shard", "context"), "tensor"),
        P("tensor", ("shard", "context")),
        P("tensor", ("shard", "context")),
        P(("shard", "context")),
        P(("shard", "context")),
        P(("shard", "context")),
        P(("shard", "context")),
        P(("shard", "context")),
        P(("shard", "context")),
        P(("shard", "context")),
        P("shard", "context", None),
    )
    out_specs = (
        P("shard", "context", None),
        P("shard", "context", None),
        P(("shard", "context"), None, "tensor"),
        P(None, "tensor", ("shard", "context")),
        P("tensor", ("shard", "context")),
        P(("shard", "context")),
        P(("shard", "context"), "tensor"),
        P("tensor", ("shard", "context")),
        P("tensor", ("shard", "context")),
        P(("shard", "context")),
        P(("shard", "context")),
        P(("shard", "context")),
        P(("shard", "context")),
        P(("shard", "context")),
        P(("shard", "context")),
        P(("shard", "context")),
    )
    return jax.shard_map(
        per_device, mesh=mesh, in_specs=in_specs, out_specs=out_specs, check_vma=False
    )
```

profile of v0, /device:TPU:0, one launch (start us, length us, event | category | flops | bytes accessed | tf_op | source)
XLA Modules:
  0.0 1033.3 jit_solution(17537131350694759622)
XLA Ops:
  9.9 22.4 %all-gather.1 = bf16[8,1,128]{2,1,0:T(2,128)(2,1)S(1)} all-gather(bf16[1,1,128]{2,1,0:T(2,128)(2,1)} %bitcast.347), channel_id=1, replica_groups=mesh['shard'=2,'context'=4,'tensor'=4] {'shard','context'}, dimensions={0}, use_global_device_ids=true | all-gather | bytes 2304 | tf_op jit(solution)/shard_map/all_gather | solution.py:184
  32.4 16.8 %all-gather.2 = bf16[8,1,128]{2,1,0:T(2,128)(2,1)S(1)} all-gather(bf16[1,1,128]{2,1,0:T(2,128)(2,1)} %bitcast.348), channel_id=1, replica_groups=mesh['shard'=2,'context'=4,'tensor'=4] {'shard','context'}, dimensions={0}, use_global_device_ids=true | all-gather | bytes 2304 | tf_op jit(solution)/shard_map/all_gather | solution.py:185
  49.2 30.6 %all_gather.46 = bf16[2,4,64]{1,0,2:T(2,128)(2,1)S(1)} all-gather(bf16[2,4,8]{1,0,2:T(2,128)(2,1)S(1)} %copy.140), channel_id=1, replica_groups=mesh['shard'=2,'context'=4,'tensor'=4] {'shard','context'}, dimensions={2}, use_global_device_ids=true | all-gather | bytes 1152 | tf_op jit(solution)/shard_map/all_gather | solution.py:177
  80.3 2.1 convert_reduce_fusion.2
  83.2 2.4 fusion.70
  85.6 4.2 fusion.74
  89.8 3.3 copy.143
  93.1 3.6 all-to-all-start
  96.8 40.5 %all-to-all-done = bf16[3,384,3,256]{1,2,0,3:T(4,128)(2,1)S(1)} async-done(((bf16[3,384,3,256]{1,2,0,3:T(4,128)(2,1)}), bf16[3,384,3,256]{1,2,0,3:T(4,128)(2,1)S(1)}, u32[]{:S(2)}, u32[]{:S(2)}) %all-to-all-start) | async-done | bytes 1769504 | tf_op jit(solution)/shard_map/all_to_all | solution.py:224
  137.8 30.9 %while.51 = (s32[]{:T(128)}, bf16[3,1536,64]{2,1,0:T(8,128)(2,1)}, f32[3,3,1,512]{3,2,1,0:T(1,128)S(1)}, bf16[3,1536,3,64]{1,3,2,0:T(8,128)(2,1)S(1)}, s32[3]{0:T(128)S(1)}, /*index=5*/s32[]{:T(128)}, s32[]{:T(128)}, s32[]{:T(128)}) while((s32[]{:T(128)}, bf16[3,1536,64]{2,1,0:T(8,128)(2,1)}, f32[3,3,1,512]{3,2,1,0:T(1,128)S(1)}, ...), condition=%wide.region_7.8_spmd, body=%wide.region_2.7_spmd.sunk | while | flops 207651840 | bytes 13733674 | solution.py:225
  138.5 8.5 while.54
  148.8 8.5 while.54
  159.1 8.5 while.54
  168.7 7.6 copy.175
  176.3 2.2 reshape.415
  178.5 3.5 all-to-all-start.1
  182.0 33.7 %all_gather.47 = bf16[256,1024]{1,0:T(8,128)(2,1)S(1)} all-gather(bf16[256,128]{1,0:T(8,128)(2,1)S(1)} %copy-done.25), channel_id=1, replica_groups=mesh['shard'=2,'context'=4,'tensor'=4] {'shard','context'}, dimensions={1}, use_global_device_ids=true | all-gather | bytes 589824 | tf_op jit(solution)/shard_map/all_gather | solution.py:178
  218.7 2.2 convolution_convert_fusion.3
  222.4 16.3 %all-gather.3 = bf16[8,1,128]{2,1,0:T(2,128)(2,1)S(1)} all-gather(bf16[1,1,128]{2,1,0:T(2,128)(2,1)S(1)} %bitcast.349), channel_id=1, replica_groups=mesh['shard'=2,'context'=4,'tensor'=4] {'shard','context'}, dimensions={0}, use_global_device_ids=true | all-gather | bytes 2304 | tf_op jit(solution)/shard_map/all_gather | solution.py:179
  238.6 18.3 %all-gather.5 = bf16[8,1,128]{2,1,0:T(2,128)(2,1)S(1)} all-gather(bf16[1,1,128]{2,1,0:T(2,128)(2,1)S(1)} %bitcast.350), channel_id=1, replica_groups=mesh['shard'=2,'context'=4,'tensor'=4] {'shard','context'}, dimensions={0}, use_global_device_ids=true | all-gather | bytes 2304 | tf_op jit(solution)/shard_map/all_gather | solution.py:186
  256.9 16.3 %all-gather.6 = bf16[8,1,128]{2,1,0:T(2,128)(2,1)S(1)} all-gather(bf16[1,1,128]{2,1,0:T(2,128)(2,1)S(1)} %bitcast.351), channel_id=1, replica_groups=mesh['shard'=2,'context'=4,'tensor'=4] {'shard','context'}, dimensions={0}, use_global_device_ids=true | all-gather | bytes 2304 | tf_op jit(solution)/shard_map/all_gather | solution.py:187
  273.2 18.3 %all-gather = bf16[8,1,128]{2,1,0:T(2,128)(2,1)S(1)} all-gather(bf16[1,1,128]{2,1,0:T(2,128)(2,1)S(1)} %bitcast.352), channel_id=1, replica_groups=mesh['shard'=2,'context'=4,'tensor'=4] {'shard','context'}, dimensions={0}, use_global_device_ids=true | all-gather | bytes 2304 | tf_op jit(solution)/shard_map/all_gather | solution.py:188
  291.5 16.3 %all-gather.4 = bf16[8,1,128]{2,1,0:T(2,128)(2,1)S(1)} all-gather(bf16[1,1,128]{2,1,0:T(2,128)(2,1)S(1)} %bitcast.353), channel_id=1, replica_groups=mesh['shard'=2,'context'=4,'tensor'=4] {'shard','context'}, dimensions={0}, use_global_device_ids=true | all-gather | bytes 2304 | tf_op jit(solution)/shard_map/all_gather | solution.py:189
  307.9 28.0 %all_gather.53 = bf16[16,64]{0,1:T(8,128)(2,1)S(1)} all-gather(bf16[16,8]{0,1:T(8,128)(2,1)S(1)} %copy-done.37), channel_id=1, replica_groups=mesh['shard'=2,'context'=4,'tensor'=4] {'shard','context'}, dimensions={1}, use_global_device_ids=true | all-gather | bytes 2304 | tf_op jit(solution)/shard_map/all_gather | solution.py:181
  336.0 3.8 fusion.63
  339.8 2.8 fusion.77
  343.9 2.9 add_convert_fusion
  346.9 8.3 multiply_convert_fusion
  355.2 22.1 %all-gather.16.cloned.1.call-done = bf16[1024,1024]{1,0:T(8,128)(2,1)} async-done(((bf16[1024,128]{1,0:T(8,128)(2,1)}), bf16[1024,1024]{1,0:T(8,128)(2,1)}) %all-gather.16.cloned.1.call-update) | async-done | bytes 2097168 | tf_op jit(solution)/shard_map/all_gather | solution.py:182
  377.3 7.9 convert_reduce_fusion.3
  386.6 3.9 convolution_convert_fusion.1
  390.5 54.0 %all-reduce.18.cloned.1.call-done = bf16[1152,1024]{1,0:T(8,128)(2,1)} async-done(((bf16[1152,1024]{1,0:T(8,128)(2,1)}), bf16[1152,1024]{1,0:T(8,128)(2,1)}) %all-reduce.18.cloned.1.call-update) | async-done | bytes 2359312 | tf_op jit(solution)/shard_map/psum | solution.py:270
  444.5 6.0 fusion.60
  450.6 4.1 multiply_reduce_fusion.1
  454.7 2.2 copy-done.6
  459.0 4.6 all-to-all-start.2
  464.2 19.3 %all-to-all-done.2 = bf16[3,384,256]{1,0,2:T(4,128)(2,1)S(1)} async-done(((bf16[3,384,256]{1,0,2:T(4,128)(2,1)}), bf16[3,384,256]{1,0,2:T(4,128)(2,1)S(1)}, u32[]{:S(2)}, u32[]{:S(2)}) %all-to-all-start.2) | async-done | bytes 589856 | tf_op jit(solution)/shard_map/all_to_all | solution.py:289
  483.6 41.5 %while.53 = (s32[]{:T(128)}, bf16[3,1536,3,64]{1,3,2,0:T(8,128)(2,1)}, bf16[3,1536,3,64]{1,3,2,0:T(8,128)(2,1)}, bf16[3,1536,64]{1,2,0:T(8,128)(2,1)S(1)}, f32[3...) while((s32[]{:T(128)}, ...), condition=%wide.region_19.20_spmd, body=%wide.region_15.19_spmd.sunk | while | flops 511737856 | bytes 23771060 | solution.py:292
  485.7 10.8 %while.55 = (s32[]{:T(128)}, f32[1536,1,64]{0,2,1:T(8,128)S(1)}, f32[1536,1,64]{0,2,1:T(8,128)S(1)}, bf16[3,512,1,64]{1,3,2,0:T(8,128)(2,1)S(1)}, bf16[3,512,1,6...) while((s32[]{:T(128)}, f32[1536,1,64]{0,2,1:T(8,128)S(1)}, ...), condition=%wide.region_18.18_spmd.clone, body=%wide.region_17.17_spmd.clone.sunk | while | flops 509380096 | bytes 16662192 | solution.py:135
  499.6 10.8 %while.55 = (s32[]{:T(128)}, f32[1536,1,64]{0,2,1:T(8,128)S(1)}, f32[1536,1,64]{0,2,1:T(8,128)S(1)}, bf16[3,512,1,64]{1,3,2,0:T(8,128)(2,1)S(1)}, bf16[3,512,1,6...) while((s32[]{:T(128)}, f32[1536,1,64]{0,2,1:T(8,128)S(1)}, ...), condition=%wide.region_18.18_spmd.clone, body=%wide.region_17.17_spmd.clone.sunk | while | flops 509380096 | bytes 16662192 | solution.py:135
  513.4 10.8 %while.55 = (s32[]{:T(128)}, f32[1536,1,64]{0,2,1:T(8,128)S(1)}, f32[1536,1,64]{0,2,1:T(8,128)S(1)}, bf16[3,512,1,64]{1,3,2,0:T(8,128)(2,1)S(1)}, bf16[3,512,1,6...) while((s32[]{:T(128)}, f32[1536,1,64]{0,2,1:T(8,128)S(1)}, ...), condition=%wide.region_18.18_spmd.clone, body=%wide.region_17.17_spmd.clone.sunk | while | flops 509380096 | bytes 16662192 | solution.py:135
  525.2 7.6 copy.153
  532.8 5.9 reshape.417
  538.7 3.6 all-to-all-start.3
  542.5 6.3 convolution_convert_fusion.2
  548.8 34.1 %all-to-all-done.3 = bf16[4,2,110592]{2,1,0:T(2,128)(2,1)S(1)} async-done(((bf16[4,2,110592]{2,1,0:T(2,128)(2,1)}), bf16[4,2,110592]{2,1,0:T(2,128)(2,1)S(1)}, u32[]{:S(2)}, u32[]{:S(2)}) %all-to-all-start.3) | async-done | bytes 1769504 | tf_op jit(solution)/shard_map/all_to_all | solution.py:295
  583.0 4.1 reshape.418
  587.1 8.6 copy.154
  598.3 3.5 convolution_convert_fusion
  602.8 4.2 fusion.76
  607.1 6.1 fusion.85
  614.8 6.2 fusion.86
  622.8 5.4 fusion.84
  630.9 19.6 %all-gather.7 = bf16[8,1,128]{2,1,0:T(2,128)(2,1)S(1)} all-gather(bf16[1,1,128]{2,1,0:T(2,128)(2,1)S(1)} %bitcast.354), channel_id=1, replica_groups=mesh['shard'=2,'context'=4,'tensor'=4] {'shard','context'}, dimensions={0}, use_global_device_ids=true | all-gather | bytes 2304 | tf_op jit(solution)/shard_map/all_gather | solution.py:183
  650.5 2.2 fusion.62
  652.8 4.1 convert_reduce_fusion.4
  656.9 37.5 %all-reduce.20.cloned.1.call-done = (bf16[1152,1024]{1,0:T(8,128)(2,1)}, bf16[1152,1024]{1,0:T(8,128)(2,1)}) async-done(((bf16[1152,1024]{1,0:T(8,128)(2,1)}, bf16[1152,1024]{1,0:T(8,128)(2,1)}), (bf16[1152,1024]{1,0:T(8,128)(2,1)}, bf16[1152,1024]{1,0:T(8,128)(2,1)})) %all-reduce.20.cloned.1.call-update) | async-done | bytes 4718608 | tf_op jit(solution)/shard_map/psum | solution.py:242
  694.4 3.9 fusion.61
  698.3 10.0 fusion.64
  708.4 38.3 %all-reduce.10 = (f32[2,4,64]{2,1,0:T(4,128)S(1)}, f32[1024]{0:T(1024)S(1)}, f32[16,64]{1,0:T(8,128)S(1)}, f32[1024]{0:T(1024)S(1)}, f32[1024]{0:T(1024)S(1)}, /...) all-reduce(f32[2,4,64]{2,1,0:T(4,128)S(1)} %pad_maximum_fusion.1, ...), channel_id=3, replica_groups=mesh['shard'=2,'context'=4,'tensor'=4] {'shard','context'}, use_global_device_ids=true, to_apply=%region_25.26.clone | all-reduce | flops 9728 | bytes 77824
  752.7 10.8 %reduce-scatter.9.cloned.1.call-done = f32[256,128]{1,0:T(8,128)} async-done(((f32[256,1024]{1,0:T(8,128)}), f32[256,128]{1,0:T(8,128)}) %reduce-scatter.9.cloned.1.call-update) | async-done | bytes 131088 | tf_op jit(solution)/shard_map/reduce_scatter | solution.py:322
  763.5 91.5 %reduce-scatter.11.cloned.1.call-done = f32[128,1024]{1,0:T(8,128)} async-done(((f32[1024,1024]{1,0:T(8,128)}), f32[128,1024]{1,0:T(8,128)}) %reduce-scatter.11.cloned.1.call-update) | async-done | bytes 524304 | tf_op jit(solution)/shard_map/reduce_scatter | solution.py:324
  855.0 92.6 %reduce-scatter.13.cloned.1.call-done = f32[1024,128]{1,0:T(8,128)} async-done(((f32[1024,1024]{1,0:T(8,128)}), f32[1024,128]{1,0:T(8,128)}) %reduce-scatter.13.cloned.1.call-update) | async-done | bytes 524304 | tf_op jit(solution)/shard_map/reduce_scatter | solution.py:326
  947.6 78.4 %reduce-scatter.7.cloned.1.call-done = f32[128,3,256]{2,0,1:T(8,128)} async-done(((f32[1024,3,256]{2,0,1:T(8,128)}), f32[128,3,256]{2,0,1:T(8,128)}) %reduce-scatter.7.cloned.1.call-update) | async-done | bytes 393232 | tf_op jit(solution)/shard_map/reduce_scatter | solution.py:320
  (384 shorter events, 100.3 us)
Async XLA Ops:
  7.2 75.2 %copy-start = (bf16[3,384,1024]{2,1,0:T(8,128)(2,1)S(1)}, bf16[3,384,1024]{2,1,0:T(8,128)(2,1)}, u32[]{:S(2)}) copy-start(bf16[3,384,1024]{2,1,0:T(8,128)(2,1)} %param.25) | copy-start | bytes 7077892
  7.2 78.5 %all-gather.12.cloned.1.call-start = ((), (), s32[]{:S(2)}) async-start(), calls=%async_computation.8 | async-start | bytes 1769472 | tf_op jit(solution)/shard_map/all_gather | solution.py:176
  32.4 53.3 %copy-start.28 = (f32[8,1,128]{2,1,0:T(1,128)}, f32[8,1,128]{2,1,0:T(1,128)S(1)}, u32[]{:S(2)}) copy-start(f32[8,1,128]{2,1,0:T(1,128)S(1)} %convert_element_type.194) | copy-start | bytes 12292
  82.4 0.8 copy-start.23
  83.2 6.6 copy-start.30
  93.1 44.2 %all-to-all-start = ((bf16[3,384,3,256]{1,2,0,3:T(4,128)(2,1)}), bf16[3,384,3,256]{1,2,0,3:T(4,128)(2,1)S(1)}, u32[]{:S(2)}, u32[]{:S(2)}) async-start(bf16[3,384,3,256]{1,2,0,3:T(4,128)(2,1)} %copy.143), calls=%async_computation | async-start | bytes 4718592 | tf_op jit(solution)/shard_map/all_to_all | solution.py:224
  96.8 41.0 %copy-start.46 = (s32[3]{0:T(128)S(1)}, s32[3]{0:T(128)}, u32[]{:S(2)}) copy-start(s32[3]{0:T(128)} %param.26) | copy-start | bytes 40
  168.7 47.1 %copy-start.9 = (bf16[3,1536,3,64]{1,3,2,0:T(8,128)(2,1)}, bf16[3,1536,3,64]{1,3,2,0:T(8,128)(2,1)S(1)}, u32[]{:S(2)}) copy-start(bf16[3,1536,3,64]{1,3,2,0:T(8,128)(2,1)S(1)} %get-tuple-element.962) | copy-start | bytes 5308420
  168.7 13.4 %copy-start.25 = (bf16[256,128]{1,0:T(8,128)(2,1)S(1)}, bf16[256,128]{1,0:T(8,128)(2,1)}, u32[]{:S(2)}) copy-start(bf16[256,128]{1,0:T(8,128)(2,1)} %param.29) | copy-start | bytes 196612
  178.5 37.3 %all-to-all-start.1 = ((bf16[4,2,36864]{2,1,0:T(2,128)(2,1)}), bf16[4,2,36864]{2,1,0:T(2,128)(2,1)S(1)}, u32[]{:S(2)}, u32[]{:S(2)}) async-start(bf16[4,2,36864]{2,1,0:T(2,128)(2,1)} %reshape.415), calls=%async_computation.1 | async-start | bytes 1179648 | tf_op jit(solution)/shard_map/all_to_all | solution.py:226
  182.0 157.8 %all-reduce.16.cloned.1.call-start = ((), (), s32[]{:S(2)}) async-start(), calls=%async_computation.9 | async-start | bytes 4718592 | tf_op jit(solution)/shard_map/psum | solution.py:228
  217.9 0.8 copy-start.12
  218.7 3.7 copy-start.38
  218.7 20.0 %copy-start.39 = (bf16[128]{0:T(256)(128)(2,1)S(1)}, bf16[128]{0:T(256)(128)(2,1)}, u32[]{:S(2)}) copy-start(bf16[128]{0:T(256)(128)(2,1)} %param.37) | copy-start | bytes 772
  218.7 38.3 %copy-start.40 = (bf16[128]{0:T(256)(128)(2,1)S(1)}, bf16[128]{0:T(256)(128)(2,1)}, u32[]{:S(2)}) copy-start(bf16[128]{0:T(256)(128)(2,1)} %param.38) | copy-start | bytes 772
  218.7 54.5 %copy-start.41 = (bf16[128]{0:T(256)(128)(2,1)S(1)}, bf16[128]{0:T(256)(128)(2,1)}, u32[]{:S(2)}) copy-start(bf16[128]{0:T(256)(128)(2,1)} %param.39) | copy-start | bytes 772
  218.7 72.8 %copy-start.42 = (bf16[128]{0:T(256)(128)(2,1)S(1)}, bf16[128]{0:T(256)(128)(2,1)}, u32[]{:S(2)}) copy-start(bf16[128]{0:T(256)(128)(2,1)} %param.40) | copy-start | bytes 772
  218.7 89.1 %copy-start.37 = (bf16[16,8]{0,1:T(8,128)(2,1)S(1)}, bf16[16,8]{0,1:T(8,128)(2,1)}, u32[]{:S(2)}) copy-start(bf16[16,8]{0,1:T(8,128)(2,1)} %param.32) | copy-start | bytes 772
  221.0 118.8 %copy-start.1 = (bf16[3,384,1024]{2,1,0:T(8,128)(2,1)S(1)}, bf16[3,384,1024]{2,1,0:T(8,128)(2,1)}, u32[]{:S(2)}) copy-start(bf16[3,384,1024]{2,1,0:T(8,128)(2,1)} %param.25) | copy-start | bytes 7077892
  221.0 125.9 %all-gather.14.cloned.1.call-start = ((), (), s32[]{:S(2)}) async-start(), calls=%async_computation.10 | async-start | bytes 2359296 | tf_op jit(solution)/shard_map/all_gather | solution.py:180
  221.7 155.6 %all-gather.16.cloned.1.call-start = ((), (), s32[]{:S(2)}) async-start(), calls=%async_computation.11 | async-start | bytes 2359296 | tf_op jit(solution)/shard_map/all_gather | solution.py:182
  222.3 222.2 %all-reduce.18.cloned.1.call-start = ((), (), s32[]{:S(2)}) async-start(), calls=%async_computation.12 | async-start | bytes 4718592 | tf_op jit(solution)/shard_map/psum | solution.py:270
  238.6 211.9 %copy-start.21 = (f32[8,1,128]{2,1,0:T(1,128)}, f32[8,1,128]{2,1,0:T(1,128)S(1)}, u32[]{:S(2)}) copy-start(f32[8,1,128]{2,1,0:T(1,128)S(1)} %convert_element_type.196) | copy-start | bytes 12292
  291.5 163.2 %copy-start.19 = (f32[8,1,128]{2,1,0:T(1,128)}, f32[8,1,128]{2,1,0:T(1,128)S(1)}, u32[]{:S(2)}) copy-start(f32[8,1,128]{2,1,0:T(1,128)S(1)} %convert_element_type.193) | copy-start | bytes 12292
  307.9 31.9 %copy-start.26 = (f32[8,1,128]{2,1,0:T(1,128)}, f32[8,1,128]{2,1,0:T(1,128)S(1)}, u32[]{:S(2)}) copy-start(f32[8,1,128]{2,1,0:T(1,128)S(1)} %convert_element_type.197) | copy-start | bytes 12292
  339.8 2.8 copy-start.3
  377.3 9.3 copy-start.44
  385.2 1.4 copy-start.48
  444.5 6.1 copy-start.4
  444.5 6.1 copy-start.7
  444.5 6.1 copy-start.11
  454.7 2.2 copy-start.6
  456.9 6.7 copy-start.14
  459.0 24.5 %all-to-all-start.2 = ((bf16[3,384,256]{1,0,2:T(4,128)(2,1)}), bf16[3,384,256]{1,0,2:T(4,128)(2,1)S(1)}, u32[]{:S(2)}, u32[]{:S(2)}) async-start(bf16[3,384,256]{1,0,2:T(4,128)(2,1)} %copy.149), calls=%async_computation.2 | async-start | bytes 1572864 | tf_op jit(solution)/shard_map/all_to_all | solution.py:289
  538.7 44.3 %all-to-all-start.3 = ((bf16[4,2,110592]{2,1,0:T(2,128)(2,1)}), bf16[4,2,110592]{2,1,0:T(2,128)(2,1)S(1)}, u32[]{:S(2)}, u32[]{:S(2)}) async-start(bf16[4,2,110592]{2,1,0:T(2,128)(2,1)} %reshape.417), calls=%async_computation.3 | async-start | bytes 3538944 | tf_op jit(solution)/shard_map/all_to_all | solution.py:295
  542.3 152.1 %all-reduce.20.cloned.1.call-start = ((), (), s32[]{:S(2)}) async-start(), calls=%async_computation.17 | async-start | bytes 9437184 | tf_op jit(solution)/shard_map/psum | solution.py:242
  595.7 6.0 copy-start.10
  595.7 2.6 copy-start.45
  596.0 1.3 copy-start.18
  601.8 1.1 copy-start.13
  601.8 1.1 copy-start.20
  601.8 5.3 copy-start.15
  601.8 161.7 %reduce-scatter.9.cloned.1.call-start = ((), (), s32[]{:S(2)}) async-start(), calls=%async_computation.14 | async-start | bytes 1179648 | tf_op jit(solution)/shard_map/reduce_scatter | solution.py:322
  607.0 248.0 %reduce-scatter.11.cloned.1.call-start = ((), (), s32[]{:S(2)}) async-start(), calls=%async_computation.15 | async-start | bytes 4718592 | tf_op jit(solution)/shard_map/reduce_scatter | solution.py:324
  613.2 1.7 copy-start.17
  613.2 334.3 %reduce-scatter.13.cloned.1.call-start = ((), (), s32[]{:S(2)}) async-start(), calls=%async_computation.16 | async-start | bytes 4718592 | tf_op jit(solution)/shard_map/reduce_scatter | solution.py:326
  621.1 1.7 copy-start.16
  621.1 404.9 %reduce-scatter.7.cloned.1.call-start = ((), (), s32[]{:S(2)}) async-start(), calls=%async_computation.13 | async-start | bytes 3538944 | tf_op jit(solution)/shard_map/reduce_scatter | solution.py:320
  628.2 0.7 copy-start.31
  628.2 0.7 copy-start.24
  628.2 0.7 copy-start.47
  628.2 2.6 copy-start.43
  628.3 22.2 %copy-start.27 = (f32[8,1,128]{2,1,0:T(1,128)S(1)}, f32[8,1,128]{2,1,0:T(1,128)}, u32[]{:S(2)}) copy-start(f32[8,1,128]{2,1,0:T(1,128)} %copy-done.26) | copy-start | bytes 12292
  628.3 24.4 %copy-start.36 = (f32[1024]{0:T(1024)S(1)}, f32[1024]{0:T(1024)}, u32[]{:S(2)}) copy-start(f32[1024]{0:T(1024)} %get-tuple-element.576) | copy-start | bytes 12292
  628.3 66.1 %copy-start.2 = (bf16[3,384,1024]{2,1,0:T(8,128)(2,1)S(1)}, bf16[3,384,1024]{2,1,0:T(8,128)(2,1)}, u32[]{:S(2)}) copy-start(bf16[3,384,1024]{2,1,0:T(8,128)(2,1)} %param.25) | copy-start | bytes 7077892
  628.3 66.1 %copy-start.29 = (f32[8,1,128]{2,1,0:T(1,128)S(1)}, f32[8,1,128]{2,1,0:T(1,128)}, u32[]{:S(2)}) copy-start(f32[8,1,128]{2,1,0:T(1,128)} %copy-done.28) | copy-start | bytes 12292
  652.8 45.5 %copy-start.22 = (f32[8,1,128]{2,1,0:T(1,128)S(1)}, f32[8,1,128]{2,1,0:T(1,128)}, u32[]{:S(2)}) copy-start(f32[8,1,128]{2,1,0:T(1,128)} %copy-done.21) | copy-start | bytes 12292
  694.4 3.9 copy-start.5
  694.4 3.9 copy-start.8
  698.3 10.1 copy-start.32
  698.3 10.1 copy-start.33
  698.3 10.1 copy-start.34
  698.3 10.1 copy-start.35
Sparse Core Ops, SparseCore 0:
  10.6 47.3 all-gather.11
  221.1 53.9 all-reduce.15
  277.2 49.2 all-gather.13
  328.4 48.8 all-gather.15
  390.6 53.8 all-reduce.17
  601.9 92.4 all-reduce.19
  698.3 65.1 reduce-scatter.8
  767.7 87.2 reduce-scatter.10
  859.2 88.2 reduce-scatter.12
  951.6 74.3 reduce-scatter.6
where the time goes:
time: 1040 us; the launch traced here: 1030 us
  waiting for transfers between devices  482 us (46%)
  blocking collectives  275 us (26%)
  matrix products  98.6 us (9%)
  local copies, waits for them, and re-layouts  77.3 us (7%)
  other arithmetic  66.5 us (6%)
  between operations  16.5 us (2%)
  starting transfers between devices  15.9 us (2%)
    reduce_scatter x1, waiting for transfers between devices, per_device(): lax.psum_scatter(grad_wdown, ('shard', 'context'), scatter_dimension=1, t...  92.6 us
    reduce_scatter x1, waiting for transfers between devices, per_device(): lax.psum_scatter(grad_wup, ('shard', 'context'), scatter_dimension=0, til...  91.5 us
    reduce_scatter x1, waiting for transfers between devices, per_device(): lax.psum_scatter(grad_wqkv, ('shard', 'context'), scatter_dimension=0, ti...  78.4 us
    psum x1, waiting for transfers between devices, per_device(): lax.psum(jnp.dot(pre_grad, wup_back.T, preferred_element_type=jnp.float32...  54 us
    all_to_all x1, waiting for transfers between devices, per_device(): lax.all_to_all(packed_local, 'context', split_axis=3, concat_axis=1, tile...  40.5 us
    unnamed x1, blocking collectives  38.3 us
    psum x1, waiting for transfers between devices, per_device(): lax.psum(jnp.dot(hidden_act, wdown_all, preferred_element_type=jnp.float3...  37.5 us
    unnamed x118, local copies, waits for them, and re-layouts  34.5 us
  transfers between devices with their start and end apart: 14, of which 10 were waited for; matrix products, arithmetic and copies ran while one was open for 8% of the time, Pallas kernels for 0%

commit v1 on v0

v1 whole, which is shorter than its diff:
```python
import functools

import jax
import jax.numpy as jnp
from jax import lax
from jax.experimental import pallas as pl
from jax.experimental.pallas import tpu as pltpu
from jax.sharding import PartitionSpec as P

HD = 64
LANES = 128
CORES = 2

eps_norm = 1e-06
masked_score = -1e30
root_half = 0.7071067811865476
inv_root_two_pi = 0.3989422804014327
score_scale = HD ** (-0.5)

bf16 = jnp.bfloat16
f32 = jnp.float32
NN = (((1,), (0,)), ((), ()))
NT = (((1,), (1,)), ((), ()))
TN = (((0,), (0,)), ((), ()))


def mm(left, right, dims=NN):
    return lax.dot_general(left, right, dims, preferred_element_type=f32)


def layer_norm(values, norm_gain, norm_shift):
    average = jnp.mean(values, axis=-1, keepdims=True)
    centred = values - average
    variance = jnp.mean(centred * centred, axis=-1, keepdims=True)
    inv_std = lax.rsqrt(variance + eps_norm)
    normed = centred * inv_std
    return (normed * norm_gain + norm_shift, normed, inv_std)


def norm_back(grad_in, normed, inv_std):
    first_mean = jnp.mean(grad_in, axis=-1, keepdims=True)
    second_mean = jnp.mean(grad_in * normed, axis=-1, keepdims=True)
    return inv_std * (grad_in - first_mean - normed * second_mean)


def low_lanes(shape):
    return lax.broadcasted_iota(jnp.int32, shape, 1) < HD


def swap(values):
    return pltpu.roll(values, HD, 1)


def fold(wide):
    half = wide.shape[0] // 2
    return wide[:half] + swap(wide[half:])


def unfold(folded):
    low = low_lanes(folded.shape)
    return jnp.concatenate(
        [jnp.where(low, folded, 0.0), jnp.where(low, swap(folded), 0.0)], axis=0
    )


def qkv_kernel(images, z_ref, x_ref, gain_ref, shift_ref, bias_ref, *refs):
    weights, outs, norm_ref, scratch = refs[:4], refs[4:12], refs[12], refs[13]
    context = len(outs) // 2
    z = z_ref[0]
    rows = x_ref.shape[0] // images
    half = rows // 2
    norm_out, _, _ = layer_norm(x_ref[...].astype(f32), gain_ref[...], shift_ref[...])
    norm_low = norm_out.astype(bf16)
    norm_ref[...] = norm_low
    low = low_lanes((rows, LANES))
    low_half = low_lanes((half, LANES))
    for piece in range(4):
        block = mm(norm_low, weights[piece][...]) + bias_ref[piece : piece + 1, :]
        for image in range(images):
            part = block[image * rows : (image + 1) * rows]
            query, key, value = part[:, :LANES], part[:, LANES : 2 * LANES], part[:, 2 * LANES :]
            head = piece * 2
            scratch[head, image, :rows] = jnp.where(low, query, swap(key)).astype(bf16)
            scratch[head + 1, image, :rows] = jnp.where(low, swap(query), key).astype(bf16)
            scratch[head, image, rows:] = jnp.where(
                low_half, value[:half], swap(value[half:])
            ).astype(bf16)
            scratch[head + 1, image, rows:] = jnp.where(
                low_half, swap(value[:half]), value[half:]
            ).astype(bf16)
    for slot in range(2 * context):
        owner = slot // context * context + lax.rem(z + slot % context, context)
        outs[slot][...] = scratch[owner]


def attend_kernel(count_ref, pos_ref, *refs):
    blocks = (len(refs) - 3) // 2
    packs, outs, log_ref, keys, values = (
        refs[:blocks],
        refs[blocks : 2 * blocks],
        refs[2 * blocks],
        refs[2 * blocks + 1],
        refs[2 * blocks + 2],
    )
    rows = packs[0].shape[1] * 2 // 3
    low = low_lanes((rows, LANES))
    for j in range(blocks):
        pack = packs[j][0].astype(f32)
        keys[j * rows : (j + 1) * rows] = jnp.where(low, swap(pack[:rows]), 0.0).astype(bf16)
        values[j * rows : (j + 1) * rows] = unfold(pack[rows:]).astype(bf16)
    valid = pos_ref[...] < count_ref[pl.program_id(0)]
    for j in range(blocks):
        query = packs[j][0, :rows] * bf16(score_scale)
        scores = jnp.where(valid, mm(query, keys[...], NT), masked_score)
        highest = jnp.max(scores, axis=1, keepdims=True)
        exponent = jnp.exp(scores - highest)
        total = jnp.sum(exponent, axis=1, keepdims=True)
        mixed = mm(exponent.astype(bf16), values[...]) / total
        outs[j][0] = fold(mixed).astype(bf16)
        log_ref[0, j * rows : (j + 1) * rows] = highest + jnp.log(total)


def attend_back_kernel(count_ref, pos_ref, log_ref, *refs):
    blocks = (len(refs) - 4) // 4
    packs, mixes, grads, outs = (refs[i * blocks : (i + 1) * blocks] for i in range(4))
    keys, values, sums, query_grads = refs[4 * blocks :]
    rows = packs[0].shape[1] * 2 // 3
    half = rows // 2
    low = low_lanes((rows, LANES))
    low_half = low_lanes((half, LANES))
    for j in range(blocks):
        pack = packs[j][0].astype(f32)
        keys[j * rows : (j + 1) * rows] = jnp.where(low, swap(pack[:rows]), 0.0).astype(bf16)
        values[j * rows : (j + 1) * rows] = unfold(pack[rows:]).astype(bf16)
    valid = pos_ref[...] < count_ref[pl.program_id(0)]
    for j in range(blocks):
        query = packs[j][0, :rows] * bf16(score_scale)
        grad_wide = unfold(grads[j][0].astype(f32))
        mix_wide = unfold(mixes[j][0].astype(f32))
        delta = jnp.sum(grad_wide * mix_wide, axis=1, keepdims=True)
        grad = grad_wide.astype(bf16)
        scores = jnp.where(valid, mm(query, keys[...], NT), masked_score)
        probs = jnp.exp(scores - log_ref[0, j * rows : (j + 1) * rows])
        weight_grad = mm(grad, values[...], NT)
        score_grad = (probs * (weight_grad - delta)).astype(bf16)
        query_grads[j] = mm(score_grad, keys[...]) * score_scale
        query_t = jnp.transpose(query.astype(f32))[:HD].astype(bf16)
        grad_t = jnp.transpose(grad_wide)[:HD].astype(bf16)
        key_part = mm(query_t, score_grad)
        value_part = mm(grad_t, probs.astype(bf16))
        if j == 0:
            sums[:HD] = key_part
            sums[HD:] = value_part
        else:
            sums[:HD] = sums[:HD] + key_part
            sums[HD:] = sums[HD:] + value_part
    for j in range(blocks):
        both = jnp.transpose(sums[:, j * rows : (j + 1) * rows])
        outs[j][0, :rows] = jnp.where(low, query_grads[j], swap(both)).astype(bf16)
        outs[j][0, rows:] = jnp.where(low_half, swap(both[:half]), both[half:]).astype(bf16)


def gather_heads(z, folded, scratch, mixed_ref):
    context = len(folded) // 2
    images, half, _ = folded[0].shape
    rows = 2 * half
    for slot in range(2 * context):
        owner = slot // context * context + lax.rem(z + slot % context, context)
        scratch[owner] = folded[slot][...]
    low = low_lanes((half, LANES))
    for pair in range(context):
        for image in range(images):
            first = scratch[2 * pair, image].astype(f32)
            second = scratch[2 * pair + 1, image].astype(f32)
            start = image * rows
            columns = slice(pair * LANES, (pair + 1) * LANES)
            mixed_ref[start : start + half, columns] = jnp.where(
                low, first, swap(second)
            ).astype(bf16)
            mixed_ref[start + half : start + rows, columns] = jnp.where(
                low, swap(first), second
            ).astype(bf16)


def project_kernel(z_ref, *refs):
    folded, weights, mixed_ref, part_ref, scratch = refs[:8], refs[8:12], refs[12], refs[13], refs[14]
    gather_heads(z_ref[0], folded, scratch, mixed_ref)
    weight = jnp.concatenate([w[...] for w in weights], axis=1)
    part_ref[...] = mm(mixed_ref[...], weight, NT).astype(bf16)


def project_back_kernel(images, z_ref, grad_ref, *refs):
    weights, outs, scratch = refs[:4], refs[4:12], refs[12]
    context = len(outs) // 2
    z = z_ref[0]
    rows = grad_ref.shape[0] // images
    half = rows // 2
    low = low_lanes((half, LANES))
    weight = jnp.concatenate([w[...] for w in weights], axis=1)
    wide = mm(grad_ref[...], weight)
    for pair in range(4):
        for image in range(images):
            block = wide[image * rows : (image + 1) * rows, pair * LANES : (pair + 1) * LANES]
            first, second = block[:half], block[half:]
            scratch[2 * pair, image] = jnp.where(low, first, swap(second)).astype(bf16)
            scratch[2 * pair + 1, image] = jnp.where(low, swap(first), second).astype(bf16)
    for slot in range(2 * context):
        owner = slot // context * context + lax.rem(z + slot % context, context)
        outs[slot][...] = scratch[owner]


def qkv_back_kernel(z_ref, *refs):
    packs, weights, grads, part_ref, scratch = (
        refs[:8],
        refs[8:12],
        refs[12:16],
        refs[16],
        refs[17],
    )
    z = z_ref[0]
    context = len(packs) // 2
    images = packs[0].shape[0]
    rows = packs[0].shape[1] * 2 // 3
    half = rows // 2
    for slot in range(2 * context):
        owner = slot // context * context + lax.rem(z + slot % context, context)
        scratch[owner] = packs[slot][...]
    low = low_lanes((rows, LANES))
    low_half = low_lanes((half, LANES))
    total = None
    for piece in range(4):
        for image in range(images):
            first = scratch[2 * piece, image].astype(f32)
            second = scratch[2 * piece + 1, image].astype(f32)
            start = image * rows
            grads[piece][start : start + rows, :LANES] = jnp.where(
                low, first[:rows], swap(second[:rows])
            ).astype(bf16)
            grads[piece][start : start + rows, LANES : 2 * LANES] = jnp.where(
                low, swap(first[:rows]), second[:rows]
            ).astype(bf16)
            grads[piece][start : start + half, 2 * LANES :] = jnp.where(
                low_half, first[rows:], swap(second[rows:])
            ).astype(bf16)
            grads[piece][start + half : start + rows, 2 * LANES :] = jnp.where(
                low_half, swap(first[rows:]), second[rows:]
            ).astype(bf16)
        part = mm(grads[piece][...], weights[piece][...], NT)
        total = part if total is None else total + part
    part_ref[...] = total.astype(bf16)


def vmem():
    return pl.BlockSpec(memory_space=pltpu.VMEM)


def smem():
    return pl.BlockSpec(memory_space=pltpu.SMEM)


def shaped(shape, dtype):
    return jax.ShapeDtypeStruct(shape, dtype)


def per_device(sizes, *args):
    (
        tokens_in,
        counts,
        w_qkv,
        b_qv,
        w_out,
        b_out,
        w_up,
        b_up,
        w_down,
        b_down,
        norm1_gain,
        norm1_bias,
        norm2_gain,
        norm2_bias,
        scale1,
        scale2,
        cotangent,
    ) = args
    n_shard, n_context, n_tensor = sizes
    images, row_count, width = tokens_in.shape
    piece_rows = w_qkv.shape[0]
    n_y = n_tensor // CORES
    rows = row_count // n_y
    half = rows // 2
    tokens = images * rows
    x = lax.axis_index("shard")
    z = lax.axis_index("context")
    y = lax.axis_index("tensor") // CORES
    z_arg = z.astype(jnp.int32).reshape(1)
    blocks = n_y * n_context

    def send(value, axis, step):
        size = {"shard": n_shard, "context": n_context}[axis]
        return lax.ppermute(value, axis, [(i, (i + step) % size) for i in range(size)])

    def across(value):
        return lax.ppermute(value, "tensor", [(i, i ^ CORES) for i in range(n_tensor)])

    def partner(value):
        return lax.ppermute(value, "tensor", [(i, i ^ 1) for i in range(n_tensor)])

    def hand_over(values, back):
        out = [values[0]]
        for slot in range(1, blocks):
            jy, jz = slot // n_context, slot % n_context
            step = -jz if back else jz
            pairs = [
                (i * n_tensor + t, (i + step) % n_context * n_tensor + (t ^ (jy * CORES)))
                for i in range(n_context)
                for t in range(n_tensor)
            ]
            out.append(lax.ppermute(values[slot], ("context", "tensor"), pairs))
        return out

    def along_context(value):
        parts = [value] + [send(value, "context", j) for j in range(1, n_context)]
        return jnp.concatenate(parts, axis=0)

    def along_shard(value):
        parts = [value] + [send(value, "shard", j) for j in range(1, n_shard)]
        return jnp.concatenate(parts, axis=0)

    def fetch(piece):
        middle = piece.shape[1] // 2
        whole = along_context(piece)
        first, second = whole[:, :middle], whole[:, middle:]
        own_a = along_shard(first)
        far_b = across(second)
        own_b = along_shard(second)
        other_a = across(own_a)
        other_b = along_shard(far_b)
        return [own_a, own_b, other_a, other_b]

    def add(left, right):
        return left.astype(f32) + right.astype(f32)

    def over_shard(value):
        part = value.reshape((n_shard, -1) + value.shape[1:])
        total = part[0].astype(f32)
        for j in range(1, n_shard):
            total = total + send(part[j], "shard", -j).astype(f32)
        return total

    def over_context(value):
        part = value.reshape((n_context, -1) + value.shape[1:])
        total = part[0].astype(f32)
        for j in range(1, n_context):
            total = total + send(part[j], "context", -j).astype(f32)
        return total

    def share(own_a, own_b, other_a, other_b):
        sum_a = over_shard(add(own_a, across(other_a)).astype(bf16))
        near, far = over_shard(own_b).astype(bf16), over_shard(other_b).astype(bf16)
        sum_b = add(near, across(far))
        return over_context(jnp.concatenate([sum_a, sum_b], axis=1).astype(bf16))

    vectors = [b_out, b_down, norm1_gain, norm1_bias, norm2_gain, norm2_bias, scale1, scale2]
    n_vec, n_qv, n_up = len(vectors) * piece_rows, b_qv.size, b_up.size
    small_size = -(-(n_vec + n_qv + n_up) // 2048) * 2048
    small = jnp.concatenate(
        vectors
        + [b_qv.reshape(-1), b_up.reshape(-1)]
        + [jnp.zeros((small_size - n_vec - n_qv - n_up,), bf16)]
    ).reshape(-1, LANES)
    shards = n_shard * n_context
    small_own = along_shard(along_context(small))
    small_other = across(small_own)
    small_own = small_own.reshape(shards, small_size)
    small_other = small_other.reshape(shards, small_size)
    position = jnp.arange(shards)
    relative_of = (x - position // n_context) % n_shard * n_context + (
        z - position % n_context
    ) % n_context
    actual_of = (x - position // n_context) % n_shard * n_context + (
        z - position % n_context
    ) % n_context

    wide = [
        small_own[:, i * piece_rows : (i + 1) * piece_rows].astype(f32).reshape(1, width)
        for i in range(len(vectors))
    ]
    bout, bdown, gain1, shift1, gain2, shift2, layer_scale1, layer_scale2 = wide
    both = jnp.take(jnp.stack([small_own, small_other]), relative_of, axis=1).astype(f32)
    n_qv_last, n_up_last = b_qv.shape[2], b_up.shape[1]
    qv_all = both[:, :, n_vec : n_vec + n_qv].reshape((2, shards) + b_qv.shape)
    qv_all = qv_all.transpose(0, 2, 3, 1, 4).reshape(2, 2, -1, 2 * HD)
    qkv_bias = jnp.stack([qv_all[:, 0], jnp.zeros_like(qv_all[:, 0]), qv_all[:, 1]], axis=2)
    qkv_bias = qkv_bias.reshape(4, 3 * LANES)
    up_all = both[:, :, n_vec + n_qv : n_vec + n_qv + n_up].reshape((2, shards) + b_up.shape)
    bup = up_all.transpose(0, 2, 1, 3).reshape(1, -1)

    columns = w_qkv.shape[2]
    middle = columns // 2
    qkv_piece = jnp.concatenate(
        [w_qkv[:, :, :middle].reshape(piece_rows, -1), w_qkv[:, :, middle:].reshape(piece_rows, -1)],
        axis=1,
    )
    wqkv = fetch(qkv_piece)
    wout = fetch(w_out.T)
    wup = jnp.concatenate(fetch(w_up), axis=1)
    wdown = jnp.concatenate(fetch(w_down.T), axis=1)

    feature = jnp.arange(width)
    target = actual_of[feature // piece_rows] * piece_rows + feature % piece_rows
    turn = (feature[:, None] == target[None, :]).astype(bf16)

    def own_rows(array):
        part = lax.dynamic_slice_in_dim(array, y * rows, rows, 1).reshape(tokens, width)
        return mm(part, turn).astype(bf16)

    def whole_rows(value):
        low = mm(value.astype(bf16), turn, NT).astype(bf16)
        other = across(low)
        low, other = (v.reshape(images, rows, width) for v in (low, other))
        out = jnp.zeros((images, row_count, width), bf16)
        out = lax.dynamic_update_slice_in_dim(out, low, y * rows, 1)
        out = lax.dynamic_update_slice_in_dim(out, other, (1 - y) * rows, 1)
        return out.astype(f32)

    residual_low = own_rows(tokens_in)
    upstream_low = own_rows(cotangent)
    residual_in = residual_low.astype(f32)
    upstream = upstream_low.astype(f32)

    pack_rows = rows + half
    packed = pl.pallas_call(
        functools.partial(qkv_kernel, images),
        name="qkv",
        in_specs=[smem()] + [vmem()] * 8,
        out_specs=[vmem()] * (blocks + 1),
        out_shape=[shaped((images, pack_rows, LANES), bf16)] * blocks
        + [shaped((tokens, width), bf16)],
        scratch_shapes=[pltpu.VMEM((blocks, images, pack_rows, LANES), bf16)],
    )(z_arg, residual_low, gain1, shift1, qkv_bias, *wqkv)
    norm_low1 = packed[blocks]
    packs = hand_over(packed[:blocks], False)

    slot = jnp.arange(blocks)
    source = (z - slot % n_context) % n_context * row_count + (y ^ (slot // n_context)) * rows
    key_place = (source[:, None] + jnp.arange(rows)[None, :]).reshape(1, -1).astype(jnp.int32)
    length = blocks * rows
    pack_spec = pl.BlockSpec((1, pack_rows, LANES), lambda i: (i, 0, 0))
    fold_spec = pl.BlockSpec((1, half, LANES), lambda i: (i, 0, 0))
    pos_spec = pl.BlockSpec((1, length), lambda i: (0, 0))
    log_spec = pl.BlockSpec((1, length, 1), lambda i: (i, 0, 0))
    attended = pl.pallas_call(
        attend_kernel,
        name="attend",
        grid=(images,),
        in_specs=[smem(), pos_spec] + [pack_spec] * blocks,
        out_specs=[fold_spec] * blocks + [log_spec],
        out_shape=[shaped((images, half, LANES), bf16)] * blocks
        + [shaped((images, length, 1), f32)],
        scratch_shapes=[pltpu.VMEM((length, LANES), bf16)] * 2,
    )(counts, key_place, *packs)
    mixes, log_total = attended[:blocks], attended[blocks]
    folded = hand_over(mixes, True)

    mixture, proj_part = pl.pallas_call(
        project_kernel,
        name="project",
        in_specs=[smem()] + [vmem()] * (blocks + 4),
        out_specs=[vmem()] * 2,
        out_shape=[
            shaped((tokens, blocks * HD), bf16),
            shaped((tokens, width), bf16),
        ],
        scratch_shapes=[pltpu.VMEM((blocks, images, half, LANES), bf16)],
    )(z_arg, *folded, *wout)

    attn_branch = add(proj_part, partner(proj_part)) + bout
    middle_rows = residual_in + layer_scale1 * attn_branch
    norm_out2, normed2, inv_std2 = layer_norm(middle_rows, gain2, shift2)
    norm_low2 = norm_out2.astype(bf16)
    hidden_pre = mm(norm_low2, wup) + bup
    erf_term = 0.5 * (1.0 + lax.erf(hidden_pre * root_half))
    hidden_act = (hidden_pre * erf_term).astype(bf16)
    down_part = mm(hidden_act, wdown, NT).astype(bf16)
    branch_wide = layer_scale2 * upstream
    branch_grad = branch_wide.astype(bf16)
    slope = erf_term + hidden_pre * inv_root_two_pi * jnp.exp(-0.5 * hidden_pre * hidden_pre)
    pre_grad = (mm(branch_grad, wdown) * slope).astype(bf16)
    norm2_part = mm(pre_grad, wup, NT).astype(bf16)
    norm2_grad = add(norm2_part, partner(norm2_part))
    mlp_branch = add(down_part, partner(down_part)) + bdown
    result = middle_rows + layer_scale2 * mlp_branch

    grad_scale2 = jnp.sum(upstream * mlp_branch, axis=0)
    grad_bdown = jnp.sum(branch_wide, axis=0)
    grad_bup = jnp.sum(pre_grad.astype(f32), axis=0)
    grad_gain2 = jnp.sum(norm2_grad * normed2, axis=0)
    grad_shift2 = jnp.sum(norm2_grad, axis=0)
    middle_grad = upstream + norm_back(norm2_grad * gain2, normed2, inv_std2)
    grad_scale1 = jnp.sum(middle_grad * attn_branch, axis=0)
    proj_wide = layer_scale1 * middle_grad
    grad_bout = jnp.sum(proj_wide, axis=0)
    proj_grad = proj_wide.astype(bf16)

    mix_grads = pl.pallas_call(
        functools.partial(project_back_kernel, images),
        name="project_back",
        in_specs=[smem()] + [vmem()] * 5,
        out_specs=[vmem()] * blocks,
        out_shape=[shaped((images, half, LANES), bf16)] * blocks,
        scratch_shapes=[pltpu.VMEM((blocks, images, half, LANES), bf16)],
    )(z_arg, proj_grad, *wout)
    mix_grads = hand_over(mix_grads, False)

    pack_grads = pl.pallas_call(
        attend_back_kernel,
        name="attend_back",
        grid=(images,),
        in_specs=[smem(), pos_spec, log_spec]
        + [pack_spec] * blocks
        + [fold_spec] * (2 * blocks),
        out_specs=[pack_spec] * blocks,
        out_shape=[shaped((images, pack_rows, LANES), bf16)] * blocks,
        scratch_shapes=[pltpu.VMEM((length, LANES), bf16)] * 2
        + [pltpu.VMEM((2 * HD, length), f32), pltpu.VMEM((blocks, rows, LANES), f32)],
    )(counts, key_place, log_total, *packs, *mixes, *mix_grads)
    pack_grads = hand_over(pack_grads, True)

    def pieces(left, right, count):
        whole = mm(left, right, TN).astype(bf16)
        size = whole.shape[1] // count
        return [whole[:, i * size : (i + 1) * size] for i in range(count)]

    grad_wdown = share(*pieces(branch_grad, hidden_act, 4)).T
    grad_wup = share(*pieces(norm_low2, pre_grad, 4))
    grad_wout = share(*pieces(proj_grad, mixture, 4)).T

    back = pl.pallas_call(
        qkv_back_kernel,
        name="qkv_back",
        in_specs=[smem()] + [vmem()] * (blocks + 4),
        out_specs=[vmem()] * 5,
        out_shape=[shaped((tokens, 3 * LANES), bf16)] * 4 + [shaped((tokens, width), bf16)],
        scratch_shapes=[pltpu.VMEM((blocks, images, pack_rows, LANES), bf16)],
    )(z_arg, *pack_grads, *wqkv)
    qkv_grads, norm1_part = back[:4], back[4]
    grad_wqkv = share(*[mm(norm_low1, g, TN).astype(bf16) for g in qkv_grads])
    grad_wqkv = grad_wqkv.reshape(piece_rows, 2, 3, middle).transpose(0, 2, 1, 3)
    grad_wqkv = grad_wqkv.reshape(piece_rows, 3, columns)

    norm1_grad = add(norm1_part, partner(norm1_part))
    _, normed1, inv_std1 = layer_norm(residual_in, gain1, shift1)
    grad_gain1 = jnp.sum(norm1_grad * normed1, axis=0)
    grad_shift1 = jnp.sum(norm1_grad, axis=0)
    input_grad = middle_grad + norm_back(norm1_grad * gain1, normed1, inv_std1)

    summed = jnp.stack([jnp.sum(g.astype(f32), axis=0) for g in qkv_grads])
    summed = summed.reshape(2, 2, 3, 2 * HD)[:, :, jnp.array([0, 2])].transpose(0, 2, 1, 3)
    qv_grad = summed.reshape(2, 2, b_qv.shape[1], shards, n_qv_last)
    qv_grad = qv_grad.transpose(0, 3, 1, 2, 4).reshape(2, shards, n_qv)
    up_grad = grad_bup.reshape(2, b_up.shape[0], shards, n_up_last)
    up_grad = up_grad.transpose(0, 2, 1, 3).reshape(2, shards, n_up)
    biases = jnp.take(jnp.concatenate([qv_grad, up_grad], axis=2), actual_of, axis=1)
    dense = jnp.stack(
        [
            grad_bout,
            grad_bdown,
            grad_gain1,
            grad_shift1,
            grad_gain2,
            grad_shift2,
            grad_scale1,
            grad_scale2,
        ]
    )
    dense = dense.reshape(-1, shards, piece_rows).transpose(1, 0, 2).reshape(shards, n_vec)
    pad = jnp.zeros((shards, small_size - n_vec - n_qv - n_up), f32)
    own = jnp.concatenate([dense, biases[0], pad], axis=1).reshape(-1, LANES)
    other = jnp.concatenate([dense, biases[1], pad], axis=1).reshape(-1, LANES)
    total = over_context(over_shard(own + across(other))).reshape(-1)
    vec = total[:n_vec].reshape(-1, piece_rows)

    return (
        whole_rows(result),
        whole_rows(input_grad),
        grad_wqkv,
        total[n_vec : n_vec + n_qv].reshape(b_qv.shape),
        grad_wout,
        vec[0],
        grad_wup,
        total[n_vec + n_qv : n_vec + n_qv + n_up].reshape(b_up.shape),
        grad_wdown,
        vec[1],
        vec[2],
        vec[3],
        vec[4],
        vec[5],
        vec[6],
        vec[7],
    )


def solution(mesh):
    in_specs = (
        P("shard", "context", None),
        P("shard"),
        P(("shard", "context"), None, "tensor"),
        P(None, "tensor", ("shard", "context")),
        P("tensor", ("shard", "context")),
        P(("shard", "context")),
        P(("shard", "context"), "tensor"),
        P("tensor", ("shard", "context")),
        P("tensor", ("shard", "context")),
        P(("shard", "context")),
        P(("shard", "context")),
        P(("shard", "context")),
        P(("shard", "context")),
        P(("shard", "context")),
        P(("shard", "context")),
        P(("shard", "context")),
        P("shard", "context", None),
    )
    out_specs = (
        P("shard", "context", None),
        P("shard", "context", None),
        P(("shard", "context"), None, "tensor"),
        P(None, "tensor", ("shard", "context")),
        P("tensor", ("shard", "context")),
        P(("shard", "context")),
        P(("shard", "context"), "tensor"),
        P("tensor", ("shard", "context")),
        P("tensor", ("shard", "context")),
        P(("shard", "context")),
        P(("shard", "context")),
        P(("shard", "context")),
        P(("shard", "context")),
        P(("shard", "context")),
        P(("shard", "context")),
        P(("shard", "context")),
    )
    sizes = tuple(mesh.shape[name] for name in ("shard", "context", "tensor"))
    return jax.shard_map(
        functools.partial(per_device, sizes),
        mesh=mesh,
        in_specs=in_specs,
        out_specs=out_specs,
        check_vma=False,
    )
```

time: 1040 us -> 643 us (0.62)
  waiting for transfers between devices: 482 us -> 155 us
  blocking collectives: 275 us -> 0 us
  starting transfers between devices: 15.9 us -> 164 us
  Pallas kernels: 0 us -> 59.8 us
  between operations: 16.5 us -> 2.58 us
    reduce_scatter x4 -> x0, waiting for transfers between devices: 273 us -> none  [the longest x1 92.6 us: per_device(): lax.psum_scatter(grad_wdown, ('shard', 'context'), scatter_dimension=1, t...]
    all_gather x11 -> x0, blocking collectives: 237 us -> none  [the longest x1 33.7 us: per_device(): lax.all_gather(w_out, ('shard', 'context'), axis=1, tiled=True)]
    ppermute x0 -> x108, starting transfers between devices: none -> 164 us  [the longest x56 77.2 us: send(): lax.ppermute(value, axis, [(i, (i + step) % size) for i in range(size)])]
    ppermute x0 -> x108, waiting for transfers between devices: none -> 155 us  [the longest x56 79.2 us: send(): lax.ppermute(value, axis, [(i, (i + step) % size) for i in range(size)])]
    all_to_all x4 -> x0, waiting for transfers between devices: 93.9 us -> none  [the longest x1 40.5 us: per_device(): lax.all_to_all(packed_local, 'context', split_axis=3, concat_axis=1, tile...]
    psum x3 -> x0, waiting for transfers between devices: 91.5 us -> none  [the longest x1 54 us: per_device(): lax.psum(jnp.dot(pre_grad, wup_back.T, preferred_element_type=jnp.float32...]
    pallas_call x0 -> x6, Pallas kernels: none -> 59.8 us  [the longest x1 23 us: per_device(): pl.pallas_call(attend_back_kernel, name='attend_back', grid=(images,), in...]
    unnamed x1 -> x0, blocking collectives: 38.3 us -> none
  transfers between devices with their start and end apart: 14 -> 108, of which waited for: 10 -> 29; matrix products, arithmetic and copies ran while one was open for 8% -> 35% of each run, Pallas kernels for 0% -> 9%
where the time goes in v1:
time: 643 us; the launch traced here: 633 us
  starting transfers between devices  164 us (26%)
  waiting for transfers between devices  155 us (24%)
  matrix products  95.8 us (15%)
  local copies, waits for them, and re-layouts  84.2 us (13%)
  other arithmetic  72.4 us (11%)
  Pallas kernels  59.8 us (9%)
    dot_general x15, matrix products, mm(): return lax.dot_general(left, right, dims, preferred_element_type=f32)  95.8 us
    ppermute x56, waiting for transfers between devices, send(): lax.ppermute(value, axis, [(i, (i + step) % size) for i in range(size)])  79.2 us
    ppermute x56, starting transfers between devices, send(): lax.ppermute(value, axis, [(i, (i + step) % size) for i in range(size)])  77.2 us
    ppermute x28, starting transfers between devices, hand_over(): out.append(lax.ppermute(values[slot], ('context', 'tensor'), pairs))  45.5 us
    ppermute x20, starting transfers between devices, across(): lax.ppermute(value, 'tensor', [(i, i ^ CORES) for i in range(n_tensor)])  41 us
    ppermute x28, waiting for transfers between devices, hand_over(): out.append(lax.ppermute(values[slot], ('context', 'tensor'), pairs))  39.2 us
    ppermute x20, waiting for transfers between devices, across(): lax.ppermute(value, 'tensor', [(i, i ^ CORES) for i in range(n_tensor)])  36.1 us
    pallas_call x1, Pallas kernels, per_device(): pl.pallas_call(attend_back_kernel, name='attend_back', grid=(images,), in...  23 us
  transfers between devices with their start and end apart: 108, of which 29 were waited for; matrix products, arithmetic and copies ran while one was open for 35% of the time, Pallas kernels for 9%

profile of v1, /device:TPU:0, one launch (start us, length us, event | category | flops | bytes accessed | tf_op | source)
XLA Modules:
  0.0 633.0 jit_solution(16961365399606248466)
XLA Ops:
  2.3 5.4 concatenate.93
  7.7 3.1 collective-permute-start
  20.9 4.5 compare_select_fusion.1
  32.5 2.8 collective-permute-start.7
  45.9 2.9 collective-permute-start.29
  53.0 7.0 %collective-permute-done.8 = bf16[512,384]{1,0:T(8,128)(2,1)S(1)} collective-permute-done((bf16[512,384]{1,0:T(8,128)(2,1)S(1)}, bf16[512,384]{1,0:T(8,128)(2,1)S(1)}, u32[]{:S(2)}, u32[]{:S(2)}) %collective-permute-start.8) | collective-permute-done | bytes 393248 | tf_op jit(solution)/shard_map/ppermute | solution.py:300
  67.4 3.4 collective-permute-done.9
  73.3 3.1 collective-permute-done.12
  80.5 7.1 %qkv.1 = (bf16[3,288,128]{2,1,0:T(8,128)(2,1)}, bf16[3,288,128]{2,1,0:T(8,128)(2,1)}, bf16[3,288,128]{2,1,0:T(8,128)(2,1)}, bf16[3,288,128]{2,1,0:T(8,128)(2,1)}...) custom-call(s32[1]{0:T(128)} %bitcast.12.z_ref, ...), custom_call_target="tpu_custom_call" | custom-call | tf_op jit(solution)/shard_map/qkv/pallas_call | solution.py:432
  89.7 2.9 collective-permute-start.15
  99.0 8.5 %collective-permute-done.14.refs_2_ = bf16[3,288,128]{2,1,0:T(8,128)(2,1)S(1)} collective-permute-done((bf16[3,288,128]{2,1,0:T(8,128)(2,1)}, bf16[3,288,128]{2,1,0:T(8,128)(2,1)S(1)}, u32[]{:S(2)}, u32[]{:S(2)}) %collective-permute-start.14) | collective-permute-done | bytes 221216 | tf_op jit(solution)/shard_map/ppermute | solution.py:318
  108.7 6.2 collective-permute-start.18
  114.9 3.8 collective-permute-start.19
  122.1 3.3 collective-permute-done.18.refs_6_
  126.2 16.5 %attend.1 = (bf16[3,96,128]{2,1,0:T(8,128)(2,1)}, bf16[3,96,128]{2,1,0:T(8,128)(2,1)}, bf16[3,96,128]{2,1,0:T(8,128)(2,1)}, bf16[3,96,128]{2,1,0:T(8,128)(2,1)},...) custom-call(s32[3]{0:T(128)} %count_ref.3, ...), custom_call_target="tpu_custom_call" | custom-call | tf_op jit(solution)/shard_map/attend/pallas_call | solution.py:452
  142.7 3.1 collective-permute-start.20
  148.6 4.7 collective-permute-start.24
  153.3 3.4 collective-permute-done.21.refs_2_
  161.3 3.1 collective-permute-done.25.refs_6_
  165.4 3.5 project.1
  172.2 3.9 collective-permute-done.45
  188.9 4.1 collective-permute-start.50
  194.1 3.0 collective-permute-done.47
  197.1 7.2 %collective-permute-start.41 = (bf16[1024,512]{1,0:T(8,128)(2,1)S(1)}, bf16[1024,512]{1,0:T(8,128)(2,1)S(1)}, u32[]{:S(2)}, u32[]{:S(2)}) collective-permute-start(bf16[1024,512]{1,0:T(8,128)(2,1)S(1)} %pad_maximum_fusion), channel_id=1, source_target_pairs={{0,2},{1,3},{2,0},{3,1},{4,6},{5,7},{6,4},{7,5},{8,10},{9,11},{10,... | collective-permute-start | bytes 3145736 | tf_op jit(solution)/shard_map/ppermute | solution.py:303
  208.0 2.8 fusion.86
  211.3 4.1 collective-permute-start.49
  216.8 14.7 %collective-permute-done.43 = bf16[512,512]{1,0:T(8,128)(2,1)S(1)} collective-permute-done((bf16[512,512]{1,0:T(8,128)(2,1)}, bf16[512,512]{1,0:T(8,128)(2,1)S(1)}, u32[]{:S(2)}, u32[]{:S(2)}) %collective-permute-start.43) | collective-permute-done | bytes 524320 | tf_op jit(solution)/shard_map/ppermute | solution.py:300
  231.6 6.7 %multiply_convert_fusion = (bf16[576,2048]{1,0:T(8,128)(2,1)S(1)}, f32[576,2048]{1,0:T(8,128)}) fusion(f32[2048]{0:T(1024)S(1)} %copy-done.91, bf16[512,512]{1,0:T(8,128)(2,1)S(1)} %collective-permute-done.43, bf16[512,512]{1,0:T(8,128)(2,1)} %collective-permute-done.42, bf16[1024,512]{1,0:T(8,128)(2,1)S(1)} %collective-permute-done.41, ...), kind=kOutput, calls=%fused_computation.10 | convolution fusion | flops 2455306240 | bytes 13652480 | tf_op jit(solution)/shard_map/dot_general | solution.py:28
  238.2 3.7 convolution_convert_fusion
  245.3 6.3 collective-permute-start.100
  251.6 22.9 %convert_reduce_fusion = (f32[2048]{0:T(1024)}, bf16[576,2048]{1,0:T(8,128)(2,1)S(1)}) fusion(f32[576,2048]{1,0:T(8,128)} %get-tuple-element.230, f32[2048]{0:T(1024)S(1)} %copy-done.91, bf16[512,512]{0,1:T(8,128)(2,1)S(1)} %collective-permute-done.51, bf16[512,512]{0,1:T(8,128)(2,1)S(1)} %collective-permute-done.50, ...), kind=kOutput, calls=%fused_computation.9 | convolution fusion | flops 2462382080 | bytes 12472320 | tf_op jit(solution)/shard_map/dot_general | solution.py:28
  274.5 4.2 convolution_convert_fusion.1
  281.8 16.4 %convolution_convert_fusion.2 = bf16[576,1024]{1,0:T(8,128)(2,1)} fusion(bf16[576,2048]{1,0:T(8,128)(2,1)S(1)} %get-tuple-element.232, bf16[512,512]{1,0:T(8,128)(2,1)S(1)} %collective-permute-done.43, bf16[512,512]{1,0:T(8,128)(2,1)} %collective-permute-done.42, bf16[1024,512]{1,0:T(8,128)(2,1)S(1)} %collective-permute-done.41, ...), kind=kOutput, calls=%fused_computation.72 | convolution fusion | flops 2445869056 | bytes 7733248 | tf_op jit(solution)/shard_map/dot_general | solution.py:28
  301.4 16.8 %convolution_convert_fusion.3 = bf16[576,1024]{1,0:T(8,128)(2,1)} fusion(bf16[576,2048]{1,0:T(8,128)(2,1)S(1)} %get-tuple-element.229, bf16[512,512]{0,1:T(8,128)(2,1)S(1)} %collective-permute-done.51, bf16[512,512]{0,1:T(8,128)(2,1)S(1)} %collective-permute-done.50, bf16[1024,512]{0,1:T(8,128)(2,1)S(1)} %collective-permute-done.49, ...), kind=kOutput, calls=%fused_computation.73 | convolution fusion | flops 2445869056 | bytes 7733248 | tf_op jit(solution)/shard_map/dot_general | solution.py:28
  334.0 9.9 %collective-permute-done.92 = bf16[1024,512]{1,0:T(8,128)(2,1)} collective-permute-done((bf16[1024,512]{1,0:T(8,128)(2,1)}, bf16[1024,512]{1,0:T(8,128)(2,1)}, u32[]{:S(2)}, u32[]{:S(2)}) %collective-permute-start.92) | collective-permute-done | bytes 1048608 | tf_op jit(solution)/shard_map/ppermute | solution.py:303
  347.6 3.5 multiply_reduce_fusion.1
  351.2 5.2 fusion.23
  361.5 3.3 project_back.1
  364.9 3.8 collective-permute-start.57
  370.8 4.5 fusion.35
  381.1 3.8 collective-permute-start.61
  387.9 23.0 %attend_back.1 = (bf16[3,288,128]{2,1,0:T(8,128)(2,1)}, bf16[3,288,128]{2,1,0:T(8,128)(2,1)}, bf16[3,288,128]{2,1,0:T(8,128)(2,1)}, bf16[3,288,128]{2,1,0:T(8,12...) custom-call(s32[3]{0:T(128)} %count_ref.3, ...), custom_call_target="tpu_custom_call" | custom-call | tf_op jit(solution)/shard_map/attend_back/pallas_call | solution.py:515
  410.9 3.4 collective-permute-start.62
  421.8 4.1 collective-permute-start.66
  426.2 13.1 %collective-permute-done.63.refs_2_ = bf16[3,288,128]{2,1,0:T(8,128)(2,1)} collective-permute-done((bf16[3,288,128]{2,1,0:T(8,128)(2,1)}, bf16[3,288,128]{2,1,0:T(8,128)(2,1)}, u32[]{:S(2)}, u32[]{:S(2)}) %collective-permute-start.63) | collective-permute-done | bytes 221216 | tf_op jit(solution)/shard_map/ppermute | solution.py:318
  443.9 5.7 collective-permute-done.67.refs_6_
  449.6 6.4 %qkv_back.1 = (bf16[576,384]{1,0:T(8,128)(2,1)}, bf16[576,384]{1,0:T(8,128)(2,1)}, bf16[576,384]{1,0:T(8,128)(2,1)}, bf16[576,384]{1,0:T(8,128)(2,1)}, bf16[576,1024]{1,0:T(8,128)(2,1)}) custom-call(s32[1]{0:T(128)} %bitcast.12.z_ref, bf16[3,288,128]{2,1,0:T(8,128)(2,1)} %get-tuple-element.83.refs_0_, bf16[3,288,128]{2,1,0:T(8,128)(2,1)} %collective-permute-done.62.refs_1_, ...), custom_call_target="tpu_custom_call" | custom-call | tf_op jit(solution)/shard_map/qkv_back/pallas_call | solution.py:538
  458.4 3.2 convolution_convert_fusion.6
  473.9 3.2 convolution_convert_fusion.7
  486.9 9.2 %collective-permute-done.89 = bf16[128,256]{0,1:T(8,128)(2,1)S(1)} collective-permute-done((bf16[128,256]{0,1:T(8,128)(2,1)S(1)}, bf16[128,256]{0,1:T(8,128)(2,1)S(1)}, u32[]{:S(2)}, u32[]{:S(2)}) %collective-permute-start.89) | collective-permute-done | bytes 65568 | tf_op jit(solution)/shard_map/ppermute | solution.py:300
  496.1 4.4 collective-permute-start.97
  500.5 7.4 %collective-permute-done.90 = bf16[128,256]{0,1:T(8,128)(2,1)S(1)} collective-permute-done((bf16[128,256]{0,1:T(8,128)(2,1)S(1)}, bf16[128,256]{0,1:T(8,128)(2,1)S(1)}, u32[]{:S(2)}, u32[]{:S(2)}) %collective-permute-start.90) | collective-permute-done | bytes 65568 | tf_op jit(solution)/shard_map/ppermute | solution.py:300
  507.8 3.0 collective-permute-start.91
  512.3 3.6 collective-permute-done.91
  522.7 3.7 collective-permute-done.74
  527.3 9.7 %collective-permute-done.98 = bf16[128,1024]{1,0:T(8,128)(2,1)S(1)} collective-permute-done((bf16[128,1024]{1,0:T(8,128)(2,1)S(1)}, bf16[128,1024]{1,0:T(8,128)(2,1)S(1)}, u32[]{:S(2)}, u32[]{:S(2)}) %collective-permute-start.98) | collective-permute-done | bytes 262176 | tf_op jit(solution)/shard_map/ppermute | solution.py:300
  545.1 4.1 collective-permute-done.73
  549.2 19.9 %collective-permute-done.75 = bf16[512,384]{0,1:T(8,128)(2,1)} collective-permute-done((bf16[512,384]{0,1:T(8,128)(2,1)}, bf16[512,384]{0,1:T(8,128)(2,1)}, u32[]{:S(2)}, u32[]{:S(2)}) %collective-permute-start.75) | collective-permute-done | bytes 393248 | tf_op jit(solution)/shard_map/ppermute | solution.py:303
  572.6 2.7 convert_element_type.346
  575.4 3.5 fusion.21
  598.6 4.8 fusion.37
  608.8 2.9 collective-permute-start.77
  618.0 4.1 collective-permute-done.77
  625.3 3.2 collective-permute-done.70
  (561 shorter events, 233.2 us)
Async XLA Ops:
  7.7 24.8 %collective-permute-start = (bf16[16,128]{1,0:T(8,128)(2,1)S(1)}, bf16[16,128]{1,0:T(8,128)(2,1)S(1)}, u32[]{:S(2)}, u32[]{:S(2)}) collective-permute-start(bf16[16,128]{1,0:T(8,128)(2,1)S(1)} %bitcast.168), channel_id=1, source_target_pairs={{0,4},{4,8},{8,12},{12,0},{1,5},{5,9},{9,13},{13,1},{2,6},{6,10},{... | collective-permute-start | bytes 12296 | tf_op jit(solution)/shard_map/ppermute | solution.py:300
  10.8 24.5 %collective-permute-start.1 = (bf16[16,128]{1,0:T(8,128)(2,1)S(1)}, bf16[16,128]{1,0:T(8,128)(2,1)S(1)}, u32[]{:S(2)}, u32[]{:S(2)}) collective-permute-start(bf16[16,128]{1,0:T(8,128)(2,1)S(1)} %bitcast.169), channel_id=1, source_target_pairs={{0,8},{4,12},{8,0},{12,4},{1,9},{5,13},{9,1},{13,5},{2,10},{6,14},... | collective-permute-start | bytes 12296 | tf_op jit(solution)/shard_map/ppermute | solution.py:300
  13.3 22.5 %collective-permute-start.2 = (bf16[16,128]{1,0:T(8,128)(2,1)S(1)}, bf16[16,128]{1,0:T(8,128)(2,1)S(1)}, u32[]{:S(2)}, u32[]{:S(2)}) collective-permute-start(bf16[16,128]{1,0:T(8,128)(2,1)S(1)} %bitcast.170), channel_id=1, source_target_pairs={{0,12},{4,0},{8,4},{12,8},{1,13},{5,1},{9,5},{13,9},{2,14},{6,2},{... | collective-permute-start | bytes 12296 | tf_op jit(solution)/shard_map/ppermute | solution.py:300
  16.2 29.7 %collective-permute-start.5 = (bf16[128,768]{1,0:T(8,128)(2,1)S(1)}, bf16[128,768]{1,0:T(8,128)(2,1)S(1)}, u32[]{:S(2)}, u32[]{:S(2)}) collective-permute-start(bf16[128,768]{1,0:T(8,128)(2,1)S(1)} %pad_maximum_fusion.12), channel_id=1, source_target_pairs={{0,4},{4,8},{8,12},{12,0},{1,5},{5,9},{9,13},{13,1},{2,6},{6,10},{... | collective-permute-start | bytes 589832 | tf_op jit(solution)/shard_map/ppermute | solution.py:300
  16.9 31.9 %collective-permute-start.6 = (bf16[128,768]{1,0:T(8,128)(2,1)S(1)}, bf16[128,768]{1,0:T(8,128)(2,1)S(1)}, u32[]{:S(2)}, u32[]{:S(2)}) collective-permute-start(bf16[128,768]{1,0:T(8,128)(2,1)S(1)} %pad_maximum_fusion.12), channel_id=1, source_target_pairs={{0,8},{4,12},{8,0},{12,4},{1,9},{5,13},{9,1},{13,5},{2,10},{6,14},... | collective-permute-start | bytes 589832 | tf_op jit(solution)/shard_map/ppermute | solution.py:300
  35.3 26.4 %collective-permute-start.27 = (bf16[128,256]{1,0:T(8,128)(2,1)S(1)}, bf16[128,256]{1,0:T(8,128)(2,1)S(1)}, u32[]{:S(2)}, u32[]{:S(2)}) collective-permute-start(bf16[128,256]{1,0:T(8,128)(2,1)S(1)} %bitcast.160), channel_id=1, source_target_pairs={{0,4},{4,8},{8,12},{12,0},{1,5},{5,9},{9,13},{13,1},{2,6},{6,10},{... | collective-permute-start | bytes 196616 | tf_op jit(solution)/shard_map/ppermute | solution.py:300
  43.6 21.0 %collective-permute-start.28 = (bf16[128,256]{1,0:T(8,128)(2,1)S(1)}, bf16[128,256]{1,0:T(8,128)(2,1)}, u32[]{:S(2)}, u32[]{:S(2)}) collective-permute-start(bf16[128,256]{1,0:T(8,128)(2,1)S(1)} %bitcast.161), channel_id=1, source_target_pairs={{0,8},{4,12},{8,0},{12,4},{1,9},{5,13},{9,1},{13,5},{2,10},{6,14},... | collective-permute-start | bytes 196616 | tf_op jit(solution)/shard_map/ppermute | solution.py:300
  45.9 18.6 %collective-permute-start.29 = (bf16[128,256]{1,0:T(8,128)(2,1)S(1)}, bf16[128,256]{1,0:T(8,128)(2,1)}, u32[]{:S(2)}, u32[]{:S(2)}) collective-permute-start(bf16[128,256]{1,0:T(8,128)(2,1)S(1)} %bitcast.162), channel_id=1, source_target_pairs={{0,12},{4,0},{8,4},{12,8},{1,13},{5,1},{9,5},{13,9},{2,14},{6,2},{... | collective-permute-start | bytes 196616 | tf_op jit(solution)/shard_map/ppermute | solution.py:300
  64.6 28.0 %collective-permute-start.36 = (bf16[128,1024]{1,0:T(8,128)(2,1)}, bf16[128,1024]{1,0:T(8,128)(2,1)}, u32[]{:S(2)}, u32[]{:S(2)}) collective-permute-start(bf16[128,1024]{1,0:T(8,128)(2,1)} %param.24), channel_id=1, source_target_pairs={{0,4},{4,8},{8,12},{12,0},{1,5},{5,9},{9,13},{13,1},{2,6},{6,10},{... | collective-permute-start | bytes 786440 | tf_op jit(solution)/shard_map/ppermute | solution.py:300
  64.6 30.2 %collective-permute-start.37 = (bf16[128,1024]{1,0:T(8,128)(2,1)}, bf16[128,1024]{1,0:T(8,128)(2,1)}, u32[]{:S(2)}, u32[]{:S(2)}) collective-permute-start(bf16[128,1024]{1,0:T(8,128)(2,1)} %param.24), channel_id=1, source_target_pairs={{0,8},{4,12},{8,0},{12,4},{1,9},{5,13},{9,1},{13,5},{2,10},{6,14},... | collective-permute-start | bytes 786440 | tf_op jit(solution)/shard_map/ppermute | solution.py:300
  89.3 18.2 %collective-permute-start.14 = (bf16[3,288,128]{2,1,0:T(8,128)(2,1)}, bf16[3,288,128]{2,1,0:T(8,128)(2,1)S(1)}, u32[]{:S(2)}, u32[]{:S(2)}) collective-permute-start(bf16[3,288,128]{2,1,0:T(8,128)(2,1)} %get-tuple-element.59), channel_id=1, source_target_pairs={{0,8},{1,9},{2,10},{3,11},{4,12},{5,13},{6,14},{7,15},{8,0},{9,1},... | collective-permute-start | bytes 663560 | tf_op jit(solution)/shard_map/ppermute | solution.py:318
  89.7 19.0 %collective-permute-start.15 = (bf16[3,288,128]{2,1,0:T(8,128)(2,1)}, bf16[3,288,128]{2,1,0:T(8,128)(2,1)S(1)}, u32[]{:S(2)}, u32[]{:S(2)}) collective-permute-start(bf16[3,288,128]{2,1,0:T(8,128)(2,1)} %get-tuple-element.60), channel_id=1, source_target_pairs={{0,12},{1,13},{2,14},{3,15},{4,0},{5,1},{6,2},{7,3},{8,4},{9,5},{1... | collective-permute-start | bytes 663560 | tf_op jit(solution)/shard_map/ppermute | solution.py:318
  92.6 22.3 %collective-permute-start.16 = (bf16[3,288,128]{2,1,0:T(8,128)(2,1)}, bf16[3,288,128]{2,1,0:T(8,128)(2,1)S(1)}, u32[]{:S(2)}, u32[]{:S(2)}) collective-permute-start(bf16[3,288,128]{2,1,0:T(8,128)(2,1)} %get-tuple-element.61), channel_id=1, source_target_pairs={{0,2},{1,3},{2,0},{3,1},{4,6},{5,7},{6,4},{7,5},{8,10},{9,11},{10,... | collective-permute-start | bytes 663560 | tf_op jit(solution)/shard_map/ppermute | solution.py:318
  94.8 52.2 %collective-permute-start.38 = (bf16[128,1024]{1,0:T(8,128)(2,1)}, bf16[128,1024]{1,0:T(8,128)(2,1)}, u32[]{:S(2)}, u32[]{:S(2)}) collective-permute-start(bf16[128,1024]{1,0:T(8,128)(2,1)} %param.24), channel_id=1, source_target_pairs={{0,12},{4,0},{8,4},{12,8},{1,13},{5,1},{9,5},{13,9},{2,14},{6,2},{... | collective-permute-start | bytes 786440 | tf_op jit(solution)/shard_map/ppermute | solution.py:300
  98.0 21.6 %collective-permute-start.17 = (bf16[3,288,128]{2,1,0:T(8,128)(2,1)}, bf16[3,288,128]{2,1,0:T(8,128)(2,1)S(1)}, u32[]{:S(2)}, u32[]{:S(2)}) collective-permute-start(bf16[3,288,128]{2,1,0:T(8,128)(2,1)} %get-tuple-element.62), channel_id=1, source_target_pairs={{0,6},{1,7},{2,4},{3,5},{4,10},{5,11},{6,8},{7,9},{8,14},{9,15},{1... | collective-permute-start | bytes 663560 | tf_op jit(solution)/shard_map/ppermute | solution.py:318
  107.5 41.1 %collective-permute-start.32 = (bf16[1024,128]{1,0:T(8,128)(2,1)S(1)}, bf16[1024,128]{1,0:T(8,128)(2,1)S(1)}, u32[]{:S(2)}, u32[]{:S(2)}) collective-permute-start(bf16[1024,128]{1,0:T(8,128)(2,1)S(1)} %pad_maximum_fusion.9.refs_8_.refs_0_), channel_id=1, source_target_pairs={{0,2},{1,3},{2,0},{3,1},{4,6},{5,7},{6,4},{7,5},{8,10},{9,11},{10,... | collective-permute-start | bytes 786440 | tf_op jit(solution)/shard_map/ppermute | solution.py:303
  119.6 28.4 %collective-permute-start.34 = (bf16[512,128]{1,0:T(8,128)(2,1)}, bf16[512,128]{1,0:T(8,128)(2,1)S(1)}, u32[]{:S(2)}, u32[]{:S(2)}) collective-permute-start(bf16[512,128]{1,0:T(8,128)(2,1)} %collective-permute-done.33), channel_id=1, source_target_pairs={{0,16},{16,0},{1,17},{17,1},{2,18},{18,2},{3,19},{19,3},{4,20},{20... | collective-permute-start | bytes 393224 | tf_op jit(solution)/shard_map/ppermute | solution.py:300
  157.8 18.3 %collective-permute-start.45 = (bf16[128,1024]{0,1:T(8,128)(2,1)}, bf16[128,1024]{0,1:T(8,128)(2,1)}, u32[]{:S(2)}, u32[]{:S(2)}) collective-permute-start(bf16[128,1024]{0,1:T(8,128)(2,1)} %bitcast.165), channel_id=1, source_target_pairs={{0,8},{4,12},{8,0},{12,4},{1,9},{5,13},{9,1},{13,5},{2,10},{6,14},... | collective-permute-start | bytes 786440 | tf_op jit(solution)/shard_map/ppermute | solution.py:300
  168.9 38.1 %collective-permute-start.35 = (bf16[576,1024]{1,0:T(8,128)(2,1)}, bf16[576,1024]{1,0:T(8,128)(2,1)S(1)}, u32[]{:S(2)}, u32[]{:S(2)}) collective-permute-start(bf16[576,1024]{1,0:T(8,128)(2,1)} %get-tuple-element.73), channel_id=1, source_target_pairs={{0,1},{1,0},{2,3},{3,2},{4,5},{5,4},{6,7},{7,6},{8,9},{9,8},{10,11... | collective-permute-start | bytes 3538952 | tf_op jit(solution)/shard_map/ppermute | solution.py:306
  170.9 18.0 %collective-permute-start.39 = (bf16[512,512]{1,0:T(8,128)(2,1)S(1)}, bf16[512,512]{1,0:T(8,128)(2,1)}, u32[]{:S(2)}, u32[]{:S(2)}) collective-permute-start(bf16[512,512]{1,0:T(8,128)(2,1)S(1)} %get-tuple-element.181), channel_id=1, source_target_pairs={{0,16},{16,0},{1,17},{17,1},{2,18},{18,2},{3,19},{19,3},{4,20},{20... | collective-permute-start | bytes 1572872 | tf_op jit(solution)/shard_map/ppermute | solution.py:300
  178.3 18.8 %collective-permute-start.47 = (bf16[512,512]{0,1:T(8,128)(2,1)S(1)}, bf16[512,512]{0,1:T(8,128)(2,1)}, u32[]{:S(2)}, u32[]{:S(2)}) collective-permute-start(bf16[512,512]{0,1:T(8,128)(2,1)S(1)} %get-tuple-element.179), channel_id=1, source_target_pairs={{0,16},{16,0},{1,17},{17,1},{2,18},{18,2},{3,19},{19,3},{4,20},{20... | collective-permute-start | bytes 1572872 | tf_op jit(solution)/shard_map/ppermute | solution.py:300
  179.8 25.6 %collective-permute-start.42 = (bf16[512,512]{1,0:T(8,128)(2,1)}, bf16[512,512]{1,0:T(8,128)(2,1)}, u32[]{:S(2)}, u32[]{:S(2)}) collective-permute-start(bf16[512,512]{1,0:T(8,128)(2,1)} %get-tuple-element.182), channel_id=1, source_target_pairs={{0,2},{1,3},{2,0},{3,1},{4,6},{5,7},{6,4},{7,5},{8,10},{9,11},{10,... | collective-permute-start | bytes 1572872 | tf_op jit(solution)/shard_map/ppermute | solution.py:303
  187.4 23.8 %collective-permute-start.40 = (bf16[512,512]{1,0:T(8,128)(2,1)}, bf16[512,512]{1,0:T(8,128)(2,1)S(1)}, u32[]{:S(2)}, u32[]{:S(2)}) collective-permute-start(bf16[512,512]{1,0:T(8,128)(2,1)} %get-tuple-element.182), channel_id=1, source_target_pairs={{0,16},{16,0},{1,17},{17,1},{2,18},{18,2},{3,19},{19,3},{4,20},{20... | collective-permute-start | bytes 1572872 | tf_op jit(solution)/shard_map/ppermute | solution.py:300
  188.9 26.4 %collective-permute-start.50 = (bf16[512,512]{0,1:T(8,128)(2,1)}, bf16[512,512]{0,1:T(8,128)(2,1)S(1)}, u32[]{:S(2)}, u32[]{:S(2)}) collective-permute-start(bf16[512,512]{0,1:T(8,128)(2,1)} %get-tuple-element.180), channel_id=1, source_target_pairs={{0,2},{1,3},{2,0},{3,1},{4,6},{5,7},{6,4},{7,5},{8,10},{9,11},{10,... | collective-permute-start | bytes 1572872 | tf_op jit(solution)/shard_map/ppermute | solution.py:303
  197.1 34.4 %collective-permute-start.41 = (bf16[1024,512]{1,0:T(8,128)(2,1)S(1)}, bf16[1024,512]{1,0:T(8,128)(2,1)S(1)}, u32[]{:S(2)}, u32[]{:S(2)}) collective-permute-start(bf16[1024,512]{1,0:T(8,128)(2,1)S(1)} %pad_maximum_fusion), channel_id=1, source_target_pairs={{0,2},{1,3},{2,0},{3,1},{4,6},{5,7},{6,4},{7,5},{8,10},{9,11},{10,... | collective-permute-start | bytes 3145736 | tf_op jit(solution)/shard_map/ppermute | solution.py:303
  205.4 39.9 %collective-permute-start.48 = (bf16[512,512]{0,1:T(8,128)(2,1)S(1)}, bf16[512,512]{0,1:T(8,128)(2,1)S(1)}, u32[]{:S(2)}, u32[]{:S(2)}) collective-permute-start(bf16[512,512]{0,1:T(8,128)(2,1)S(1)} %copy-done.48), channel_id=1, source_target_pairs={{0,16},{16,0},{1,17},{17,1},{2,18},{18,2},{3,19},{19,3},{4,20},{20... | collective-permute-start | bytes 1572872 | tf_op jit(solution)/shard_map/ppermute | solution.py:300
  207.0 24.6 %collective-permute-start.43 = (bf16[512,512]{1,0:T(8,128)(2,1)}, bf16[512,512]{1,0:T(8,128)(2,1)S(1)}, u32[]{:S(2)}, u32[]{:S(2)}) collective-permute-start(bf16[512,512]{1,0:T(8,128)(2,1)} %collective-permute-done.42), channel_id=1, source_target_pairs={{0,16},{16,0},{1,17},{17,1},{2,18},{18,2},{3,19},{19,3},{4,20},{20... | collective-permute-start | bytes 1572872 | tf_op jit(solution)/shard_map/ppermute | solution.py:300
  211.3 40.3 %collective-permute-start.49 = (bf16[1024,512]{0,1:T(8,128)(2,1)S(1)}, bf16[1024,512]{0,1:T(8,128)(2,1)S(1)}, u32[]{:S(2)}, u32[]{:S(2)}) collective-permute-start(bf16[1024,512]{0,1:T(8,128)(2,1)S(1)} %pad_maximum_fusion.2), channel_id=1, source_target_pairs={{0,2},{1,3},{2,0},{3,1},{4,6},{5,7},{6,4},{7,5},{8,10},{9,11},{10,... | collective-permute-start | bytes 3145736 | tf_op jit(solution)/shard_map/ppermute | solution.py:303
  215.4 36.2 %collective-permute-start.51 = (bf16[512,512]{0,1:T(8,128)(2,1)S(1)}, bf16[512,512]{0,1:T(8,128)(2,1)S(1)}, u32[]{:S(2)}, u32[]{:S(2)}) collective-permute-start(bf16[512,512]{0,1:T(8,128)(2,1)S(1)} %collective-permute-done.50), channel_id=1, source_target_pairs={{0,16},{16,0},{1,17},{17,1},{2,18},{18,2},{3,19},{19,3},{4,20},{20... | collective-permute-start | bytes 1572872 | tf_op jit(solution)/shard_map/ppermute | solution.py:300
  243.2 55.0 %collective-permute-start.103 = (bf16[512,512]{1,0:T(8,128)(2,1)S(1)}, bf16[512,512]{1,0:T(8,128)(2,1)S(1)}, u32[]{:S(2)}, u32[]{:S(2)}) collective-permute-start(bf16[512,512]{1,0:T(8,128)(2,1)S(1)} %get-tuple-element.164), channel_id=1, source_target_pairs={{0,16},{16,0},{1,17},{17,1},{2,18},{18,2},{3,19},{19,3},{4,20},{20... | collective-permute-start | bytes 1572872 | tf_op jit(solution)/shard_map/ppermute | solution.py:300
  244.7 74.6 %collective-permute-start.102 = (bf16[512,512]{1,0:T(8,128)(2,1)S(1)}, bf16[512,512]{1,0:T(8,128)(2,1)S(1)}, u32[]{:S(2)}, u32[]{:S(2)}) collective-permute-start(bf16[512,512]{1,0:T(8,128)(2,1)S(1)} %get-tuple-element.163), channel_id=1, source_target_pairs={{0,16},{16,0},{1,17},{17,1},{2,18},{18,2},{3,19},{19,3},{4,20},{20... | collective-permute-start | bytes 1572872 | tf_op jit(solution)/shard_map/ppermute | solution.py:300
  245.3 85.7 %collective-permute-start.100 = (bf16[1024,512]{1,0:T(8,128)(2,1)}, bf16[1024,512]{1,0:T(8,128)(2,1)}, u32[]{:S(2)}, u32[]{:S(2)}) collective-permute-start(bf16[1024,512]{1,0:T(8,128)(2,1)} %slice.514), channel_id=1, source_target_pairs={{0,2},{1,3},{2,0},{3,1},{4,6},{5,7},{6,4},{7,5},{8,10},{9,11},{10,... | collective-permute-start | bytes 3145736 | tf_op jit(solution)/shard_map/ppermute | solution.py:303
  279.8 19.4 %collective-permute-start.95 = (bf16[512,512]{1,0:T(8,128)(2,1)S(1)}, bf16[512,512]{1,0:T(8,128)(2,1)S(1)}, u32[]{:S(2)}, u32[]{:S(2)}) collective-permute-start(bf16[512,512]{1,0:T(8,128)(2,1)S(1)} %get-tuple-element.166), channel_id=1, source_target_pairs={{0,16},{16,0},{1,17},{17,1},{2,18},{18,2},{3,19},{19,3},{4,20},{20... | collective-permute-start | bytes 1572872 | tf_op jit(solution)/shard_map/ppermute | solution.py:300
  281.3 47.4 %collective-permute-start.94 = (bf16[512,512]{1,0:T(8,128)(2,1)}, bf16[512,512]{1,0:T(8,128)(2,1)}, u32[]{:S(2)}, u32[]{:S(2)}) collective-permute-start(bf16[512,512]{1,0:T(8,128)(2,1)} %get-tuple-element.165), channel_id=1, source_target_pairs={{0,16},{16,0},{1,17},{17,1},{2,18},{18,2},{3,19},{19,3},{4,20},{20... | collective-permute-start | bytes 1572872 | tf_op jit(solution)/shard_map/ppermute | solution.py:300
  298.4 21.8 %collective-permute-start.104 = (bf16[512,512]{1,0:T(8,128)(2,1)S(1)}, bf16[512,512]{1,0:T(8,128)(2,1)S(1)}, u32[]{:S(2)}, u32[]{:S(2)}) collective-permute-start(bf16[512,512]{1,0:T(8,128)(2,1)S(1)} %add_convert_fusion.7), channel_id=1, source_target_pairs={{0,2},{1,3},{2,0},{3,1},{4,6},{5,7},{6,4},{7,5},{8,10},{9,11},{10,... | collective-permute-start | bytes 1572872 | tf_op jit(solution)/shard_map/ppermute | solution.py:303
  300.2 28.5 %collective-permute-start.96 = (bf16[512,512]{1,0:T(8,128)(2,1)}, bf16[512,512]{1,0:T(8,128)(2,1)}, u32[]{:S(2)}, u32[]{:S(2)}) collective-permute-start(bf16[512,512]{1,0:T(8,128)(2,1)} %add_convert_fusion.11), channel_id=1, source_target_pairs={{0,2},{1,3},{2,0},{3,1},{4,6},{5,7},{6,4},{7,5},{8,10},{9,11},{10,... | collective-permute-start | bytes 1572872 | tf_op jit(solution)/shard_map/ppermute | solution.py:303
  319.4 24.5 %collective-permute-start.92 = (bf16[1024,512]{1,0:T(8,128)(2,1)}, bf16[1024,512]{1,0:T(8,128)(2,1)}, u32[]{:S(2)}, u32[]{:S(2)}) collective-permute-start(bf16[1024,512]{1,0:T(8,128)(2,1)} %slice.499), channel_id=1, source_target_pairs={{0,2},{1,3},{2,0},{3,1},{4,6},{5,7},{6,4},{7,5},{8,10},{9,11},{10,... | collective-permute-start | bytes 3145736 | tf_op jit(solution)/shard_map/ppermute | solution.py:303
  320.2 27.4 %collective-permute-start.54 = (bf16[576,1024]{1,0:T(8,128)(2,1)}, bf16[576,1024]{1,0:T(8,128)(2,1)}, u32[]{:S(2)}, u32[]{:S(2)}) collective-permute-start(bf16[576,1024]{1,0:T(8,128)(2,1)} %convolution_convert_fusion.2), channel_id=1, source_target_pairs={{0,1},{1,0},{2,3},{3,2},{4,5},{5,4},{6,7},{7,6},{8,9},{9,8},{10,11... | collective-permute-start | bytes 3538952 | tf_op jit(solution)/shard_map/ppermute | solution.py:306
  328.7 22.5 %collective-permute-start.52 = (bf16[576,1024]{1,0:T(8,128)(2,1)}, bf16[576,1024]{1,0:T(8,128)(2,1)S(1)}, u32[]{:S(2)}, u32[]{:S(2)}) collective-permute-start(bf16[576,1024]{1,0:T(8,128)(2,1)} %convolution_convert_fusion.3), channel_id=1, source_target_pairs={{0,1},{1,0},{2,3},{3,2},{4,5},{5,4},{6,7},{7,6},{8,9},{9,8},{10,11... | collective-permute-start | bytes 3538952 | tf_op jit(solution)/shard_map/ppermute | solution.py:306
  360.1 54.3 %collective-permute-start.87 = (bf16[512,128]{0,1:T(8,128)(2,1)}, bf16[512,128]{0,1:T(8,128)(2,1)}, u32[]{:S(2)}, u32[]{:S(2)}) collective-permute-start(bf16[512,128]{0,1:T(8,128)(2,1)} %get-tuple-element.178), channel_id=1, source_target_pairs={{0,16},{16,0},{1,17},{17,1},{2,18},{18,2},{3,19},{19,3},{4,20},{20... | collective-permute-start | bytes 393224 | tf_op jit(solution)/shard_map/ppermute | solution.py:300
  377.5 38.5 %collective-permute-start.84 = (bf16[1024,128]{0,1:T(8,128)(2,1)}, bf16[1024,128]{0,1:T(8,128)(2,1)}, u32[]{:S(2)}, u32[]{:S(2)}) collective-permute-start(bf16[1024,128]{0,1:T(8,128)(2,1)} %slice.484), channel_id=1, source_target_pairs={{0,2},{1,3},{2,0},{3,1},{4,6},{5,7},{6,4},{7,5},{8,10},{9,11},{10,... | collective-permute-start | bytes 786440 | tf_op jit(solution)/shard_map/ppermute | solution.py:303
  387.3 32.7 %collective-permute-start.86 = (bf16[512,128]{0,1:T(8,128)(2,1)}, bf16[512,128]{0,1:T(8,128)(2,1)}, u32[]{:S(2)}, u32[]{:S(2)}) collective-permute-start(bf16[512,128]{0,1:T(8,128)(2,1)} %get-tuple-element.177), channel_id=1, source_target_pairs={{0,16},{16,0},{1,17},{17,1},{2,18},{18,2},{3,19},{19,3},{4,20},{20... | collective-permute-start | bytes 393224 | tf_op jit(solution)/shard_map/ppermute | solution.py:300
  414.3 25.0 %collective-permute-start.63 = (bf16[3,288,128]{2,1,0:T(8,128)(2,1)}, bf16[3,288,128]{2,1,0:T(8,128)(2,1)}, u32[]{:S(2)}, u32[]{:S(2)}) collective-permute-start(bf16[3,288,128]{2,1,0:T(8,128)(2,1)} %get-tuple-element.85), channel_id=1, source_target_pairs={{0,8},{1,9},{2,10},{3,11},{4,12},{5,13},{6,14},{7,15},{8,0},{9,1},... | collective-permute-start | bytes 663560 | tf_op jit(solution)/shard_map/ppermute | solution.py:318
  414.3 26.9 %collective-permute-start.64 = (bf16[3,288,128]{2,1,0:T(8,128)(2,1)}, bf16[3,288,128]{2,1,0:T(8,128)(2,1)}, u32[]{:S(2)}, u32[]{:S(2)}) collective-permute-start(bf16[3,288,128]{2,1,0:T(8,128)(2,1)} %get-tuple-element.86), channel_id=1, source_target_pairs={{0,4},{1,5},{2,6},{3,7},{4,8},{5,9},{6,10},{7,11},{8,12},{9,13},{1... | collective-permute-start | bytes 663560 | tf_op jit(solution)/shard_map/ppermute | solution.py:318
  420.0 21.8 %collective-permute-start.65 = (bf16[3,288,128]{2,1,0:T(8,128)(2,1)}, bf16[3,288,128]{2,1,0:T(8,128)(2,1)}, u32[]{:S(2)}, u32[]{:S(2)}) collective-permute-start(bf16[3,288,128]{2,1,0:T(8,128)(2,1)} %get-tuple-element.87), channel_id=1, source_target_pairs={{0,2},{1,3},{2,0},{3,1},{4,6},{5,7},{6,4},{7,5},{8,10},{9,11},{10,... | collective-permute-start | bytes 663560 | tf_op jit(solution)/shard_map/ppermute | solution.py:318
  421.8 21.4 %collective-permute-start.66 = (bf16[3,288,128]{2,1,0:T(8,128)(2,1)}, bf16[3,288,128]{2,1,0:T(8,128)(2,1)}, u32[]{:S(2)}, u32[]{:S(2)}) collective-permute-start(bf16[3,288,128]{2,1,0:T(8,128)(2,1)} %get-tuple-element.88), channel_id=1, source_target_pairs={{0,14},{1,15},{2,12},{3,13},{4,2},{5,3},{6,0},{7,1},{8,6},{9,7},{1... | collective-permute-start | bytes 663560 | tf_op jit(solution)/shard_map/ppermute | solution.py:318
  425.9 23.7 %collective-permute-start.67 = (bf16[3,288,128]{2,1,0:T(8,128)(2,1)}, bf16[3,288,128]{2,1,0:T(8,128)(2,1)}, u32[]{:S(2)}, u32[]{:S(2)}) collective-permute-start(bf16[3,288,128]{2,1,0:T(8,128)(2,1)} %get-tuple-element.89), channel_id=1, source_target_pairs={{0,10},{1,11},{2,8},{3,9},{4,14},{5,15},{6,12},{7,13},{8,2},{9,3},... | collective-permute-start | bytes 663560 | tf_op jit(solution)/shard_map/ppermute | solution.py:318
  441.2 36.0 %collective-permute-start.101 = (bf16[512,512]{1,0:T(8,128)(2,1)}, bf16[512,512]{1,0:T(8,128)(2,1)}, u32[]{:S(2)}, u32[]{:S(2)}) collective-permute-start(bf16[512,512]{1,0:T(8,128)(2,1)} %slice.516), channel_id=1, source_target_pairs={{0,16},{16,0},{1,17},{17,1},{2,18},{18,2},{3,19},{19,3},{4,20},{20... | collective-permute-start | bytes 1572872 | tf_op jit(solution)/shard_map/ppermute | solution.py:300
  441.8 40.8 %collective-permute-start.93 = (bf16[512,512]{1,0:T(8,128)(2,1)}, bf16[512,512]{1,0:T(8,128)(2,1)}, u32[]{:S(2)}, u32[]{:S(2)}) collective-permute-start(bf16[512,512]{1,0:T(8,128)(2,1)} %slice.501), channel_id=1, source_target_pairs={{0,16},{16,0},{1,17},{17,1},{2,18},{18,2},{3,19},{19,3},{4,20},{20... | collective-permute-start | bytes 1572872 | tf_op jit(solution)/shard_map/ppermute | solution.py:300
  443.2 40.6 %collective-permute-start.85 = (bf16[512,128]{0,1:T(8,128)(2,1)}, bf16[512,128]{0,1:T(8,128)(2,1)}, u32[]{:S(2)}, u32[]{:S(2)}) collective-permute-start(bf16[512,128]{0,1:T(8,128)(2,1)} %slice.486), channel_id=1, source_target_pairs={{0,16},{16,0},{1,17},{17,1},{2,18},{18,2},{3,19},{19,3},{4,20},{20... | collective-permute-start | bytes 393224 | tf_op jit(solution)/shard_map/ppermute | solution.py:300
  478.6 37.9 %collective-permute-start.105 = (bf16[128,1024]{1,0:T(8,128)(2,1)S(1)}, bf16[128,1024]{1,0:T(8,128)(2,1)S(1)}, u32[]{:S(2)}, u32[]{:S(2)}) collective-permute-start(bf16[128,1024]{1,0:T(8,128)(2,1)S(1)} %get-tuple-element.171), channel_id=1, source_target_pairs={{0,12},{4,0},{8,4},{12,8},{1,13},{5,1},{9,5},{13,9},{2,14},{6,2},{... | collective-permute-start | bytes 786440 | tf_op jit(solution)/shard_map/ppermute | solution.py:300
  478.8 39.0 %collective-permute-start.106 = (bf16[128,1024]{1,0:T(8,128)(2,1)S(1)}, bf16[128,1024]{1,0:T(8,128)(2,1)S(1)}, u32[]{:S(2)}, u32[]{:S(2)}) collective-permute-start(bf16[128,1024]{1,0:T(8,128)(2,1)S(1)} %get-tuple-element.173), channel_id=1, source_target_pairs={{0,8},{4,12},{8,0},{12,4},{1,9},{5,13},{9,1},{13,5},{2,10},{6,14},... | collective-permute-start | bytes 786440 | tf_op jit(solution)/shard_map/ppermute | solution.py:300
  480.7 38.5 %collective-permute-start.107 = (bf16[128,1024]{1,0:T(8,128)(2,1)S(1)}, bf16[128,1024]{1,0:T(8,128)(2,1)S(1)}, u32[]{:S(2)}, u32[]{:S(2)}) collective-permute-start(bf16[128,1024]{1,0:T(8,128)(2,1)S(1)} %get-tuple-element.172), channel_id=1, source_target_pairs={{0,4},{4,8},{8,12},{12,0},{1,5},{5,9},{9,13},{13,1},{2,6},{6,10},{... | collective-permute-start | bytes 786440 | tf_op jit(solution)/shard_map/ppermute | solution.py:300
  486.8 21.1 %collective-permute-start.90 = (bf16[128,256]{0,1:T(8,128)(2,1)S(1)}, bf16[128,256]{0,1:T(8,128)(2,1)S(1)}, u32[]{:S(2)}, u32[]{:S(2)}) collective-permute-start(bf16[128,256]{0,1:T(8,128)(2,1)S(1)} %get-tuple-element.190), channel_id=1, source_target_pairs={{0,8},{4,12},{8,0},{12,4},{1,9},{5,13},{9,1},{13,5},{2,10},{6,14},... | collective-permute-start | bytes 196616 | tf_op jit(solution)/shard_map/ppermute | solution.py:300
  496.1 23.3 %collective-permute-start.97 = (bf16[128,1024]{1,0:T(8,128)(2,1)S(1)}, bf16[128,1024]{1,0:T(8,128)(2,1)S(1)}, u32[]{:S(2)}, u32[]{:S(2)}) collective-permute-start(bf16[128,1024]{1,0:T(8,128)(2,1)S(1)} %get-tuple-element.174), channel_id=1, source_target_pairs={{0,12},{4,0},{8,4},{12,8},{1,13},{5,1},{9,5},{13,9},{2,14},{6,2},{... | collective-permute-start | bytes 786440 | tf_op jit(solution)/shard_map/ppermute | solution.py:300
  516.5 25.5 %collective-permute-start.71 = (bf16[1024,384]{0,1:T(8,128)(2,1)}, bf16[1024,384]{0,1:T(8,128)(2,1)}, u32[]{:S(2)}, u32[]{:S(2)}) collective-permute-start(bf16[1024,384]{0,1:T(8,128)(2,1)} %convolution_convert_fusion.7), channel_id=1, source_target_pairs={{0,2},{1,3},{2,0},{3,1},{4,6},{5,7},{6,4},{7,5},{8,10},{9,11},{10,... | collective-permute-start | bytes 2359304 | tf_op jit(solution)/shard_map/ppermute | solution.py:303
  517.8 53.4 %collective-permute-start.53 = (bf16[576,1024]{1,0:T(8,128)(2,1)}, bf16[576,1024]{1,0:T(8,128)(2,1)}, u32[]{:S(2)}, u32[]{:S(2)}) collective-permute-start(bf16[576,1024]{1,0:T(8,128)(2,1)} %fusion.35), channel_id=1, source_target_pairs={{0,2},{1,3},{2,0},{3,1},{4,6},{5,7},{6,4},{7,5},{8,10},{9,11},{10,... | collective-permute-start | bytes 3538952 | tf_op jit(solution)/shard_map/ppermute | solution.py:303
  519.2 17.7 %collective-permute-start.98 = (bf16[128,1024]{1,0:T(8,128)(2,1)S(1)}, bf16[128,1024]{1,0:T(8,128)(2,1)S(1)}, u32[]{:S(2)}, u32[]{:S(2)}) collective-permute-start(bf16[128,1024]{1,0:T(8,128)(2,1)S(1)} %get-tuple-element.176), channel_id=1, source_target_pairs={{0,8},{4,12},{8,0},{12,4},{1,9},{5,13},{9,1},{13,5},{2,10},{6,14},... | collective-permute-start | bytes 786440 | tf_op jit(solution)/shard_map/ppermute | solution.py:300
  519.4 19.0 %collective-permute-start.99 = (bf16[128,1024]{1,0:T(8,128)(2,1)S(1)}, bf16[128,1024]{1,0:T(8,128)(2,1)S(1)}, u32[]{:S(2)}, u32[]{:S(2)}) collective-permute-start(bf16[128,1024]{1,0:T(8,128)(2,1)S(1)} %get-tuple-element.175), channel_id=1, source_target_pairs={{0,4},{4,8},{8,12},{12,0},{1,5},{5,9},{9,13},{13,1},{2,6},{6,10},{... | collective-permute-start | bytes 786440 | tf_op jit(solution)/shard_map/ppermute | solution.py:300
  526.4 48.9 %collective-permute-start.69 = (bf16[576,1024]{1,0:T(8,128)(2,1)}, bf16[576,1024]{1,0:T(8,128)(2,1)}, u32[]{:S(2)}, u32[]{:S(2)}) collective-permute-start(bf16[576,1024]{1,0:T(8,128)(2,1)} %get-tuple-element.91), channel_id=1, source_target_pairs={{0,1},{1,0},{2,3},{3,2},{4,5},{5,4},{6,7},{7,6},{8,9},{9,8},{10,11... | collective-permute-start | bytes 3538952 | tf_op jit(solution)/shard_map/ppermute | solution.py:306
  538.4 30.7 %collective-permute-start.75 = (bf16[512,384]{0,1:T(8,128)(2,1)}, bf16[512,384]{0,1:T(8,128)(2,1)}, u32[]{:S(2)}, u32[]{:S(2)}) collective-permute-start(bf16[512,384]{0,1:T(8,128)(2,1)} %add_convert_fusion.15), channel_id=1, source_target_pairs={{0,2},{1,3},{2,0},{3,1},{4,6},{5,7},{6,4},{7,5},{8,10},{9,11},{10,... | collective-permute-start | bytes 1179656 | tf_op jit(solution)/shard_map/ppermute | solution.py:303
  544.5 42.0 %collective-permute-start.72 = (bf16[512,384]{0,1:T(8,128)(2,1)}, bf16[512,384]{0,1:T(8,128)(2,1)}, u32[]{:S(2)}, u32[]{:S(2)}) collective-permute-start(bf16[512,384]{0,1:T(8,128)(2,1)} %slice.463), channel_id=1, source_target_pairs={{0,16},{16,0},{1,17},{17,1},{2,18},{18,2},{3,19},{19,3},{4,20},{20... | collective-permute-start | bytes 1179656 | tf_op jit(solution)/shard_map/ppermute | solution.py:300
  590.4 27.6 %collective-permute-start.76 = (bf16[128,768]{0,1:T(8,128)(2,1)}, bf16[128,768]{0,1:T(8,128)(2,1)}, u32[]{:S(2)}, u32[]{:S(2)}) collective-permute-start(bf16[128,768]{0,1:T(8,128)(2,1)} %get-tuple-element.183), channel_id=1, source_target_pairs={{0,12},{4,0},{8,4},{12,8},{1,13},{5,1},{9,5},{13,9},{2,14},{6,2},{... | collective-permute-start | bytes 589832 | tf_op jit(solution)/shard_map/ppermute | solution.py:300
  603.4 25.1 %collective-permute-start.70 = (bf16[576,1024]{1,0:T(8,128)(2,1)}, bf16[576,1024]{1,0:T(8,128)(2,1)}, u32[]{:S(2)}, u32[]{:S(2)}) collective-permute-start(bf16[576,1024]{1,0:T(8,128)(2,1)} %fusion.37), channel_id=1, source_target_pairs={{0,2},{1,3},{2,0},{3,1},{4,6},{5,7},{6,4},{7,5},{8,10},{9,11},{10,... | collective-permute-start | bytes 3538952 | tf_op jit(solution)/shard_map/ppermute | solution.py:303
  (147 other events, 1599.4 us)

commit v2 on v1

v2 whole, which is shorter than its diff:
```python
import functools

import jax
import jax.numpy as jnp
from jax import lax
from jax.experimental import pallas as pl
from jax.experimental.pallas import tpu as pltpu
from jax.sharding import Mesh
from jax.sharding import PartitionSpec as P

HD = 64
LANES = 128
CORES = 2
SMALL_ROWS = 16
SMALL_LANES = 3 * LANES

eps_norm = 1e-06
masked_score = -1e30
root_half = 0.7071067811865476
inv_root_two_pi = 0.3989422804014327
score_scale = HD ** (-0.5)

bf16 = jnp.bfloat16
f32 = jnp.float32
NN = (((1,), (0,)), ((), ()))
NT = (((1,), (1,)), ((), ()))

B_OUT, B_DOWN, GAIN1, SHIFT1, GAIN2, SHIFT2, SCALE1, SCALE2 = range(8)


def mm(left, right, dims=NN):
    return lax.dot_general(left, right, dims, preferred_element_type=f32)


def turn(values):
    return jnp.transpose(values.astype(f32)).astype(bf16)


def normalise(values):
    average = jnp.mean(values, axis=-1, keepdims=True)
    centred = values - average
    variance = jnp.mean(centred * centred, axis=-1, keepdims=True)
    inv_std = lax.rsqrt(variance + eps_norm)
    return centred * inv_std, inv_std


def norm_back(grad_in, normed, inv_std):
    first_mean = jnp.mean(grad_in, axis=-1, keepdims=True)
    second_mean = jnp.mean(grad_in * normed, axis=-1, keepdims=True)
    return inv_std * (grad_in - first_mean - normed * second_mean)


def row(table, index):
    return table[index : index + 1, :]


def column_sum(values):
    return jnp.sum(values, axis=0, keepdims=True)


def low_lanes(shape):
    return lax.broadcasted_iota(jnp.int32, shape, 1) < HD


def swap(values):
    return pltpu.roll(values, HD, 1)


def fold(wide):
    half = wide.shape[0] // 2
    return wide[:half] + swap(wide[half:])


def unfold(folded):
    low = low_lanes(folded.shape)
    return jnp.concatenate(
        [jnp.where(low, folded, 0.0), jnp.where(low, swap(folded), 0.0)], axis=0
    )


def owner_of(place_ref, slot, context):
    z, y = place_ref[1], place_ref[2]
    group = y if slot < context else 1 - y
    return group * context + lax.rem(z + slot % context, context)


def spread_mask(sc, last, columns):
    entry = lax.broadcasted_iota(jnp.int32, (LANES, columns), 0)
    column = lax.broadcasted_iota(jnp.int32, (LANES, columns), 1)
    return jnp.where(
        (entry < last) & (lax.rem(column, HD) == sc * last + entry), 1.0, 0.0
    ).astype(bf16)


def stack_kernel(place_ref, *refs):
    count = (len(refs) - 3) // 2
    pieces, smalls = refs[:count], refs[count : 2 * count]
    top_ref, bottom_ref, whole = refs[2 * count :]
    z = place_ref[1]
    rows = pieces[0].shape[0]
    split = top_ref.shape[0]
    whole[count * rows :, :] = jnp.zeros_like(whole[count * rows :, :])
    for j in range(count):
        spot = lax.rem(z - j + count, count)
        whole[pl.ds(pl.multiple_of(spot * rows, 16), rows), :] = pieces[j][...]
        start = pl.multiple_of(count * rows + spot * SMALL_ROWS, 16)
        whole[pl.ds(start, SMALL_ROWS), :SMALL_LANES] = smalls[j][...]
    top_ref[...] = whole[:split]
    bottom_ref[...] = whole[split:]


def qkv_kernel(sizes, place_ref, x_ref, *refs):
    n_shard, n_context, images, last, blocks = sizes
    n_stack = 4 * n_shard
    stacks, outs = refs[:n_stack], refs[n_stack : n_stack + blocks]
    norm_ref, wqkv_ref, wout_ref, vec_ref, bup_ref = refs[n_stack + blocks : n_stack + blocks + 5]
    scratch, bias_ref = refs[n_stack + blocks + 5 :]
    x, y = place_ref[0], place_ref[2]
    width = x_ref.shape[1]
    part_rows = width // n_shard
    piece_rows = part_rows // n_context
    head_columns = wout_ref.shape[2]
    qkv_columns = wqkv_ref.shape[2]
    up_columns = bup_ref.shape[2]
    vec = None
    for yr in range(2):
        y_spot = y if yr == 0 else 1 - y
        up, qv = None, None
        for xr in range(n_shard):
            x_spot = lax.rem(x - xr + n_shard, n_shard)
            top, bottom = stacks[4 * xr + 2 * yr], stacks[4 * xr + 2 * yr + 1]
            split = top.shape[0]
            start = pl.multiple_of(x_spot * part_rows, 16)
            here = pl.ds(start, split)
            wqkv_ref[y_spot, here, :] = top[:, :qkv_columns]
            wout_ref[y_spot, here, :] = top[:, qkv_columns:]
            rest = part_rows - split
            there = pl.ds(start + split, rest)
            wqkv_ref[y_spot, there, :] = bottom[:rest, :qkv_columns]
            wout_ref[y_spot, there, :] = bottom[:rest, qkv_columns:]
            for c in range(n_context):
                sc = x_spot * n_context + c
                lines = slice(rest + c * SMALL_ROWS, rest + (c + 1) * SMALL_ROWS)
                if yr == 0:
                    entry = lax.broadcasted_iota(jnp.int32, (LANES, width), 0)
                    column = lax.broadcasted_iota(jnp.int32, (LANES, width), 1)
                    place = jnp.where(
                        (entry < piece_rows) & (column == sc * piece_rows + entry), 1.0, 0.0
                    ).astype(bf16)
                    term = mm(bottom[lines, :LANES], place)
                    vec = term if vec is None else vec + term
                term = mm(bottom[lines, LANES : 2 * LANES], spread_mask(sc, last, up_columns))
                up = term if up is None else up + term
                term = mm(bottom[lines, 2 * LANES : 3 * LANES], spread_mask(sc, last, head_columns))
                qv = term if qv is None else qv + term
        line = lax.broadcasted_iota(jnp.int32, up.shape, 0)
        column = lax.broadcasted_iota(jnp.int32, up.shape, 1)
        bup_ref[y_spot] = column_sum(jnp.where(column // HD == line, up, 0.0))
        heads = head_columns // HD
        line = lax.broadcasted_iota(jnp.int32, qv.shape, 0)
        column = lax.broadcasted_iota(jnp.int32, qv.shape, 1) // HD
        bias_ref[y_spot, 0:1, :] = column_sum(jnp.where(column == line, qv, 0.0))
        bias_ref[y_spot, 1:2, :] = column_sum(jnp.where(column + heads == line, qv, 0.0))
    vec_ref[...] = vec
    rows = x_ref.shape[0] // images
    half = rows // 2
    normed, _ = normalise(x_ref[...].astype(f32))
    norm_low = (normed * row(vec, GAIN1) + row(vec, SHIFT1)).astype(bf16)
    norm_ref[...] = norm_low
    low = low_lanes((rows, LANES))
    low_half = low_lanes((half, LANES))
    for group in range(2):
        block = mm(norm_low, wqkv_ref[group])
        queries = block[:, :head_columns] + bias_ref[group, 0:1, :]
        keys = block[:, head_columns : 2 * head_columns]
        values = block[:, 2 * head_columns :] + bias_ref[group, 1:2, :]
        for pair in range(head_columns // LANES):
            lanes = slice(pair * LANES, (pair + 1) * LANES)
            head = group * n_context + 2 * pair
            for image in range(images):
                lines = slice(image * rows, (image + 1) * rows)
                query, key, value = queries[lines, lanes], keys[lines, lanes], values[lines, lanes]
                scratch[head, image, :rows] = jnp.where(low, query, swap(key)).astype(bf16)
                scratch[head + 1, image, :rows] = jnp.where(low, swap(query), key).astype(bf16)
                scratch[head, image, rows:] = jnp.where(
                    low_half, value[:half], swap(value[half:])
                ).astype(bf16)
                scratch[head + 1, image, rows:] = jnp.where(
                    low_half, swap(value[:half]), value[half:]
                ).astype(bf16)
    for slot in range(blocks):
        outs[slot][...] = scratch[owner_of(place_ref, slot, n_context)]


def attend_kernel(count_ref, pos_ref, *refs):
    blocks = (len(refs) - 3) // 2
    packs, outs, log_ref, keys, values = (
        refs[:blocks],
        refs[blocks : 2 * blocks],
        refs[2 * blocks],
        refs[2 * blocks + 1],
        refs[2 * blocks + 2],
    )
    rows = packs[0].shape[1] * 2 // 3
    low = low_lanes((rows, LANES))
    for j in range(blocks):
        pack = packs[j][0].astype(f32)
        keys[j * rows : (j + 1) * rows] = jnp.where(low, swap(pack[:rows]), 0.0).astype(bf16)
        values[j * rows : (j + 1) * rows] = unfold(pack[rows:]).astype(bf16)
    valid = pos_ref[...] < count_ref[pl.program_id(0)]
    for j in range(blocks):
        query = packs[j][0, :rows] * bf16(score_scale)
        scores = jnp.where(valid, mm(query, keys[...], NT), masked_score)
        highest = jnp.max(scores, axis=1, keepdims=True)
        exponent = jnp.exp(scores - highest)
        total = jnp.sum(exponent, axis=1, keepdims=True)
        mixed = mm(exponent.astype(bf16), values[...]) / total
        outs[j][0] = fold(mixed).astype(bf16)
        log_ref[0, j * rows : (j + 1) * rows] = highest + jnp.log(total)


def attend_back_kernel(count_ref, pos_ref, log_ref, *refs):
    blocks = (len(refs) - 4) // 4
    packs, mixes, grads, outs = (refs[i * blocks : (i + 1) * blocks] for i in range(4))
    keys, values, sums, query_grads = refs[4 * blocks :]
    rows = packs[0].shape[1] * 2 // 3
    half = rows // 2
    low = low_lanes((rows, LANES))
    low_half = low_lanes((half, LANES))
    for j in range(blocks):
        pack = packs[j][0].astype(f32)
        keys[j * rows : (j + 1) * rows] = jnp.where(low, swap(pack[:rows]), 0.0).astype(bf16)
        values[j * rows : (j + 1) * rows] = unfold(pack[rows:]).astype(bf16)
    valid = pos_ref[...] < count_ref[pl.program_id(0)]
    for j in range(blocks):
        query = packs[j][0, :rows] * bf16(score_scale)
        grad_wide = unfold(grads[j][0].astype(f32))
        mix_wide = unfold(mixes[j][0].astype(f32))
        delta = jnp.sum(grad_wide * mix_wide, axis=1, keepdims=True)
        grad = grad_wide.astype(bf16)
        scores = jnp.where(valid, mm(query, keys[...], NT), masked_score)
        probs = jnp.exp(scores - log_ref[0, j * rows : (j + 1) * rows])
        weight_grad = mm(grad, values[...], NT)
        score_grad = (probs * (weight_grad - delta)).astype(bf16)
        query_grads[j] = mm(score_grad, keys[...]) * score_scale
        query_t = jnp.transpose(query.astype(f32))[:HD].astype(bf16)
        grad_t = jnp.transpose(grad_wide)[:HD].astype(bf16)
        key_part = mm(query_t, score_grad)
        value_part = mm(grad_t, probs.astype(bf16))
        if j == 0:
            sums[:HD] = key_part
            sums[HD:] = value_part
        else:
            sums[:HD] = sums[:HD] + key_part
            sums[HD:] = sums[HD:] + value_part
    for j in range(blocks):
        both = jnp.transpose(sums[:, j * rows : (j + 1) * rows])
        outs[j][0, :rows] = jnp.where(low, query_grads[j], swap(both)).astype(bf16)
        outs[j][0, rows:] = jnp.where(low_half, swap(both[:half]), both[half:]).astype(bf16)


def project_kernel(n_context, place_ref, *refs):
    blocks = len(refs) - 4
    folded, (weight_ref, mixed_ref, part_ref, scratch) = refs[:blocks], refs[blocks:]
    images, half, _ = folded[0].shape
    rows = 2 * half
    for slot in range(blocks):
        scratch[owner_of(place_ref, slot, n_context)] = folded[slot][...]
    low = low_lanes((half, LANES))
    for pair in range(blocks // 2):
        columns = slice(pair * LANES, (pair + 1) * LANES)
        for image in range(images):
            first = scratch[2 * pair, image].astype(f32)
            second = scratch[2 * pair + 1, image].astype(f32)
            start = image * rows
            mixed_ref[start : start + half, columns] = jnp.where(
                low, first, swap(second)
            ).astype(bf16)
            mixed_ref[start + half : start + rows, columns] = jnp.where(
                low, swap(first), second
            ).astype(bf16)
    size = weight_ref.shape[2]
    part_ref[...] = (
        mm(mixed_ref[:, :size], weight_ref[0], NT) + mm(mixed_ref[:, size:], weight_ref[1], NT)
    ).astype(bf16)


def mlp_kernel(
    x_ref, cot_ref, part_ref, other_ref, vec_ref, bup_ref, feed_ref,
    norm_ref, grad_ref, act_ref, pre_ref, parts_ref, gup_ref,
):
    tokens = x_ref.shape[0]
    vec = vec_ref[...]
    branch = part_ref[...].astype(f32) + other_ref[...].astype(f32) + row(vec, B_OUT)
    middle = x_ref[...].astype(f32) + row(vec, SCALE1) * branch
    normed, _ = normalise(middle)
    norm_low = (normed * row(vec, GAIN2) + row(vec, SHIFT2)).astype(bf16)
    norm_ref[...] = norm_low
    branch_grad = (row(vec, SCALE2) * cot_ref[...].astype(f32)).astype(bf16)
    grad_ref[...] = branch_grad
    width = x_ref.shape[1]
    per_group = feed_ref.shape[1] // 2
    step = per_group // 2
    down, back = None, None
    for group in range(2):
        lines = slice(group * width, (group + 1) * width)
        for part in range(2):
            columns = slice(part * step, (part + 1) * step)
            up = feed_ref[lines, columns]
            turned = feed_ref[lines, per_group + part * step : per_group + (part + 1) * step]
            target = slice(group * per_group + part * step, group * per_group + (part + 1) * step)
            pre = mm(norm_low, up) + bup_ref[group, :, columns]
            erf_term = 0.5 * (1.0 + lax.erf(pre * root_half))
            act = (pre * erf_term).astype(bf16)
            act_ref[:, target] = act
            term = mm(act, turned, NT)
            down = term if down is None else down + term
            slope = erf_term + pre * inv_root_two_pi * jnp.exp(-0.5 * pre * pre)
            pre_grad = (mm(branch_grad, turned) * slope).astype(bf16)
            pre_ref[:, target] = pre_grad
            gup_ref[:, target] = column_sum(pre_grad.astype(f32))
            term = mm(pre_grad, up, NT)
            back = term if back is None else back + term
    parts_ref[:tokens] = down.astype(bf16)
    parts_ref[tokens:] = back.astype(bf16)


def mlp_weights_kernel(norm_ref, grad_ref, act_ref, pre_ref, out_ref):
    width = norm_ref.shape[1]
    per_group = act_ref.shape[1] // 2
    norm_t, grad_t = turn(norm_ref[...]), turn(grad_ref[...])
    for group in range(2):
        columns = slice(group * per_group, (group + 1) * per_group)
        lines = slice(group * width, (group + 1) * width)
        out_ref[lines, :per_group] = mm(norm_t, pre_ref[:, columns]).astype(bf16)
        out_ref[lines, per_group:] = mm(grad_t, act_ref[:, columns]).astype(bf16)


def back_kernel(
    images, n_context, place_ref, x_ref, cot_ref, part_ref, other_ref, parts_ref, others_ref,
    vec_ref, weight_ref, *refs
):
    result_ref, middle_grad_ref, proj_ref, sums_ref = refs[:4]
    outs, scratch = refs[4:-1], refs[-1]
    tokens = x_ref.shape[0]
    vec = vec_ref[...]
    upstream = cot_ref[...].astype(f32)
    branch = part_ref[...].astype(f32) + other_ref[...].astype(f32) + row(vec, B_OUT)
    middle = x_ref[...].astype(f32) + row(vec, SCALE1) * branch
    normed, inv_std = normalise(middle)
    mlp = parts_ref[:tokens].astype(f32) + others_ref[:tokens].astype(f32) + row(vec, B_DOWN)
    result_ref[...] = (middle + row(vec, SCALE2) * mlp).astype(bf16)
    norm_grad = parts_ref[tokens:].astype(f32) + others_ref[tokens:].astype(f32)
    middle_grad = upstream + norm_back(norm_grad * row(vec, GAIN2), normed, inv_std)
    middle_grad_ref[...] = middle_grad
    proj_wide = row(vec, SCALE1) * middle_grad
    proj = proj_wide.astype(bf16)
    proj_ref[...] = proj
    sums_ref[...] = jnp.zeros_like(sums_ref)
    for place, value in (
        (B_OUT, proj_wide),
        (B_DOWN, row(vec, SCALE2) * upstream),
        (GAIN2, norm_grad * normed),
        (SHIFT2, norm_grad),
        (SCALE1, middle_grad * branch),
        (SCALE2, upstream * mlp),
    ):
        sums_ref[place : place + 1, :] = column_sum(value)
    rows = tokens // images
    half = rows // 2
    low = low_lanes((half, LANES))
    size = weight_ref.shape[2]
    for group in range(2):
        wide = mm(proj, weight_ref[group])
        for pair in range(size // LANES):
            head = group * n_context + 2 * pair
            for image in range(images):
                block = wide[image * rows : (image + 1) * rows, pair * LANES : (pair + 1) * LANES]
                first, second = block[:half], block[half:]
                scratch[head, image] = jnp.where(low, first, swap(second)).astype(bf16)
                scratch[head + 1, image] = jnp.where(low, swap(first), second).astype(bf16)
    for slot in range(len(outs)):
        outs[slot][...] = scratch[owner_of(place_ref, slot, n_context)]


def qkv_back_kernel(sizes, place_ref, *refs):
    n_shard, n_context, blocks = sizes
    packs = refs[:blocks]
    weight_ref, norm_ref, proj_ref, mixed_ref = refs[blocks : blocks + 4]
    part_ref, sum_ref = refs[blocks + 4 : blocks + 6]
    quads = refs[blocks + 6 : -2]
    scratch, grads = refs[-2:]
    images = packs[0].shape[0]
    rows = packs[0].shape[1] * 2 // 3
    half = rows // 2
    columns = mixed_ref.shape[1] // 2
    for slot in range(blocks):
        scratch[owner_of(place_ref, slot, n_context)] = packs[slot][...]
    low = low_lanes((rows, LANES))
    low_half = low_lanes((half, LANES))
    total = None
    for group in range(2):
        for pair in range(columns // LANES):
            head = group * n_context + 2 * pair
            lanes = slice(pair * LANES, (pair + 1) * LANES)
            for image in range(images):
                first = scratch[head, image].astype(f32)
                second = scratch[head + 1, image].astype(f32)
                start = image * rows
                here = slice(start, start + rows)
                grads[group, 0, here, lanes] = jnp.where(
                    low, first[:rows], swap(second[:rows])
                ).astype(bf16)
                grads[group, 1, here, lanes] = jnp.where(
                    low, swap(first[:rows]), second[:rows]
                ).astype(bf16)
                grads[group, 2, start : start + half, lanes] = jnp.where(
                    low_half, first[rows:], swap(second[rows:])
                ).astype(bf16)
                grads[group, 2, start + half : start + rows, lanes] = jnp.where(
                    low_half, swap(first[rows:]), second[rows:]
                ).astype(bf16)
        for part in range(3):
            term = mm(
                grads[group, part],
                weight_ref[group, :, part * columns : (part + 1) * columns],
                NT,
            )
            total = term if total is None else total + term
        sum_ref[group, 0:1, :] = column_sum(grads[group, 0].astype(f32))
        sum_ref[group, 1:2, :] = column_sum(grads[group, 2].astype(f32))
    part_ref[...] = total.astype(bf16)
    x, y = place_ref[0], place_ref[2]
    part_rows = norm_ref.shape[1] // n_shard
    split = part_rows // 2
    for xr in range(n_shard):
        x_spot = lax.rem(x - xr + n_shard, n_shard)
        lanes = pl.ds(pl.multiple_of(x_spot * part_rows, LANES), part_rows)
        norm_part, proj_part = turn(norm_ref[:, lanes]), turn(proj_ref[:, lanes])
        for yr in range(2):
            y_spot = y if yr == 0 else 1 - y
            top, bottom = quads[4 * xr + 2 * yr], quads[4 * xr + 2 * yr + 1]
            mixed = mixed_ref[:, pl.ds(pl.multiple_of(y_spot * columns, LANES), columns)]
            for part in range(4):
                if part < 3:
                    value = mm(norm_part, grads[y_spot, part])
                else:
                    value = mm(proj_part, mixed)
                place = slice(part * columns, (part + 1) * columns)
                top[:, place] = value[:split].astype(bf16)
                bottom[:, place] = value[split:].astype(bf16)


def finish_kernel(
    sizes, place_ref, x_ref, middle_grad_ref, part_ref, other_ref, vec_ref, sums_ref, gup_ref,
    gqv_ref, out_ref, own_ref, far_ref,
):
    n_shard, n_context, last = sizes
    x, z, y = place_ref[0], place_ref[1], place_ref[2]
    width = x_ref.shape[1]
    piece_rows = width // (n_shard * n_context)
    norm_grad = part_ref[...].astype(f32) + other_ref[...].astype(f32)
    normed, inv_std = normalise(x_ref[...].astype(f32))
    gain = vec_ref[GAIN1 : GAIN1 + 1, :]
    out_ref[...] = (
        middle_grad_ref[...] + norm_back(norm_grad * gain, normed, inv_std)
    ).astype(bf16)
    line = lax.broadcasted_iota(jnp.int32, sums_ref.shape, 0)
    sums = jnp.where(line == GAIN1, column_sum(norm_grad * normed), sums_ref[...])
    sums = jnp.where(line == SHIFT1, column_sum(norm_grad), sums).astype(bf16)
    heads = gqv_ref.shape[2] // HD
    for target, y_spot in ((own_ref, y), (far_ref, 1 - y)):
        up = gup_ref[y_spot]
        line = lax.broadcasted_iota(jnp.int32, (SMALL_ROWS, up.shape[1]), 0)
        column = lax.broadcasted_iota(jnp.int32, (SMALL_ROWS, up.shape[1]), 1) // HD
        up = jnp.where(column == line, up, 0.0).astype(bf16)
        both = gqv_ref[y_spot]
        line = lax.broadcasted_iota(jnp.int32, (SMALL_ROWS, both.shape[1]), 0)
        column = lax.broadcasted_iota(jnp.int32, (SMALL_ROWS, both.shape[1]), 1) // HD
        qv = jnp.where(column == line, both[0:1], 0.0)
        qv = (qv + jnp.where(column + heads == line, both[1:2], 0.0)).astype(bf16)
        for xr in range(n_shard):
            for zr in range(n_context):
                sc = lax.rem(x - xr + n_shard, n_shard) * n_context
                sc = sc + lax.rem(z - zr + n_context, n_context)
                start = (xr * n_context + zr) * SMALL_ROWS
                lines = slice(start, start + SMALL_ROWS)
                entry = lax.broadcasted_iota(jnp.int32, (LANES, width), 0)
                column = lax.broadcasted_iota(jnp.int32, (LANES, width), 1)
                place = jnp.where(
                    (entry < piece_rows) & (column == sc * piece_rows + entry), 1.0, 0.0
                ).astype(bf16)
                target[lines, :LANES] = mm(sums, place, NT)
                target[lines, LANES : 2 * LANES] = mm(
                    up, spread_mask(sc, last, up.shape[1]), NT
                )
                target[lines, 2 * LANES :] = mm(qv, spread_mask(sc, last, qv.shape[1]), NT)


def deal_kernel(place_ref, *refs):
    own_top, own_bottom = refs[0], refs[1]
    tops, bottoms, outs, whole = refs[2], refs[3], refs[4], refs[5]
    z = place_ref[1]
    split = own_top.shape[0]
    count = len(outs)
    top, bottom = own_top[...].astype(f32), own_bottom[...].astype(f32)
    for ref in tops:
        top = top + ref[...].astype(f32)
    for ref in bottoms:
        bottom = bottom + ref[...].astype(f32)
    whole[:split] = top
    whole[split:] = bottom
    rows = 2 * split // count
    for j in range(count):
        spot = lax.rem(z - j + count, count)
        value = whole[pl.ds(pl.multiple_of(spot * rows, 16), rows), :]
        outs[j][...] = value.astype(outs[j].dtype)


def merge_kernel(place_ref, own_ref, near_ref, far_ref, out_ref):
    y, core = place_ref[2], place_ref[3]
    images, _, width = out_ref.shape
    tokens = own_ref.shape[0]
    rows = tokens // images
    half = tokens // 2
    other = lambda first: jnp.where(core == first, near_ref[...], far_ref[...])
    first, second = other(0).astype(f32), other(1).astype(f32)
    both = jnp.concatenate([first, second], axis=0)
    for image in range(images):
        lines = slice(image * rows, (image + 1) * rows)
        here = pl.ds(pl.multiple_of(y * rows, 8), rows)
        there = pl.ds(pl.multiple_of((1 - y) * rows, 8), rows)
        out_ref[image, here, :] = own_ref[lines, :].astype(f32)
        out_ref[image, there, :] = both[lines]


def vmem():
    return pl.BlockSpec(memory_space=pltpu.VMEM)


def smem():
    return pl.BlockSpec(memory_space=pltpu.SMEM)


def shaped(shape, dtype):
    return jax.ShapeDtypeStruct(shape, dtype)


def call(kernel, name, out_shape, scratch, place, *operands):
    return pl.pallas_call(
        kernel,
        name=name,
        in_specs=[smem()] + [vmem()] * len(operands),
        out_specs=[vmem()] * len(out_shape),
        out_shape=out_shape,
        scratch_shapes=scratch,
    )(place, *operands)


def per_device(sizes, *args):
    (
        tokens_in,
        counts,
        w_qkv,
        b_qv,
        w_out,
        b_out,
        w_up,
        b_up,
        w_down,
        b_down,
        norm1_gain,
        norm1_bias,
        norm2_gain,
        norm2_bias,
        scale1,
        scale2,
        cotangent,
    ) = args
    n_shard, n_context, n_y = sizes
    images, row_count, width = tokens_in.shape
    piece_rows = w_qkv.shape[0]
    head_columns = w_qkv.shape[2]
    hidden = w_up.shape[1]
    last = b_up.shape[1]
    rows = row_count // n_y
    half = rows // 2
    tokens = images * rows
    x = lax.axis_index("shard")
    z = lax.axis_index("context")
    y = lax.axis_index("y")
    core = lax.axis_index("core")
    place = jnp.stack([x, z, y, core]).astype(jnp.int32)
    blocks = n_y * n_context
    everyone = ("y", "shard", "context")

    def send(value, axis, step):
        size = {"shard": n_shard, "context": n_context}[axis]
        return lax.ppermute(value, axis, [(i, (i + step) % size) for i in range(size)])

    def across(value):
        return lax.ppermute(value, "y", [(0, 1), (1, 0)])

    def partner(value):
        return lax.ppermute(value, "core", [(0, 1), (1, 0)])

    def hand_over(values, back):
        out = [values[0]]
        for slot in range(1, blocks):
            jy, jz = slot // n_context, slot % n_context
            step = -jz if back else jz
            pairs = [
                (i * n_y + t, (i + step) % n_context * n_y + (t ^ jy))
                for i in range(n_context)
                for t in range(n_y)
            ]
            out.append(lax.ppermute(values[slot], ("context", "y"), pairs))
        return out

    feed = lax.all_gather(
        jnp.concatenate([w_up, w_down.T], axis=1), everyone, axis=0, tiled=True
    )

    piece = jnp.concatenate([w_qkv.reshape(piece_rows, -1), w_out.T], axis=1)
    vectors = [b_out, b_down, norm1_gain, norm1_bias, norm2_gain, norm2_bias, scale1, scale2]

    def block_of(value):
        return jnp.pad(value, ((0, SMALL_ROWS - value.shape[0]), (0, LANES - value.shape[1])))

    small = jnp.concatenate(
        [block_of(jnp.stack(vectors)), block_of(b_up), block_of(b_qv.reshape(-1, last))], axis=1
    )
    pieces = [piece] + [send(piece, "context", j) for j in range(1, n_context)]
    smalls = [small] + [send(small, "context", j) for j in range(1, n_context)]
    stack_rows = n_context * (piece_rows + SMALL_ROWS)
    split = stack_rows // 2
    columns = piece.shape[1]
    top, bottom = call(
        stack_kernel,
        "stack",
        [shaped((split, columns), bf16)] * 2,
        [pltpu.VMEM((stack_rows, columns), bf16)],
        place,
        *pieces,
        *smalls,
    )
    y_bottom = across(bottom)
    x_tops = [send(top, "shard", j) for j in range(1, n_shard)]
    x_bottoms = [send(bottom, "shard", j) for j in range(1, n_shard)]
    y_top = across(top)
    far_tops = [across(value) for value in x_tops]
    far_bottoms = [send(y_bottom, "shard", j) for j in range(1, n_shard)]
    stacks = [top, bottom, y_top, y_bottom]
    for j in range(n_shard - 1):
        stacks += [x_tops[j], x_bottoms[j], far_tops[j], far_bottoms[j]]

    def own_rows(array):
        return lax.dynamic_slice_in_dim(array, y * rows, rows, 1).reshape(tokens, width)

    residual = own_rows(tokens_in)
    upstream = own_rows(cotangent)

    pack_rows = rows + half
    packed = call(
        functools.partial(qkv_kernel, (n_shard, n_context, images, last, blocks)),
        "qkv",
        [shaped((images, pack_rows, LANES), bf16)] * blocks
        + [
            shaped((tokens, width), bf16),
            shaped((n_y, width, 3 * head_columns), bf16),
            shaped((n_y, width, head_columns), bf16),
            shaped((SMALL_ROWS, width), f32),
            shaped((n_y, 1, hidden), f32),
        ],
        [
            pltpu.VMEM((blocks, images, pack_rows, LANES), bf16),
            pltpu.VMEM((n_y, 8, head_columns), f32),
        ],
        place,
        residual,
        *stacks,
    )
    norm_low1, wqkv, wout, vec, bup = packed[blocks:]
    packs = hand_over(packed[:blocks], False)

    slot = jnp.arange(blocks)
    source = (z - slot % n_context) % n_context * row_count + (y ^ (slot // n_context)) * rows
    key_place = (source[:, None] + jnp.arange(rows)[None, :]).reshape(1, -1).astype(jnp.int32)
    length = blocks * rows
    pack_spec = pl.BlockSpec((1, pack_rows, LANES), lambda i: (i, 0, 0))
    fold_spec = pl.BlockSpec((1, half, LANES), lambda i: (i, 0, 0))
    pos_spec = pl.BlockSpec((1, length), lambda i: (0, 0))
    log_spec = pl.BlockSpec((1, length, 1), lambda i: (i, 0, 0))
    attended = pl.pallas_call(
        attend_kernel,
        name="attend",
        grid=(images,),
        in_specs=[smem(), pos_spec] + [pack_spec] * blocks,
        out_specs=[fold_spec] * blocks + [log_spec],
        out_shape=[shaped((images, half, LANES), bf16)] * blocks
        + [shaped((images, length, 1), f32)],
        scratch_shapes=[pltpu.VMEM((length, LANES), bf16)] * 2,
    )(counts, key_place, *packs)
    mixes, log_total = attended[:blocks], attended[blocks]
    folded = hand_over(mixes, True)

    fold_scratch = pltpu.VMEM((blocks, images, half, LANES), bf16)
    mixture, proj_part = call(
        functools.partial(project_kernel, n_context),
        "project",
        [shaped((tokens, blocks * HD), bf16), shaped((tokens, width), bf16)],
        [fold_scratch],
        place,
        *folded,
        wout,
    )
    proj_other = partner(proj_part)

    norm_low2, branch_grad, hidden_act, pre_grad, parts, grad_bup = pl.pallas_call(
        mlp_kernel,
        name="mlp",
        in_specs=[vmem()] * 7,
        out_specs=[vmem()] * 6,
        out_shape=[
            shaped((tokens, width), bf16),
            shaped((tokens, width), bf16),
            shaped((tokens, n_y * hidden), bf16),
            shaped((tokens, n_y * hidden), bf16),
            shaped((2 * tokens, width), bf16),
            shaped((1, n_y * hidden), f32),
        ],
    )(residual, upstream, proj_part, proj_other, vec, bup, feed)
    others = partner(parts)
    feed_grad = pl.pallas_call(
        mlp_weights_kernel,
        name="mlp_weights",
        in_specs=[vmem()] * 4,
        out_specs=vmem(),
        out_shape=shaped((n_y * width, 2 * hidden), bf16),
    )(norm_low2, branch_grad, hidden_act, pre_grad)
    feed_grad = lax.psum_scatter(feed_grad, everyone, scatter_dimension=0, tiled=True)

    back = call(
        functools.partial(back_kernel, images, n_context),
        "back",
        [
            shaped((tokens, width), bf16),
            shaped((tokens, width), f32),
            shaped((tokens, width), bf16),
            shaped((SMALL_ROWS, width), f32),
        ]
        + [shaped((images, half, LANES), bf16)] * blocks,
        [fold_scratch],
        place,
        residual,
        upstream,
        proj_part,
        proj_other,
        parts,
        others,
        vec,
        wout,
    )
    result, middle_grad, proj_grad, sums = back[:4]
    mix_grads = hand_over(back[4:], False)

    pack_grads = pl.pallas_call(
        attend_back_kernel,
        name="attend_back",
        grid=(images,),
        in_specs=[smem(), pos_spec, log_spec]
        + [pack_spec] * blocks
        + [fold_spec] * (2 * blocks),
        out_specs=[pack_spec] * blocks,
        out_shape=[shaped((images, pack_rows, LANES), bf16)] * blocks,
        scratch_shapes=[pltpu.VMEM((length, LANES), bf16)] * 2
        + [pltpu.VMEM((2 * HD, length), f32), pltpu.VMEM((blocks, rows, LANES), f32)],
    )(counts, key_place, log_total, *packs, *mixes, *mix_grads)
    pack_grads = hand_over(pack_grads, True)

    part_rows = n_context * piece_rows
    last_back = call(
        functools.partial(qkv_back_kernel, (n_shard, n_context, blocks)),
        "qkv_back",
        [shaped((tokens, width), bf16), shaped((n_y, 8, head_columns), f32)]
        + [shaped((part_rows // 2, columns), bf16)] * (4 * n_shard),
        [
            pltpu.VMEM((blocks, images, pack_rows, LANES), bf16),
            pltpu.VMEM((n_y, 3, tokens, head_columns), bf16),
        ],
        place,
        *pack_grads,
        wqkv,
        norm_low1,
        proj_grad,
        mixture,
    )
    norm1_part, grad_qv, quads = last_back[0], last_back[1], last_back[2:]

    def add(first, *rest):
        total = first.astype(f32)
        for value in rest:
            total = total + value.astype(f32)
        return total.astype(bf16)

    norm1_other = partner(norm1_part)
    tops, bottoms = [], []
    bottom_far = [quads[3]]
    for j in range(1, n_shard):
        x_top, x_bottom, far_top, far_bottom = quads[4 * j : 4 * j + 4]
        far_top = across(far_top)
        bottom_far.append(send(far_bottom, "shard", -j))
        bottoms.append(send(x_bottom, "shard", -j))
        tops.append(send(add(x_top, far_top), "shard", -j))
    tops.append(across(quads[2]))
    bottoms.append(across(add(*bottom_far)))
    dealt = pl.pallas_call(
        lambda place_ref, *refs: deal_kernel(
            place_ref,
            refs[0],
            refs[1],
            refs[2 : 2 + n_shard],
            refs[2 + n_shard : 2 + 2 * n_shard],
            refs[2 + 2 * n_shard : -1],
            refs[-1],
        ),
        name="deal",
        in_specs=[smem()] + [vmem()] * (2 + 2 * n_shard),
        out_specs=[vmem()] * n_context,
        out_shape=[shaped((piece_rows, columns), f32)]
        + [shaped((piece_rows, columns), bf16)] * (n_context - 1),
        scratch_shapes=[pltpu.VMEM((part_rows, columns), f32)],
    )(place, quads[0], quads[1], *tops, *bottoms)
    grad_piece = dealt[0]
    for j in range(1, n_context):
        grad_piece = grad_piece + send(dealt[j], "context", -j).astype(f32)

    input_grad, own, far = call(
        functools.partial(finish_kernel, (n_shard, n_context, last)),
        "finish",
        [shaped((tokens, width), bf16)]
        + [shaped((n_shard * n_context * SMALL_ROWS, SMALL_LANES), f32)] * 2,
        [],
        place,
        residual,
        middle_grad,
        norm1_part,
        norm1_other,
        vec,
        sums,
        grad_bup.reshape(n_y, 1, hidden),
        grad_qv,
    )
    total = (own + across(far)).reshape(n_shard, -1, SMALL_LANES)
    over_shard = total[0]
    for j in range(1, n_shard):
        over_shard = over_shard + send(total[j], "shard", -j)
    over_shard = over_shard.reshape(n_context, SMALL_ROWS, SMALL_LANES)
    small_grad = over_shard[0]
    for j in range(1, n_context):
        small_grad = small_grad + send(over_shard[j], "context", -j)

    def whole_rows(value):
        mine = lax.dynamic_slice_in_dim(value, core * (tokens // 2), tokens // 2, 0)
        near = across(mine)
        far = partner(near)
        return call(
            merge_kernel,
            "merge",
            [shaped((images, row_count, width), f32)],
            [],
            place,
            value,
            near,
            far,
        )[0]

    vec_grad = small_grad[: len(vectors), :piece_rows]
    return (
        whole_rows(result),
        whole_rows(input_grad),
        grad_piece[:, : 3 * head_columns].reshape(piece_rows, 3, head_columns),
        small_grad[: b_qv.shape[0] * b_qv.shape[1], 2 * LANES : 2 * LANES + last].reshape(
            b_qv.shape
        ),
        grad_piece[:, 3 * head_columns :].T,
        vec_grad[B_OUT],
        feed_grad[:, :hidden].astype(f32),
        small_grad[: b_up.shape[0], LANES : LANES + last],
        feed_grad[:, hidden:].astype(f32).T,
        vec_grad[B_DOWN],
        vec_grad[GAIN1],
        vec_grad[SHIFT1],
        vec_grad[GAIN2],
        vec_grad[SHIFT2],
        vec_grad[SCALE1],
        vec_grad[SCALE2],
    )


def solution(mesh):
    pair = ("y", "core")
    both = ("shard", "context")
    tokens = P("shard", "context", None)
    vector = P(both)
    in_specs = (
        tokens,
        P("shard"),
        P(both, None, pair),
        P(None, pair, both),
        P(pair, both),
        vector,
        P(both, pair),
        P(pair, both),
        P(pair, both),
    ) + (vector,) * 7
    in_specs = in_specs + (tokens,)
    out_specs = (
        tokens,
        tokens,
        P(both, None, pair),
        P(None, pair, both),
        P(pair, both),
        vector,
        P(both, pair),
        P(pair, both),
        P(pair, both),
    ) + (vector,) * 7
    sizes = tuple(mesh.shape[name] for name in ("shard", "context", "tensor"))
    split = Mesh(
        mesh.devices.reshape(sizes[0], sizes[1], sizes[2] // CORES, CORES),
        ("shard", "context", "y", "core"),
    )
    return jax.shard_map(
        functools.partial(per_device, split.devices.shape[:3]),
        mesh=split,
        in_specs=in_specs,
        out_specs=out_specs,
        check_vma=False,
    )
```

time: 643 us -> 580 us (0.902)
  matrix products: 95.8 us -> 0 us
  waiting for transfers between devices: 155 us -> 247 us
  Pallas kernels: 59.8 us -> 134 us
  other arithmetic: 72.4 us -> 9.1 us
  local copies, waits for them, and re-layouts: 84.2 us -> 21.4 us
  starting transfers between devices: 164 us -> 144 us
  between operations: 2.58 us -> 15.2 us
    ppermute x52 -> x42, waiting for transfers between devices: 75.3 us -> 179 us  [the longest x28 105 us: hand_over(): out.append(lax.ppermute(values[slot], ('context', 'y'), pairs))]
    dot_general x15 -> x0, matrix products: 95.8 us -> none  [mm(): return lax.dot_general(left, right, dims, preferred_element_type=f32)]
    pallas_call x4 -> x11, Pallas kernels: 20.3 us -> 94.8 us  [the longest x8 49.1 us: call(): pl.pallas_call(kernel, name=name, in_specs=[smem()] + [vmem()] * len(oper...]
    ppermute x56 -> x19, starting transfers between devices: 77.2 us -> 37.4 us  [send(): lax.ppermute(value, axis, [(i, (i + step) % size) for i in range(size)])]
    ppermute x52 -> x42, starting transfers between devices: 86.6 us -> 107 us  [the longest x28 98.5 us: hand_over(): out.append(lax.ppermute(values[slot], ('context', 'y'), pairs))]
    slice x28 -> x6, local copies, waits for them, and re-layouts: 19.5 us -> 0.8 us  [the longest x1 0.6 us: per_device(): small_grad[:b_qv.shape[0] * b_qv.shape[1], 2 * LANES:2 * LANES + last]]
    reduce_sum x9 -> x0, other arithmetic: 18 us -> none  [the longest x1 5.19 us: per_device(): grad_scale2 = jnp.sum(upstream * mlp_branch, axis=0)]
    reshape x19 -> x1, local copies, waits for them, and re-layouts: 15.3 us -> 0.15 us  [per_device(): piece = jnp.concatenate([w_qkv.reshape(piece_rows, -1), w_out.T], axis=1)]
  transfers between devices with their start and end apart: 108 -> 63, of which waited for: 29 -> 29; matrix products, arithmetic and copies ran while one was open for 35% -> 2% of each run, Pallas kernels for 9% -> 16%
where the time goes in v2:
time: 580 us; the launch traced here: 571 us
  waiting for transfers between devices  247 us (43%)
  starting transfers between devices  144 us (25%)
  Pallas kernels  134 us (23%)
  local copies, waits for them, and re-layouts  21.4 us (4%)
  between operations  15.2 us (3%)
  other arithmetic  9.1 us (2%)
    ppermute x28, waiting for transfers between devices, hand_over(): out.append(lax.ppermute(values[slot], ('context', 'y'), pairs))  105 us
    ppermute x28, starting transfers between devices, hand_over(): out.append(lax.ppermute(values[slot], ('context', 'y'), pairs))  98.5 us
    ppermute x9, waiting for transfers between devices, across(): return lax.ppermute(value, 'y', [(0, 1), (1, 0)])  69.4 us
    ppermute x19, waiting for transfers between devices, send(): lax.ppermute(value, axis, [(i, (i + step) % size) for i in range(size)])  67.3 us
    pallas_call x8, Pallas kernels, call(): pl.pallas_call(kernel, name=name, in_specs=[smem()] + [vmem()] * len(oper...  49.1 us
    ppermute x19, starting transfers between devices, send(): lax.ppermute(value, axis, [(i, (i + step) % size) for i in range(size)])  37.4 us
    pallas_call x1, Pallas kernels, per_device(): pl.pallas_call(mlp_weights_kernel, name='mlp_weights', in_specs=[vmem()]...  23.9 us
    pallas_call x1, Pallas kernels, per_device(): pl.pallas_call(attend_back_kernel, name='attend_back', grid=(images,), in...  23.1 us
  transfers between devices with their start and end apart: 63, of which 29 were waited for; matrix products, arithmetic and copies ran while one was open for 2% of the time, Pallas kernels for 16%

profile of v2, /device:TPU:0, one launch (start us, length us, event | category | flops | bytes accessed | tf_op | source)
XLA Modules:
  0.0 570.9 jit_solution(13749625449041502497)
XLA Ops:
  8.5 1.8 pad_maximum_fusion
  10.9 5.1 collective-permute-start.2
  17.3 2.9 collective-permute-start.5
  21.3 18.1 %collective-permute-done.5.refs_7_ = bf16[16,384]{1,0:T(8,128)(2,1)S(1)} collective-permute-done((bf16[16,384]{1,0:T(8,128)(2,1)S(1)}, bf16[16,384]{1,0:T(8,128)(2,1)S(1)}, u32[]{:S(2)}, u32[]{:S(2)}) %collective-permute-start.5) | collective-permute-done | bytes 12320 | tf_op jit(solution)/shard_map/ppermute | solution.py:599
  39.4 11.6 %collective-permute-start.3 = (bf16[16,384]{1,0:T(8,128)(2,1)S(1)}, bf16[16,384]{1,0:T(8,128)(2,1)S(1)}, u32[]{:S(2)}, u32[]{:S(2)}) collective-permute-start(bf16[16,384]{1,0:T(8,128)(2,1)S(1)} %fusion.7.refs_4_), channel_id=1, source_target_pairs={{0,4},{4,8},{8,12},{12,0},{1,5},{5,9},{9,13},{13,1},{2,6},{6,10},{... | collective-permute-start | bytes 36872 | tf_op jit(solution)/shard_map/ppermute | solution.py:599
  54.0 2.3 stack.57
  60.4 25.0 %collective-permute-done.8.refs_4_ = bf16[288,1024]{1,0:T(8,128)(2,1)S(1)} collective-permute-done((bf16[288,1024]{1,0:T(8,128)(2,1)}, bf16[288,1024]{1,0:T(8,128)(2,1)S(1)}, u32[]{:S(2)}, u32[]{:S(2)}) %collective-permute-start.8) | collective-permute-done | bytes 589856 | tf_op jit(solution)/shard_map/ppermute | solution.py:599
  89.5 2.4 collective-permute-done.6.refs_2_
  91.9 6.9 %collective-permute-done.9.refs_5_ = bf16[288,1024]{1,0:T(8,128)(2,1)} collective-permute-done((bf16[288,1024]{1,0:T(8,128)(2,1)}, bf16[288,1024]{1,0:T(8,128)(2,1)}, u32[]{:S(2)}, u32[]{:S(2)}) %collective-permute-start.9) | collective-permute-done | bytes 589856 | tf_op jit(solution)/shard_map/ppermute | solution.py:599
  98.8 3.1 collective-permute-done.10.refs_6_
  102.0 13.1 %collective-permute-done.11.refs_7_ = bf16[288,1024]{1,0:T(8,128)(2,1)} collective-permute-done((bf16[288,1024]{1,0:T(8,128)(2,1)S(1)}, bf16[288,1024]{1,0:T(8,128)(2,1)}, u32[]{:S(2)}, u32[]{:S(2)}) %collective-permute-start.11) | collective-permute-done | bytes 589856 | tf_op jit(solution)/shard_map/ppermute | solution.py:599
  115.0 8.2 %qkv.1 = (bf16[3,288,128]{2,1,0:T(8,128)(2,1)}, bf16[3,288,128]{2,1,0:T(8,128)(2,1)}, bf16[3,288,128]{2,1,0:T(8,128)(2,1)}, bf16[3,288,128]{2,1,0:T(8,128)(2,1)}...) custom-call(s32[4]{0:T(128)} %pad_add_fusion.place_ref, ...), custom_call_target="tpu_custom_call" | custom-call | tf_op jit(solution)/shard_map/qkv/pallas_call | solution.py:550
  123.2 2.7 collective-permute-start.12
  125.9 1.8 collective-permute-start.13
  127.7 2.5 collective-permute-start.14
  131.7 6.6 %collective-permute-done.12.refs_1_ = bf16[3,288,128]{2,1,0:T(8,128)(2,1)S(1)} collective-permute-done((bf16[3,288,128]{2,1,0:T(8,128)(2,1)}, bf16[3,288,128]{2,1,0:T(8,128)(2,1)S(1)}, u32[]{:S(2)}, u32[]{:S(2)}) %collective-permute-start.12) | collective-permute-done | bytes 221216 | tf_op jit(solution)/shard_map/ppermute | solution.py:617
  138.3 15.9 %collective-permute-start.17 = (bf16[3,288,128]{2,1,0:T(8,128)(2,1)}, bf16[3,288,128]{2,1,0:T(8,128)(2,1)S(1)}, u32[]{:S(2)}, u32[]{:S(2)}) collective-permute-start(bf16[3,288,128]{2,1,0:T(8,128)(2,1)} %get-tuple-element.93), channel_id=1, source_target_pairs={{0,10},{2,8},{4,14},{6,12},{8,2},{10,0},{12,6},{14,4},{1,11},{3,9}... | collective-permute-start | bytes 663560 | tf_op jit(solution)/shard_map/ppermute | solution.py:617
  154.2 23.0 %collective-permute-start.18 = (bf16[3,288,128]{2,1,0:T(8,128)(2,1)}, bf16[3,288,128]{2,1,0:T(8,128)(2,1)S(1)}, u32[]{:S(2)}, u32[]{:S(2)}) collective-permute-start(bf16[3,288,128]{2,1,0:T(8,128)(2,1)} %get-tuple-element.94), channel_id=1, source_target_pairs={{0,14},{2,12},{4,2},{6,0},{8,6},{10,4},{12,10},{14,8},{1,15},{3,13... | collective-permute-start | bytes 663560 | tf_op jit(solution)/shard_map/ppermute | solution.py:617
  178.0 7.2 %collective-permute-done.17.refs_6_ = bf16[3,288,128]{2,1,0:T(8,128)(2,1)S(1)} collective-permute-done((bf16[3,288,128]{2,1,0:T(8,128)(2,1)}, bf16[3,288,128]{2,1,0:T(8,128)(2,1)S(1)}, u32[]{:S(2)}, u32[]{:S(2)}) %collective-permute-start.17) | collective-permute-done | bytes 221216 | tf_op jit(solution)/shard_map/ppermute | solution.py:617
  186.1 16.5 %attend.1 = (bf16[3,96,128]{2,1,0:T(8,128)(2,1)}, bf16[3,96,128]{2,1,0:T(8,128)(2,1)}, bf16[3,96,128]{2,1,0:T(8,128)(2,1)}, bf16[3,96,128]{2,1,0:T(8,128)(2,1)},...) custom-call(s32[3]{0:T(128)} %count_ref.3, ...), custom_call_target="tpu_custom_call" | custom-call | tf_op jit(solution)/shard_map/attend/pallas_call | solution.py:694
  202.6 5.7 collective-permute-start.19
  210.3 3.7 collective-permute-start.23
  215.5 1.6 collective-permute-done.20.refs_2_
  217.4 3.7 collective-permute-done.24.refs_6_
  221.1 3.5 collective-permute-done.25.refs_7_
  225.3 3.5 project.1
  228.7 2.4 constant_dynamic-slice_fusion.2
  232.9 18.3 %mlp.1 = (bf16[576,1024]{1,0:T(8,128)(2,1)}, bf16[576,1024]{1,0:T(8,128)(2,1)}, bf16[576,2048]{1,0:T(8,128)(2,1)}, bf16[576,2048]{1,0:T(8,128)(2,1)}, bf16[1152,1024]{1,0:T(8,128)(2,1)}, /*index=5*/f32[1,2048]{1,0:T(1,128)}) custom-call(bf16[576,1024]{1,0:T(8,128)(2,1)} %bitcast.42, bf16[576,1024]{1,0:T(8,128)(2,1)} %bitcast.45, ...), custom_call_target="tpu_custom_call" | custom-call | tf_op jit(solution)/shard_map/mlp/pallas_call | solution.py:719
  251.2 23.9 %mlp_weights.1 = bf16[2048,2048]{1,0:T(8,128)(2,1)} custom-call(bf16[576,1024]{1,0:T(8,128)(2,1)} %get-tuple-element.150.norm_ref, bf16[576,1024]{1,0:T(8,128)(2,1)} %get-tuple-element.151.grad_ref, bf16[576,2048]{1,0:T(8,128)(2,1)} %get-tuple-element.152.act_ref, bf16[576,2048]{1,0:T(8,128)(2,1)} %get-tuple-element.153.pre_ref), custom_call_target="tpu_custom_call" | custom-call | tf_op jit(solution)/shard_map/mlp_weights/pallas_call | solution.py:734
  275.1 1.6 copy-done.5
  276.9 4.5 collective-permute-done.27.others_ref
  281.4 10.1 %back.1 = (bf16[576,1024]{1,0:T(8,128)(2,1)}, f32[576,1024]{1,0:T(8,128)}, bf16[576,1024]{1,0:T(8,128)(2,1)}, f32[16,1024]{1,0:T(8,128)}, bf16[3,96,128]{2,1,0:T...) custom-call(s32[4]{0:T(128)} %pad_add_fusion.place_ref, ...), custom_call_target="tpu_custom_call" | custom-call | tf_op jit(solution)/shard_map/back/pallas_call | solution.py:550
  291.8 3.6 collective-permute-start.32
  295.7 1.7 collective-permute-start.34
  297.4 2.9 collective-permute-done.30.refs_17_
  300.5 4.8 collective-permute-done.31.refs_18_
  305.3 4.1 collective-permute-start.36
  309.5 8.3 %collective-permute-done.35.refs_22_ = bf16[3,96,128]{2,1,0:T(8,128)(2,1)S(1)} collective-permute-done((bf16[3,96,128]{2,1,0:T(8,128)(2,1)}, bf16[3,96,128]{2,1,0:T(8,128)(2,1)S(1)}, u32[]{:S(2)}, u32[]{:S(2)}) %collective-permute-start.35) | collective-permute-done | bytes 73760 | tf_op jit(solution)/shard_map/ppermute | solution.py:617
  318.5 23.1 %attend_back.1 = (bf16[3,288,128]{2,1,0:T(8,128)(2,1)}, bf16[3,288,128]{2,1,0:T(8,128)(2,1)}, bf16[3,288,128]{2,1,0:T(8,128)(2,1)}, bf16[3,288,128]{2,1,0:T(8,12...) custom-call(s32[3]{0:T(128)} %count_ref.3, ...), custom_call_target="tpu_custom_call" | custom-call | tf_op jit(solution)/shard_map/attend_back/pallas_call | solution.py:767
  341.6 6.7 %collective-permute-start.37 = (bf16[3,288,128]{2,1,0:T(8,128)(2,1)}, bf16[3,288,128]{2,1,0:T(8,128)(2,1)S(1)}, u32[]{:S(2)}, u32[]{:S(2)}) collective-permute-start(bf16[3,288,128]{2,1,0:T(8,128)(2,1)} %get-tuple-element.120), channel_id=1, source_target_pairs={{0,12},{2,14},{4,0},{6,2},{8,4},{10,6},{12,8},{14,10},{1,13},{3,15... | collective-permute-start | bytes 663560 | tf_op jit(solution)/shard_map/ppermute | solution.py:617
  349.7 2.3 collective-permute-start.40
  352.0 3.3 collective-permute-start.41
  355.2 6.3 %collective-permute-done.37.refs_1_ = bf16[3,288,128]{2,1,0:T(8,128)(2,1)S(1)} collective-permute-done((bf16[3,288,128]{2,1,0:T(8,128)(2,1)}, bf16[3,288,128]{2,1,0:T(8,128)(2,1)S(1)}, u32[]{:S(2)}, u32[]{:S(2)}) %collective-permute-start.37) | collective-permute-done | bytes 221216 | tf_op jit(solution)/shard_map/ppermute | solution.py:617
  361.5 14.0 %collective-permute-start.42 = (bf16[3,288,128]{2,1,0:T(8,128)(2,1)}, bf16[3,288,128]{2,1,0:T(8,128)(2,1)S(1)}, u32[]{:S(2)}, u32[]{:S(2)}) collective-permute-start(bf16[3,288,128]{2,1,0:T(8,128)(2,1)} %get-tuple-element.125), channel_id=1, source_target_pairs={{0,10},{2,8},{4,14},{6,12},{8,2},{10,0},{12,6},{14,4},{1,11},{3,9}... | collective-permute-start | bytes 663560 | tf_op jit(solution)/shard_map/ppermute | solution.py:617
  375.5 18.8 %collective-permute-done.38.refs_2_ = bf16[3,288,128]{2,1,0:T(8,128)(2,1)S(1)} collective-permute-done((bf16[3,288,128]{2,1,0:T(8,128)(2,1)}, bf16[3,288,128]{2,1,0:T(8,128)(2,1)S(1)}, u32[]{:S(2)}, u32[]{:S(2)}) %collective-permute-start.38) | collective-permute-done | bytes 221216 | tf_op jit(solution)/shard_map/ppermute | solution.py:617
  394.6 40.6 %collective-permute-done.42.refs_6_ = bf16[3,288,128]{2,1,0:T(8,128)(2,1)S(1)} collective-permute-done((bf16[3,288,128]{2,1,0:T(8,128)(2,1)}, bf16[3,288,128]{2,1,0:T(8,128)(2,1)S(1)}, u32[]{:S(2)}, u32[]{:S(2)}) %collective-permute-start.42) | collective-permute-done | bytes 221216 | tf_op jit(solution)/shard_map/ppermute | solution.py:617
  436.0 10.4 %qkv_back.1 = (bf16[576,1024]{1,0:T(8,128)(2,1)}, f32[2,8,256]{2,1,0:T(8,128)}, bf16[256,1024]{1,0:T(8,128)(2,1)}, bf16[256,1024]{1,0:T(8,128)(2,1)}, bf16[256,1...) custom-call(s32[4]{0:T(128)} %pad_add_fusion.place_ref, ...), custom_call_target="tpu_custom_call" | custom-call | tf_op jit(solution)/shard_map/qkv_back/pallas_call | solution.py:550
  446.7 1.6 collective-permute-start.51
  448.4 2.0 collective-permute-start.28
  450.5 21.9 %collective-permute-done.47 = bf16[256,1024]{1,0:T(8,128)(2,1)} collective-permute-done((bf16[256,1024]{1,0:T(8,128)(2,1)}, bf16[256,1024]{1,0:T(8,128)(2,1)}, u32[]{:S(2)}, u32[]{:S(2)}) %collective-permute-start.47) | collective-permute-done | bytes 524320 | tf_op jit(solution)/shard_map/ppermute | solution.py:602
  473.7 2.1 collective-permute-start.48
  477.0 19.9 %collective-permute-done.28.near_ref = bf16[288,1024]{1,0:T(8,128)(2,1)S(1)} collective-permute-done((bf16[288,1024]{1,0:T(8,128)(2,1)S(1)}, bf16[288,1024]{1,0:T(8,128)(2,1)S(1)}, u32[]{:S(2)}, u32[]{:S(2)}) %collective-permute-start.28) | collective-permute-done | bytes 589856 | tf_op jit(solution)/shard_map/ppermute | solution.py:602
  496.9 11.2 %collective-permute-done.49.refs_3_ = bf16[256,1024]{1,0:T(8,128)(2,1)S(1)} collective-permute-done((bf16[256,1024]{1,0:T(8,128)(2,1)}, bf16[256,1024]{1,0:T(8,128)(2,1)S(1)}, u32[]{:S(2)}, u32[]{:S(2)}) %collective-permute-start.49) | collective-permute-done | bytes 524320 | tf_op jit(solution)/shard_map/ppermute | solution.py:602
  508.2 9.7 %collective-permute-done.52.refs_5_ = bf16[256,1024]{1,0:T(8,128)(2,1)S(1)} collective-permute-done((bf16[256,1024]{1,0:T(8,128)(2,1)S(1)}, bf16[256,1024]{1,0:T(8,128)(2,1)S(1)}, u32[]{:S(2)}, u32[]{:S(2)}) %collective-permute-start.52) | collective-permute-done | bytes 524320 | tf_op jit(solution)/shard_map/ppermute | solution.py:602
  518.7 3.5 deal.1
  522.3 1.9 collective-permute-start.55
  525.2 6.2 %finish.1 = (bf16[576,1024]{1,0:T(8,128)(2,1)}, f32[128,384]{1,0:T(8,128)}, f32[128,384]{1,0:T(8,128)}) custom-call(s32[4]{0:T(128)} %pad_add_fusion.place_ref, bf16[576,1024]{1,0:T(8,128)(2,1)} %bitcast.44, f32[576,1024]{1,0:T(8,128)} %get-tuple-element.109.middle_grad_ref, bf16[576,1024]{1,0:T(8,128)(2,1)} %get-tuple-element.131.part_ref, ...), custom_call_target="tpu_custom_call" | custom-call | tf_op jit(solution)/shard_map/finish/pallas_call | solution.py:550
  533.7 4.1 merge.2
  539.9 1.8 collective-permute-done.54
  542.9 1.5 collective-permute-done.57
  544.5 2.4 collective-permute-start.58
  547.0 3.9 collective-permute-start.59
  556.5 4.3 merge.3
  560.7 1.9 convert_bitcast_fusion
  (253 shorter events, 45.7 us)
Async XLA Ops:
  7.2 81.2 %copy-start = (bf16[3,384,1024]{2,1,0:T(8,128)(2,1)S(1)}, bf16[3,384,1024]{2,1,0:T(8,128)(2,1)}, u32[]{:S(2)}) copy-start(bf16[3,384,1024]{2,1,0:T(8,128)(2,1)} %param.17) | copy-start | bytes 7077892
  7.2 224.6 %all-gather.2.cloned.1.call-start = ((), (), s32[]{:S(2)}) async-start(), calls=%async_computation.1 | async-start | bytes 8912896 | tf_op jit(solution)/shard_map/all_gather | solution.py:620
  10.4 550.3 %reduce-scatter.2.cloned.1.call-start = ((), (), s32[]{:S(2)}) async-start(), calls=%async_computation.2 | async-start | bytes 8912896 | tf_op jit(solution)/shard_map/reduce_scatter | solution.py:741
  10.9 41.5 %collective-permute-start.2 = (bf16[128,1024]{1,0:T(8,128)(2,1)S(1)}, bf16[128,1024]{1,0:T(8,128)(2,1)S(1)}, u32[]{:S(2)}, u32[]{:S(2)}) collective-permute-start(bf16[128,1024]{1,0:T(8,128)(2,1)S(1)} %pad_maximum_fusion.1.refs_0_), channel_id=1, source_target_pairs={{0,12},{4,0},{8,4},{12,8},{1,13},{5,1},{9,5},{13,9},{2,14},{6,2},{... | collective-permute-start | bytes 786440 | tf_op jit(solution)/shard_map/ppermute | solution.py:599
  16.1 36.4 %collective-permute-start.1 = (bf16[128,1024]{1,0:T(8,128)(2,1)S(1)}, bf16[128,1024]{1,0:T(8,128)(2,1)S(1)}, u32[]{:S(2)}, u32[]{:S(2)}) collective-permute-start(bf16[128,1024]{1,0:T(8,128)(2,1)S(1)} %pad_maximum_fusion.1.refs_0_), channel_id=1, source_target_pairs={{0,8},{4,12},{8,0},{12,4},{1,9},{5,13},{9,1},{13,5},{2,10},{6,14},... | collective-permute-start | bytes 786440 | tf_op jit(solution)/shard_map/ppermute | solution.py:599
  16.1 36.4 %collective-permute-start = (bf16[128,1024]{1,0:T(8,128)(2,1)S(1)}, bf16[128,1024]{1,0:T(8,128)(2,1)S(1)}, u32[]{:S(2)}, u32[]{:S(2)}) collective-permute-start(bf16[128,1024]{1,0:T(8,128)(2,1)S(1)} %pad_maximum_fusion.1.refs_0_), channel_id=1, source_target_pairs={{0,4},{4,8},{8,12},{12,0},{1,5},{5,9},{9,13},{13,1},{2,6},{6,10},{... | collective-permute-start | bytes 786440 | tf_op jit(solution)/shard_map/ppermute | solution.py:599
  17.3 22.1 %collective-permute-start.5 = (bf16[16,384]{1,0:T(8,128)(2,1)S(1)}, bf16[16,384]{1,0:T(8,128)(2,1)S(1)}, u32[]{:S(2)}, u32[]{:S(2)}) collective-permute-start(bf16[16,384]{1,0:T(8,128)(2,1)S(1)} %fusion.7.refs_4_), channel_id=1, source_target_pairs={{0,12},{4,0},{8,4},{12,8},{1,13},{5,1},{9,5},{13,9},{2,14},{6,2},{... | collective-permute-start | bytes 36872 | tf_op jit(solution)/shard_map/ppermute | solution.py:599
  20.2 31.5 %collective-permute-start.4 = (bf16[16,384]{1,0:T(8,128)(2,1)S(1)}, bf16[16,384]{1,0:T(8,128)(2,1)S(1)}, u32[]{:S(2)}, u32[]{:S(2)}) collective-permute-start(bf16[16,384]{1,0:T(8,128)(2,1)S(1)} %fusion.7.refs_4_), channel_id=1, source_target_pairs={{0,8},{4,12},{8,0},{12,4},{1,9},{5,13},{9,1},{13,5},{2,10},{6,14},... | collective-permute-start | bytes 36872 | tf_op jit(solution)/shard_map/ppermute | solution.py:599
  39.4 13.0 %collective-permute-start.3 = (bf16[16,384]{1,0:T(8,128)(2,1)S(1)}, bf16[16,384]{1,0:T(8,128)(2,1)S(1)}, u32[]{:S(2)}, u32[]{:S(2)}) collective-permute-start(bf16[16,384]{1,0:T(8,128)(2,1)S(1)} %fusion.7.refs_4_), channel_id=1, source_target_pairs={{0,4},{4,8},{8,12},{12,0},{1,5},{5,9},{9,13},{13,1},{2,6},{6,10},{... | collective-permute-start | bytes 36872 | tf_op jit(solution)/shard_map/ppermute | solution.py:599
  56.3 29.0 %collective-permute-start.8 = (bf16[288,1024]{1,0:T(8,128)(2,1)}, bf16[288,1024]{1,0:T(8,128)(2,1)S(1)}, u32[]{:S(2)}, u32[]{:S(2)}) collective-permute-start(bf16[288,1024]{1,0:T(8,128)(2,1)} %get-tuple-element.85.refs_0_), channel_id=1, source_target_pairs={{0,16},{16,0},{1,17},{17,1},{2,18},{18,2},{3,19},{19,3},{4,20},{20... | collective-permute-start | bytes 1769480 | tf_op jit(solution)/shard_map/ppermute | solution.py:599
  57.8 29.1 %collective-permute-start.7 = (bf16[288,1024]{1,0:T(8,128)(2,1)}, bf16[288,1024]{1,0:T(8,128)(2,1)S(1)}, u32[]{:S(2)}, u32[]{:S(2)}) collective-permute-start(bf16[288,1024]{1,0:T(8,128)(2,1)} %get-tuple-element.86.refs_1_), channel_id=1, source_target_pairs={{0,2},{2,0},{1,3},{3,1},{4,6},{6,4},{5,7},{7,5},{8,10},{10,8},{9,1... | collective-permute-start | bytes 1769480 | tf_op jit(solution)/shard_map/ppermute | solution.py:602
  59.3 32.6 %collective-permute-start.6 = (bf16[288,1024]{1,0:T(8,128)(2,1)}, bf16[288,1024]{1,0:T(8,128)(2,1)}, u32[]{:S(2)}, u32[]{:S(2)}) collective-permute-start(bf16[288,1024]{1,0:T(8,128)(2,1)} %get-tuple-element.85.refs_0_), channel_id=1, source_target_pairs={{0,2},{2,0},{1,3},{3,1},{4,6},{6,4},{5,7},{7,5},{8,10},{10,8},{9,1... | collective-permute-start | bytes 1769480 | tf_op jit(solution)/shard_map/ppermute | solution.py:602
  59.8 39.0 %collective-permute-start.9 = (bf16[288,1024]{1,0:T(8,128)(2,1)}, bf16[288,1024]{1,0:T(8,128)(2,1)}, u32[]{:S(2)}, u32[]{:S(2)}) collective-permute-start(bf16[288,1024]{1,0:T(8,128)(2,1)} %get-tuple-element.86.refs_1_), channel_id=1, source_target_pairs={{0,16},{16,0},{1,17},{17,1},{2,18},{18,2},{3,19},{19,3},{4,20},{20... | collective-permute-start | bytes 1769480 | tf_op jit(solution)/shard_map/ppermute | solution.py:599
  85.4 16.6 %collective-permute-start.10 = (bf16[288,1024]{1,0:T(8,128)(2,1)S(1)}, bf16[288,1024]{1,0:T(8,128)(2,1)}, u32[]{:S(2)}, u32[]{:S(2)}) collective-permute-start(bf16[288,1024]{1,0:T(8,128)(2,1)S(1)} %collective-permute-done.8.refs_4_), channel_id=1, source_target_pairs={{0,2},{2,0},{1,3},{3,1},{4,6},{6,4},{5,7},{7,5},{8,10},{10,8},{9,1... | collective-permute-start | bytes 1769480 | tf_op jit(solution)/shard_map/ppermute | solution.py:602
  86.9 28.1 %collective-permute-start.11 = (bf16[288,1024]{1,0:T(8,128)(2,1)S(1)}, bf16[288,1024]{1,0:T(8,128)(2,1)}, u32[]{:S(2)}, u32[]{:S(2)}) collective-permute-start(bf16[288,1024]{1,0:T(8,128)(2,1)S(1)} %collective-permute-done.7.refs_3_), channel_id=1, source_target_pairs={{0,16},{16,0},{1,17},{17,1},{2,18},{18,2},{3,19},{19,3},{4,20},{20... | collective-permute-start | bytes 1769480 | tf_op jit(solution)/shard_map/ppermute | solution.py:599
  123.2 15.1 %collective-permute-start.12 = (bf16[3,288,128]{2,1,0:T(8,128)(2,1)}, bf16[3,288,128]{2,1,0:T(8,128)(2,1)S(1)}, u32[]{:S(2)}, u32[]{:S(2)}) collective-permute-start(bf16[3,288,128]{2,1,0:T(8,128)(2,1)} %get-tuple-element.88), channel_id=1, source_target_pairs={{0,4},{2,6},{4,8},{6,10},{8,12},{10,14},{12,0},{14,2},{1,5},{3,7},... | collective-permute-start | bytes 663560 | tf_op jit(solution)/shard_map/ppermute | solution.py:617
  125.9 28.3 %collective-permute-start.13 = (bf16[3,288,128]{2,1,0:T(8,128)(2,1)}, bf16[3,288,128]{2,1,0:T(8,128)(2,1)S(1)}, u32[]{:S(2)}, u32[]{:S(2)}) collective-permute-start(bf16[3,288,128]{2,1,0:T(8,128)(2,1)} %get-tuple-element.89), channel_id=1, source_target_pairs={{0,8},{2,10},{4,12},{6,14},{8,0},{10,2},{12,4},{14,6},{1,9},{3,11}... | collective-permute-start | bytes 663560 | tf_op jit(solution)/shard_map/ppermute | solution.py:617
  127.7 50.3 %collective-permute-start.14 = (bf16[3,288,128]{2,1,0:T(8,128)(2,1)}, bf16[3,288,128]{2,1,0:T(8,128)(2,1)S(1)}, u32[]{:S(2)}, u32[]{:S(2)}) collective-permute-start(bf16[3,288,128]{2,1,0:T(8,128)(2,1)} %get-tuple-element.90), channel_id=1, source_target_pairs={{0,12},{2,14},{4,0},{6,2},{8,4},{10,6},{12,8},{14,10},{1,13},{3,15... | collective-permute-start | bytes 663560 | tf_op jit(solution)/shard_map/ppermute | solution.py:617
  130.2 47.8 %collective-permute-start.15 = (bf16[3,288,128]{2,1,0:T(8,128)(2,1)}, bf16[3,288,128]{2,1,0:T(8,128)(2,1)S(1)}, u32[]{:S(2)}, u32[]{:S(2)}) collective-permute-start(bf16[3,288,128]{2,1,0:T(8,128)(2,1)} %get-tuple-element.91), channel_id=1, source_target_pairs={{0,2},{2,0},{4,6},{6,4},{8,10},{10,8},{12,14},{14,12},{1,3},{3,1},... | collective-permute-start | bytes 663560 | tf_op jit(solution)/shard_map/ppermute | solution.py:617
  131.7 46.3 %collective-permute-start.16 = (bf16[3,288,128]{2,1,0:T(8,128)(2,1)}, bf16[3,288,128]{2,1,0:T(8,128)(2,1)S(1)}, u32[]{:S(2)}, u32[]{:S(2)}) collective-permute-start(bf16[3,288,128]{2,1,0:T(8,128)(2,1)} %get-tuple-element.92), channel_id=1, source_target_pairs={{0,6},{2,4},{4,10},{6,8},{8,14},{10,12},{12,2},{14,0},{1,7},{3,5},... | collective-permute-start | bytes 663560 | tf_op jit(solution)/shard_map/ppermute | solution.py:617
  138.3 46.8 %collective-permute-start.17 = (bf16[3,288,128]{2,1,0:T(8,128)(2,1)}, bf16[3,288,128]{2,1,0:T(8,128)(2,1)S(1)}, u32[]{:S(2)}, u32[]{:S(2)}) collective-permute-start(bf16[3,288,128]{2,1,0:T(8,128)(2,1)} %get-tuple-element.93), channel_id=1, source_target_pairs={{0,10},{2,8},{4,14},{6,12},{8,2},{10,0},{12,6},{14,4},{1,11},{3,9}... | collective-permute-start | bytes 663560 | tf_op jit(solution)/shard_map/ppermute | solution.py:617
  154.2 31.2 %collective-permute-start.18 = (bf16[3,288,128]{2,1,0:T(8,128)(2,1)}, bf16[3,288,128]{2,1,0:T(8,128)(2,1)S(1)}, u32[]{:S(2)}, u32[]{:S(2)}) collective-permute-start(bf16[3,288,128]{2,1,0:T(8,128)(2,1)} %get-tuple-element.94), channel_id=1, source_target_pairs={{0,14},{2,12},{4,2},{6,0},{8,6},{10,4},{12,10},{14,8},{1,15},{3,13... | collective-permute-start | bytes 663560 | tf_op jit(solution)/shard_map/ppermute | solution.py:617
  202.6 11.4 %collective-permute-start.19 = (bf16[3,96,128]{2,1,0:T(8,128)(2,1)}, bf16[3,96,128]{2,1,0:T(8,128)(2,1)S(1)}, u32[]{:S(2)}, u32[]{:S(2)}) collective-permute-start(bf16[3,96,128]{2,1,0:T(8,128)(2,1)} %get-tuple-element.96.refs_9_), channel_id=1, source_target_pairs={{0,12},{2,14},{4,0},{6,2},{8,4},{10,6},{12,8},{14,10},{1,13},{3,15... | collective-permute-start | bytes 221192 | tf_op jit(solution)/shard_map/ppermute | solution.py:617
  208.3 8.8 %collective-permute-start.20 = (bf16[3,96,128]{2,1,0:T(8,128)(2,1)}, bf16[3,96,128]{2,1,0:T(8,128)(2,1)S(1)}, u32[]{:S(2)}, u32[]{:S(2)}) collective-permute-start(bf16[3,96,128]{2,1,0:T(8,128)(2,1)} %get-tuple-element.97.refs_10_), channel_id=1, source_target_pairs={{0,8},{2,10},{4,12},{6,14},{8,0},{10,2},{12,4},{14,6},{1,9},{3,11}... | collective-permute-start | bytes 221192 | tf_op jit(solution)/shard_map/ppermute | solution.py:617
  208.7 8.7 %collective-permute-start.21 = (bf16[3,96,128]{2,1,0:T(8,128)(2,1)}, bf16[3,96,128]{2,1,0:T(8,128)(2,1)S(1)}, u32[]{:S(2)}, u32[]{:S(2)}) collective-permute-start(bf16[3,96,128]{2,1,0:T(8,128)(2,1)} %get-tuple-element.98.refs_11_), channel_id=1, source_target_pairs={{0,4},{2,6},{4,8},{6,10},{8,12},{10,14},{12,0},{14,2},{1,5},{3,7},... | collective-permute-start | bytes 221192 | tf_op jit(solution)/shard_map/ppermute | solution.py:617
  209.0 8.4 %collective-permute-start.22 = (bf16[3,96,128]{2,1,0:T(8,128)(2,1)}, bf16[3,96,128]{2,1,0:T(8,128)(2,1)S(1)}, u32[]{:S(2)}, u32[]{:S(2)}) collective-permute-start(bf16[3,96,128]{2,1,0:T(8,128)(2,1)} %get-tuple-element.99.refs_12_), channel_id=1, source_target_pairs={{0,2},{2,0},{4,6},{6,4},{8,10},{10,8},{12,14},{14,12},{1,3},{3,1},... | collective-permute-start | bytes 221192 | tf_op jit(solution)/shard_map/ppermute | solution.py:617
  210.3 7.1 %collective-permute-start.23 = (bf16[3,96,128]{2,1,0:T(8,128)(2,1)}, bf16[3,96,128]{2,1,0:T(8,128)(2,1)S(1)}, u32[]{:S(2)}, u32[]{:S(2)}) collective-permute-start(bf16[3,96,128]{2,1,0:T(8,128)(2,1)} %get-tuple-element.100.refs_13_), channel_id=1, source_target_pairs={{0,14},{2,12},{4,2},{6,0},{8,6},{10,4},{12,10},{14,8},{1,15},{3,13... | collective-permute-start | bytes 221192 | tf_op jit(solution)/shard_map/ppermute | solution.py:617
  214.0 7.1 %collective-permute-start.24 = (bf16[3,96,128]{2,1,0:T(8,128)(2,1)}, bf16[3,96,128]{2,1,0:T(8,128)(2,1)S(1)}, u32[]{:S(2)}, u32[]{:S(2)}) collective-permute-start(bf16[3,96,128]{2,1,0:T(8,128)(2,1)} %get-tuple-element.101.refs_14_), channel_id=1, source_target_pairs={{0,10},{2,8},{4,14},{6,12},{8,2},{10,0},{12,6},{14,4},{1,11},{3,9}... | collective-permute-start | bytes 221192 | tf_op jit(solution)/shard_map/ppermute | solution.py:617
  217.1 7.5 %collective-permute-start.25 = (bf16[3,96,128]{2,1,0:T(8,128)(2,1)}, bf16[3,96,128]{2,1,0:T(8,128)(2,1)S(1)}, u32[]{:S(2)}, u32[]{:S(2)}) collective-permute-start(bf16[3,96,128]{2,1,0:T(8,128)(2,1)} %get-tuple-element.102.refs_15_), channel_id=1, source_target_pairs={{0,6},{2,4},{4,10},{6,8},{8,14},{10,12},{12,2},{14,0},{1,7},{3,5},... | collective-permute-start | bytes 221192 | tf_op jit(solution)/shard_map/ppermute | solution.py:617
  228.7 3.1 collective-permute-start.26
  276.7 4.7 collective-permute-start.27
  291.5 8.8 %collective-permute-start.30 = (bf16[3,96,128]{2,1,0:T(8,128)(2,1)}, bf16[3,96,128]{2,1,0:T(8,128)(2,1)S(1)}, u32[]{:S(2)}, u32[]{:S(2)}) collective-permute-start(bf16[3,96,128]{2,1,0:T(8,128)(2,1)} %get-tuple-element.112), channel_id=1, source_target_pairs={{0,4},{2,6},{4,8},{6,10},{8,12},{10,14},{12,0},{14,2},{1,5},{3,7},... | collective-permute-start | bytes 221192 | tf_op jit(solution)/shard_map/ppermute | solution.py:617
  291.5 13.7 %collective-permute-start.31 = (bf16[3,96,128]{2,1,0:T(8,128)(2,1)}, bf16[3,96,128]{2,1,0:T(8,128)(2,1)S(1)}, u32[]{:S(2)}, u32[]{:S(2)}) collective-permute-start(bf16[3,96,128]{2,1,0:T(8,128)(2,1)} %get-tuple-element.113), channel_id=1, source_target_pairs={{0,8},{2,10},{4,12},{6,14},{8,0},{10,2},{12,4},{14,6},{1,9},{3,11}... | collective-permute-start | bytes 221192 | tf_op jit(solution)/shard_map/ppermute | solution.py:617
  291.8 17.6 %collective-permute-start.32 = (bf16[3,96,128]{2,1,0:T(8,128)(2,1)}, bf16[3,96,128]{2,1,0:T(8,128)(2,1)S(1)}, u32[]{:S(2)}, u32[]{:S(2)}) collective-permute-start(bf16[3,96,128]{2,1,0:T(8,128)(2,1)} %get-tuple-element.114), channel_id=1, source_target_pairs={{0,12},{2,14},{4,0},{6,2},{8,4},{10,6},{12,8},{14,10},{1,13},{3,15... | collective-permute-start | bytes 221192 | tf_op jit(solution)/shard_map/ppermute | solution.py:617
  295.4 14.0 %collective-permute-start.33 = (bf16[3,96,128]{2,1,0:T(8,128)(2,1)}, bf16[3,96,128]{2,1,0:T(8,128)(2,1)S(1)}, u32[]{:S(2)}, u32[]{:S(2)}) collective-permute-start(bf16[3,96,128]{2,1,0:T(8,128)(2,1)} %get-tuple-element.115), channel_id=1, source_target_pairs={{0,2},{2,0},{4,6},{6,4},{8,10},{10,8},{12,14},{14,12},{1,3},{3,1},... | collective-permute-start | bytes 221192 | tf_op jit(solution)/shard_map/ppermute | solution.py:617
  295.7 13.8 %collective-permute-start.34 = (bf16[3,96,128]{2,1,0:T(8,128)(2,1)}, bf16[3,96,128]{2,1,0:T(8,128)(2,1)S(1)}, u32[]{:S(2)}, u32[]{:S(2)}) collective-permute-start(bf16[3,96,128]{2,1,0:T(8,128)(2,1)} %get-tuple-element.116), channel_id=1, source_target_pairs={{0,6},{2,4},{4,10},{6,8},{8,14},{10,12},{12,2},{14,0},{1,7},{3,5},... | collective-permute-start | bytes 221192 | tf_op jit(solution)/shard_map/ppermute | solution.py:617
  300.3 17.6 %collective-permute-start.35 = (bf16[3,96,128]{2,1,0:T(8,128)(2,1)}, bf16[3,96,128]{2,1,0:T(8,128)(2,1)S(1)}, u32[]{:S(2)}, u32[]{:S(2)}) collective-permute-start(bf16[3,96,128]{2,1,0:T(8,128)(2,1)} %get-tuple-element.117), channel_id=1, source_target_pairs={{0,10},{2,8},{4,14},{6,12},{8,2},{10,0},{12,6},{14,4},{1,11},{3,9}... | collective-permute-start | bytes 221192 | tf_op jit(solution)/shard_map/ppermute | solution.py:617
  305.3 12.6 %collective-permute-start.36 = (bf16[3,96,128]{2,1,0:T(8,128)(2,1)}, bf16[3,96,128]{2,1,0:T(8,128)(2,1)S(1)}, u32[]{:S(2)}, u32[]{:S(2)}) collective-permute-start(bf16[3,96,128]{2,1,0:T(8,128)(2,1)} %get-tuple-element.118), channel_id=1, source_target_pairs={{0,14},{2,12},{4,2},{6,0},{8,6},{10,4},{12,10},{14,8},{1,15},{3,13... | collective-permute-start | bytes 221192 | tf_op jit(solution)/shard_map/ppermute | solution.py:617
  341.6 19.9 %collective-permute-start.37 = (bf16[3,288,128]{2,1,0:T(8,128)(2,1)}, bf16[3,288,128]{2,1,0:T(8,128)(2,1)S(1)}, u32[]{:S(2)}, u32[]{:S(2)}) collective-permute-start(bf16[3,288,128]{2,1,0:T(8,128)(2,1)} %get-tuple-element.120), channel_id=1, source_target_pairs={{0,12},{2,14},{4,0},{6,2},{8,4},{10,6},{12,8},{14,10},{1,13},{3,15... | collective-permute-start | bytes 663560 | tf_op jit(solution)/shard_map/ppermute | solution.py:617
  348.3 46.1 %collective-permute-start.38 = (bf16[3,288,128]{2,1,0:T(8,128)(2,1)}, bf16[3,288,128]{2,1,0:T(8,128)(2,1)S(1)}, u32[]{:S(2)}, u32[]{:S(2)}) collective-permute-start(bf16[3,288,128]{2,1,0:T(8,128)(2,1)} %get-tuple-element.121), channel_id=1, source_target_pairs={{0,8},{2,10},{4,12},{6,14},{8,0},{10,2},{12,4},{14,6},{1,9},{3,11}... | collective-permute-start | bytes 663560 | tf_op jit(solution)/shard_map/ppermute | solution.py:617
  349.5 45.1 %collective-permute-start.39 = (bf16[3,288,128]{2,1,0:T(8,128)(2,1)}, bf16[3,288,128]{2,1,0:T(8,128)(2,1)S(1)}, u32[]{:S(2)}, u32[]{:S(2)}) collective-permute-start(bf16[3,288,128]{2,1,0:T(8,128)(2,1)} %get-tuple-element.122), channel_id=1, source_target_pairs={{0,4},{2,6},{4,8},{6,10},{8,12},{10,14},{12,0},{14,2},{1,5},{3,7},... | collective-permute-start | bytes 663560 | tf_op jit(solution)/shard_map/ppermute | solution.py:617
  349.7 44.9 %collective-permute-start.40 = (bf16[3,288,128]{2,1,0:T(8,128)(2,1)}, bf16[3,288,128]{2,1,0:T(8,128)(2,1)S(1)}, u32[]{:S(2)}, u32[]{:S(2)}) collective-permute-start(bf16[3,288,128]{2,1,0:T(8,128)(2,1)} %get-tuple-element.123), channel_id=1, source_target_pairs={{0,2},{2,0},{4,6},{6,4},{8,10},{10,8},{12,14},{14,12},{1,3},{3,1},... | collective-permute-start | bytes 663560 | tf_op jit(solution)/shard_map/ppermute | solution.py:617
  352.0 42.6 %collective-permute-start.41 = (bf16[3,288,128]{2,1,0:T(8,128)(2,1)}, bf16[3,288,128]{2,1,0:T(8,128)(2,1)S(1)}, u32[]{:S(2)}, u32[]{:S(2)}) collective-permute-start(bf16[3,288,128]{2,1,0:T(8,128)(2,1)} %get-tuple-element.124), channel_id=1, source_target_pairs={{0,14},{2,12},{4,2},{6,0},{8,6},{10,4},{12,10},{14,8},{1,15},{3,13... | collective-permute-start | bytes 663560 | tf_op jit(solution)/shard_map/ppermute | solution.py:617
  361.5 73.7 %collective-permute-start.42 = (bf16[3,288,128]{2,1,0:T(8,128)(2,1)}, bf16[3,288,128]{2,1,0:T(8,128)(2,1)S(1)}, u32[]{:S(2)}, u32[]{:S(2)}) collective-permute-start(bf16[3,288,128]{2,1,0:T(8,128)(2,1)} %get-tuple-element.125), channel_id=1, source_target_pairs={{0,10},{2,8},{4,14},{6,12},{8,2},{10,0},{12,6},{14,4},{1,11},{3,9}... | collective-permute-start | bytes 663560 | tf_op jit(solution)/shard_map/ppermute | solution.py:617
  394.4 40.8 %collective-permute-start.43 = (bf16[3,288,128]{2,1,0:T(8,128)(2,1)}, bf16[3,288,128]{2,1,0:T(8,128)(2,1)S(1)}, u32[]{:S(2)}, u32[]{:S(2)}) collective-permute-start(bf16[3,288,128]{2,1,0:T(8,128)(2,1)} %get-tuple-element.126), channel_id=1, source_target_pairs={{0,6},{2,4},{4,10},{6,8},{8,14},{10,12},{12,2},{14,0},{1,7},{3,5},... | collective-permute-start | bytes 663560 | tf_op jit(solution)/shard_map/ppermute | solution.py:617
  446.4 26.0 %collective-permute-start.47 = (bf16[256,1024]{1,0:T(8,128)(2,1)}, bf16[256,1024]{1,0:T(8,128)(2,1)}, u32[]{:S(2)}, u32[]{:S(2)}) collective-permute-start(bf16[256,1024]{1,0:T(8,128)(2,1)} %get-tuple-element.139), channel_id=1, source_target_pairs={{0,2},{2,0},{1,3},{3,1},{4,6},{6,4},{5,7},{7,5},{8,10},{10,8},{9,1... | collective-permute-start | bytes 1572872 | tf_op jit(solution)/shard_map/ppermute | solution.py:602
  446.7 27.0 %collective-permute-start.51 = (bf16[256,1024]{1,0:T(8,128)(2,1)}, bf16[256,1024]{1,0:T(8,128)(2,1)}, u32[]{:S(2)}, u32[]{:S(2)}) collective-permute-start(bf16[256,1024]{1,0:T(8,128)(2,1)} %get-tuple-element.143), channel_id=1, source_target_pairs={{0,16},{16,0},{1,17},{17,1},{2,18},{18,2},{3,19},{19,3},{4,20},{20... | collective-permute-start | bytes 1572872 | tf_op jit(solution)/shard_map/ppermute | solution.py:599
  448.3 75.9 %collective-permute-start.44 = (bf16[576,1024]{1,0:T(8,128)(2,1)}, bf16[576,1024]{1,0:T(8,128)(2,1)S(1)}, u32[]{:S(2)}, u32[]{:S(2)}) collective-permute-start(bf16[576,1024]{1,0:T(8,128)(2,1)} %get-tuple-element.131.part_ref), channel_id=1, source_target_pairs={{0,1},{1,0},{2,3},{3,2},{4,5},{5,4},{6,7},{7,6},{8,9},{9,8},{10,11... | collective-permute-start | bytes 3538952 | tf_op jit(solution)/shard_map/ppermute | solution.py:605
  448.4 48.5 %collective-permute-start.28 = (bf16[288,1024]{1,0:T(8,128)(2,1)S(1)}, bf16[288,1024]{1,0:T(8,128)(2,1)S(1)}, u32[]{:S(2)}, u32[]{:S(2)}) collective-permute-start(bf16[288,1024]{1,0:T(8,128)(2,1)S(1)} %constant_dynamic-slice_fusion.1), channel_id=1, source_target_pairs={{0,2},{2,0},{1,3},{3,1},{4,6},{6,4},{5,7},{7,5},{8,10},{10,8},{9,1... | collective-permute-start | bytes 1769480 | tf_op jit(solution)/shard_map/ppermute | solution.py:602
  450.4 57.7 %collective-permute-start.49 = (bf16[256,1024]{1,0:T(8,128)(2,1)}, bf16[256,1024]{1,0:T(8,128)(2,1)S(1)}, u32[]{:S(2)}, u32[]{:S(2)}) collective-permute-start(bf16[256,1024]{1,0:T(8,128)(2,1)} %get-tuple-element.140), channel_id=1, source_target_pairs={{0,2},{2,0},{1,3},{3,1},{4,6},{6,4},{5,7},{7,5},{8,10},{10,8},{9,1... | collective-permute-start | bytes 1572872 | tf_op jit(solution)/shard_map/ppermute | solution.py:602
  472.4 35.7 %collective-permute-start.50 = (bf16[256,1024]{1,0:T(8,128)(2,1)S(1)}, bf16[256,1024]{1,0:T(8,128)(2,1)S(1)}, u32[]{:S(2)}, u32[]{:S(2)}) collective-permute-start(bf16[256,1024]{1,0:T(8,128)(2,1)S(1)} %copy-done.69), channel_id=1, source_target_pairs={{0,16},{16,0},{1,17},{17,1},{2,18},{18,2},{3,19},{19,3},{4,20},{20... | collective-permute-start | bytes 1572872 | tf_op jit(solution)/shard_map/ppermute | solution.py:599
  473.7 34.5 %collective-permute-start.48 = (bf16[256,1024]{1,0:T(8,128)(2,1)S(1)}, bf16[256,1024]{1,0:T(8,128)(2,1)S(1)}, u32[]{:S(2)}, u32[]{:S(2)}) collective-permute-start(bf16[256,1024]{1,0:T(8,128)(2,1)S(1)} %add_convert_fusion.1), channel_id=1, source_target_pairs={{0,16},{16,0},{1,17},{17,1},{2,18},{18,2},{3,19},{19,3},{4,20},{20... | collective-permute-start | bytes 1572872 | tf_op jit(solution)/shard_map/ppermute | solution.py:599
  496.9 21.0 %collective-permute-start.52 = (bf16[256,1024]{1,0:T(8,128)(2,1)S(1)}, bf16[256,1024]{1,0:T(8,128)(2,1)S(1)}, u32[]{:S(2)}, u32[]{:S(2)}) collective-permute-start(bf16[256,1024]{1,0:T(8,128)(2,1)S(1)} %add_convert_fusion), channel_id=1, source_target_pairs={{0,2},{2,0},{1,3},{3,1},{4,6},{6,4},{5,7},{7,5},{8,10},{10,8},{9,1... | collective-permute-start | bytes 1572872 | tf_op jit(solution)/shard_map/ppermute | solution.py:602
  508.1 24.8 %collective-permute-start.29 = (bf16[288,1024]{1,0:T(8,128)(2,1)S(1)}, bf16[288,1024]{1,0:T(8,128)(2,1)S(1)}, u32[]{:S(2)}, u32[]{:S(2)}) collective-permute-start(bf16[288,1024]{1,0:T(8,128)(2,1)S(1)} %collective-permute-done.28.near_ref), channel_id=1, source_target_pairs={{0,1},{1,0},{2,3},{3,2},{4,5},{5,4},{6,7},{7,6},{8,9},{9,8},{10,11... | collective-permute-start | bytes 1769480 | tf_op jit(solution)/shard_map/ppermute | solution.py:605
  522.2 17.6 %collective-permute-start.53 = (bf16[128,1024]{1,0:T(8,128)(2,1)}, bf16[128,1024]{1,0:T(8,128)(2,1)}, u32[]{:S(2)}, u32[]{:S(2)}) collective-permute-start(bf16[128,1024]{1,0:T(8,128)(2,1)} %get-tuple-element.145), channel_id=1, source_target_pairs={{0,12},{4,0},{8,4},{12,8},{1,13},{5,1},{9,5},{13,9},{2,14},{6,2},{... | collective-permute-start | bytes 786440 | tf_op jit(solution)/shard_map/ppermute | solution.py:599
  522.2 19.4 %collective-permute-start.54 = (bf16[128,1024]{1,0:T(8,128)(2,1)}, bf16[128,1024]{1,0:T(8,128)(2,1)}, u32[]{:S(2)}, u32[]{:S(2)}) collective-permute-start(bf16[128,1024]{1,0:T(8,128)(2,1)} %get-tuple-element.146), channel_id=1, source_target_pairs={{0,8},{4,12},{8,0},{12,4},{1,9},{5,13},{9,1},{13,5},{2,10},{6,14},... | collective-permute-start | bytes 786440 | tf_op jit(solution)/shard_map/ppermute | solution.py:599
  522.3 19.4 %collective-permute-start.55 = (bf16[128,1024]{1,0:T(8,128)(2,1)}, bf16[128,1024]{1,0:T(8,128)(2,1)}, u32[]{:S(2)}, u32[]{:S(2)}) collective-permute-start(bf16[128,1024]{1,0:T(8,128)(2,1)} %get-tuple-element.147), channel_id=1, source_target_pairs={{0,4},{4,8},{8,12},{12,0},{1,5},{5,9},{9,13},{13,1},{2,6},{6,10},{... | collective-permute-start | bytes 786440 | tf_op jit(solution)/shard_map/ppermute | solution.py:599
  531.4 7.1 %collective-permute-start.56 = (f32[128,384]{1,0:T(8,128)}, f32[128,384]{1,0:T(8,128)}, u32[]{:S(2)}, u32[]{:S(2)}) collective-permute-start(f32[128,384]{1,0:T(8,128)} %get-tuple-element.149), channel_id=1, source_target_pairs={{0,2},{2,0},{1,3},{3,1},{4,6},{6,4},{5,7},{7,5},{8,10},{10,8},{9,1... | collective-permute-start | bytes 589832 | tf_op jit(solution)/shard_map/ppermute | solution.py:602
  537.9 14.0 %collective-permute-start.45 = (bf16[288,1024]{1,0:T(8,128)(2,1)S(1)}, bf16[288,1024]{1,0:T(8,128)(2,1)S(1)}, u32[]{:S(2)}, u32[]{:S(2)}) collective-permute-start(bf16[288,1024]{1,0:T(8,128)(2,1)S(1)} %constant_dynamic-slice_fusion), channel_id=1, source_target_pairs={{0,2},{2,0},{1,3},{3,1},{4,6},{6,4},{5,7},{7,5},{8,10},{10,8},{9,1... | collective-permute-start | bytes 1769480 | tf_op jit(solution)/shard_map/ppermute | solution.py:602
  539.8 4.7 collective-permute-start.57
  544.5 9.3 %collective-permute-start.58 = (f32[16,384]{1,0:T(8,128)S(1)}, f32[16,384]{1,0:T(8,128)S(1)}, u32[]{:S(2)}, u32[]{:S(2)}) collective-permute-start(f32[16,384]{1,0:T(8,128)S(1)} %get-tuple-element.188), channel_id=1, source_target_pairs={{0,12},{4,0},{8,4},{12,8},{1,13},{5,1},{9,5},{13,9},{2,14},{6,2},{... | collective-permute-start | bytes 73736 | tf_op jit(solution)/shard_map/ppermute | solution.py:599
  546.9 6.9 %collective-permute-start.60 = (f32[16,384]{1,0:T(8,128)S(1)}, f32[16,384]{1,0:T(8,128)S(1)}, u32[]{:S(2)}, u32[]{:S(2)}) collective-permute-start(f32[16,384]{1,0:T(8,128)S(1)} %get-tuple-element.189), channel_id=1, source_target_pairs={{0,4},{4,8},{8,12},{12,0},{1,5},{5,9},{9,13},{13,1},{2,6},{6,10},{... | collective-permute-start | bytes 73736 | tf_op jit(solution)/shard_map/ppermute | solution.py:599
  547.0 6.8 %collective-permute-start.59 = (f32[16,384]{1,0:T(8,128)S(1)}, f32[16,384]{1,0:T(8,128)S(1)}, u32[]{:S(2)}, u32[]{:S(2)}) collective-permute-start(f32[16,384]{1,0:T(8,128)S(1)} %get-tuple-element.190), channel_id=1, source_target_pairs={{0,8},{4,12},{8,0},{12,4},{1,9},{5,13},{9,1},{13,5},{2,10},{6,14},... | collective-permute-start | bytes 73736 | tf_op jit(solution)/shard_map/ppermute | solution.py:599
  551.9 3.7 collective-permute-start.46
  (69 other events, 786.4 us)
Sparse Core Ops, SparseCore 0:
  11.4 171.0 all-gather.1
  275.2 224.3 reduce-scatter.1

commit v3 on v2

v3 whole, which is shorter than its diff:
```python
import functools

import jax
import jax.numpy as jnp
from jax import lax
from jax.experimental import pallas as pl
from jax.experimental.pallas import tpu as pltpu
from jax.sharding import Mesh
from jax.sharding import PartitionSpec as P

HD = 64
LANES = 128
CORES = 2
SMALL_ROWS = 16
SMALL_LANES = 3 * LANES
FLOPS, BYTES = 1e+09, 3e+06

eps_norm = 1e-06
masked_score = -1e30
root_half = 0.7071067811865476
inv_root_two_pi = 0.3989422804014327
score_scale = HD ** (-0.5)

bf16 = jnp.bfloat16
f32 = jnp.float32
NN = (((1,), (0,)), ((), ()))
NT = (((1,), (1,)), ((), ()))

B_OUT, B_DOWN, GAIN1, SHIFT1, GAIN2, SHIFT2, SCALE1, SCALE2 = range(8)


def mm(left, right, dims=NN):
    return lax.dot_general(left, right, dims, preferred_element_type=f32)


def turn(values):
    return jnp.transpose(values.astype(f32)).astype(bf16)


def normalise(values):
    average = jnp.mean(values, axis=-1, keepdims=True)
    centred = values - average
    variance = jnp.mean(centred * centred, axis=-1, keepdims=True)
    inv_std = lax.rsqrt(variance + eps_norm)
    return centred * inv_std, inv_std


def norm_back(grad_in, normed, inv_std):
    first_mean = jnp.mean(grad_in, axis=-1, keepdims=True)
    second_mean = jnp.mean(grad_in * normed, axis=-1, keepdims=True)
    return inv_std * (grad_in - first_mean - normed * second_mean)


def row(table, index):
    return table[index : index + 1, :]


def column_sum(values):
    return jnp.sum(values, axis=0, keepdims=True)


def low_lanes(shape):
    return lax.broadcasted_iota(jnp.int32, shape, 1) < HD


def swap(values):
    return pltpu.roll(values, HD, 1)


def fold(wide):
    half = wide.shape[0] // 2
    return wide[:half] + swap(wide[half:])


def unfold(folded):
    low = low_lanes(folded.shape)
    return jnp.concatenate(
        [jnp.where(low, folded, 0.0), jnp.where(low, swap(folded), 0.0)], axis=0
    )


def owner_of(place_ref, slot, context):
    z, y = place_ref[1], place_ref[2]
    group = y if slot < context else 1 - y
    return group * context + lax.rem(z + slot % context, context)


def spread_mask(sc, last, columns):
    entry = lax.broadcasted_iota(jnp.int32, (LANES, columns), 0)
    column = lax.broadcasted_iota(jnp.int32, (LANES, columns), 1)
    return jnp.where(
        (entry < last) & (lax.rem(column, HD) == sc * last + entry), 1.0, 0.0
    ).astype(bf16)


def block_rows(step_rows):
    return -(-step_rows // (4 * SMALL_ROWS)) * SMALL_ROWS


def chunks_of(first, size, block):
    while size:
        count = min(size, block - first % block)
        yield first, count, first // block * 2 * LANES, first % block
        first, size = first + count, size - count


def bundle_kernel(place_ref, w_ref, small_ref, tokens_ref, own_ref, *refs):
    outs, scratch = refs[:-1], refs[-1]
    z, spot = place_ref[1], 2 * place_ref[2] + place_ref[3]
    rows = w_ref.shape[0]
    step_rows = rows + small_ref.shape[0]
    block = own_ref.shape[0]
    count = len(outs) + 1
    columns = w_ref.shape[1] // 3
    images, row_count, _ = tokens_ref.shape
    quarter = row_count // 4
    low = low_lanes((rows, LANES))
    scratch[...] = jnp.zeros_like(scratch)
    for head in range(count):
        first = head // 2 * LANES
        query, key, value = (
            w_ref[:, part * columns + first : part * columns + first + LANES].astype(f32)
            for part in range(3)
        )
        if head % 2:
            query, value = swap(query), swap(value)
        else:
            key = swap(key)
        both = jnp.where(low, query, key).astype(bf16)
        value = jnp.where(low, value, 0.0).astype(bf16)
        for start, size, lane, line in chunks_of(0, rows, block):
            here = slice(line, line + size)
            scratch[head, here, lane : lane + LANES] = both[start : start + size]
            scratch[head, here, lane + LANES : lane + 2 * LANES] = value[start : start + size]
        for start, size, lane, line in chunks_of(rows, step_rows - rows, block):
            here = slice(line, line + size)
            scratch[head, here, lane : lane + LANES] = small_ref[start - rows : start - rows + size]
    own_ref[...] = scratch[z]
    for j, out in enumerate(outs):
        for image in range(images):
            there = pl.ds(pl.multiple_of(spot * quarter, 16), quarter)
            out[image * quarter : (image + 1) * quarter, :] = tokens_ref[image, there, :]
        out[images * quarter :, :] = scratch[lax.rem(z + j + 1, count)]


def prepare_kernel(sizes, place_ref, *refs):
    n_shard, n_context, last, heads = sizes
    stacks = refs[:n_shard]
    weight_ref, vec_ref, bias_ref, bup_ref = refs[n_shard:]
    x, z = place_ref[0], place_ref[1]
    width = weight_ref.shape[0]
    piece_rows = width // (n_shard * n_context)
    block = stacks[0].shape[0] // n_context
    vec, qv, up = None, None, None
    for xr in range(n_shard):
        for zr in range(n_context):
            sc = lax.rem(x - xr + n_shard, n_shard) * n_context
            sc = sc + lax.rem(z - zr + n_context, n_context)
            stack = stacks[xr]
            base = pl.multiple_of(sc * piece_rows, 16)
            for start, size, lane, line in chunks_of(0, piece_rows, block):
                line = zr * block + line
                weight_ref[pl.ds(base + start, size), :] = stack[
                    line : line + size, lane : lane + 2 * LANES
                ]

            def small(index):
                start = piece_rows + index * SMALL_ROWS
                lane, line = start // block * 2 * LANES, zr * block + start % block
                return stack[line : line + SMALL_ROWS, lane : lane + LANES]

            entry = lax.broadcasted_iota(jnp.int32, (LANES, width), 0)
            column = lax.broadcasted_iota(jnp.int32, (LANES, width), 1)
            place = jnp.where(
                (entry < piece_rows) & (column == sc * piece_rows + entry), 1.0, 0.0
            ).astype(bf16)
            term = mm(small(0), place)
            vec = term if vec is None else vec + term
            term = mm(small(1), spread_mask(sc, last, bup_ref.shape[1]))
            up = term if up is None else up + term
            term = mm(small(2), spread_mask(sc, last, 2 * LANES))
            qv = term if qv is None else qv + term
    vec_ref[...] = vec
    line = lax.broadcasted_iota(jnp.int32, up.shape, 0)
    column = lax.broadcasted_iota(jnp.int32, up.shape, 1)
    bup_ref[...] = column_sum(jnp.where(column // HD == line, up, 0.0))
    line = lax.broadcasted_iota(jnp.int32, qv.shape, 0)
    column = lax.broadcasted_iota(jnp.int32, qv.shape, 1) // HD
    chosen = ((line == z) & (column == 0)) | ((line == heads + z) & (column == 2))
    bias_ref[...] = jnp.zeros_like(bias_ref)
    bias_ref[0:1, :] = column_sum(jnp.where(chosen, qv, 0.0))


def attend_kernel(
    n_context, count_ref, place_ref, pos_ref, weight_ref, vec_ref, bias_ref, own_ref, *refs
):
    blocks = 2 * n_context
    n_quarter = 4 * (n_context - 1)
    quarters = refs[:n_quarter]
    outs = refs[n_quarter : n_quarter + blocks]
    log_ref, norm_ref, qk_ref, v_ref, keys, tokens = refs[n_quarter + blocks :]
    y, core = place_ref[2], place_ref[3]
    rows = own_ref.shape[1] // 2
    half = rows // 2
    gain, shift = vec_ref[GAIN1 : GAIN1 + 1, :], vec_ref[SHIFT1 : SHIFT1 + 1, :]
    low = low_lanes((rows, LANES))
    for jz in range(n_context):
        for jy in range(2):
            slot = jy * n_context + jz
            lines = slice(slot * rows, (slot + 1) * rows)
            if jz == 0:
                first = pl.multiple_of((y if jy == 0 else 1 - y) * rows, 16)
                block = own_ref[0, pl.ds(first, rows), :]
            else:
                for other in range(2):
                    spot = core if other == 0 else 1 - core
                    first = pl.multiple_of(spot * half, 16)
                    quarter = quarters[4 * (jz - 1) + 2 * other + jy]
                    tokens[pl.ds(first, half), :] = quarter[...]
                block = tokens[...]
            normed, _ = normalise(block.astype(f32))
            norm_low = (normed * gain + shift).astype(bf16)
            norm_ref[0, lines, :] = norm_low
            qkv = mm(norm_low, weight_ref[...]) + bias_ref[0:1, :]
            qk_ref[0, lines, :] = qkv[:, :LANES].astype(bf16)
            v_ref[0, lines, :] = qkv[:, LANES:].astype(bf16)
            keys[lines, :] = jnp.where(low, swap(qkv[:, :LANES]), 0.0).astype(bf16)
    valid = pos_ref[...] < count_ref[pl.program_id(0)]
    for j in range(blocks):
        query = qk_ref[0, j * rows : (j + 1) * rows] * bf16(score_scale)
        scores = jnp.where(valid, mm(query, keys[...], NT), masked_score)
        highest = jnp.max(scores, axis=1, keepdims=True)
        exponent = jnp.exp(scores - highest)
        total = jnp.sum(exponent, axis=1, keepdims=True)
        mixed = mm(exponent.astype(bf16), v_ref[0]) / total
        outs[j][0] = fold(mixed).astype(bf16)
        log_ref[0, j * rows : (j + 1) * rows] = highest + jnp.log(total)


def attend_back_kernel(count_ref, pos_ref, log_ref, norm_ref, qk_ref, v_ref, *refs):
    blocks = (len(refs) - 6) // 3
    mixes, grads, outs = (refs[i * blocks : (i + 1) * blocks] for i in range(3))
    weight_ref, bias_ref, keys, sums, query_grads, turned = refs[3 * blocks :]
    rows = qk_ref.shape[1] // blocks
    half = rows // 2
    low = low_lanes((rows, LANES))
    low_half = low_lanes((half, LANES))
    for j in range(blocks):
        pack = qk_ref[0, j * rows : (j + 1) * rows].astype(f32)
        keys[j * rows : (j + 1) * rows] = jnp.where(low, swap(pack), 0.0).astype(bf16)
    valid = pos_ref[...] < count_ref[pl.program_id(0)]
    for j in range(blocks):
        lines = slice(j * rows, (j + 1) * rows)
        query = qk_ref[0, lines] * bf16(score_scale)
        grad_wide = unfold(grads[j][0].astype(f32))
        mix_wide = unfold(mixes[j][0].astype(f32))
        delta = jnp.sum(grad_wide * mix_wide, axis=1, keepdims=True)
        grad = grad_wide.astype(bf16)
        scores = jnp.where(valid, mm(query, keys[...], NT), masked_score)
        probs = jnp.exp(scores - log_ref[0, lines])
        weight_grad = mm(grad, v_ref[0], NT)
        score_grad = (probs * (weight_grad - delta)).astype(bf16)
        query_grads[lines] = mm(score_grad, keys[...]) * score_scale
        query_t = jnp.transpose(query.astype(f32))[:HD].astype(bf16)
        grad_t = jnp.transpose(grad_wide)[:HD].astype(bf16)
        key_part = mm(query_t, score_grad)
        value_part = mm(grad_t, probs.astype(bf16))
        if j == 0:
            sums[:HD] = key_part
            sums[HD:] = value_part
        else:
            sums[:HD] = sums[:HD] + key_part
            sums[HD:] = sums[HD:] + value_part
    query_sum, value_sum = None, None
    for j in range(blocks):
        lines = slice(j * rows, (j + 1) * rows)
        both = jnp.transpose(sums[:, lines])
        query_grad = query_grads[lines]
        outs[j][0, :rows] = jnp.where(low, query_grad, swap(both)).astype(bf16)
        outs[j][0, rows:] = jnp.where(low_half, swap(both[:half]), both[half:]).astype(bf16)
        term = column_sum(query_grad.astype(bf16).astype(f32))
        query_sum = term if query_sum is None else query_sum + term
        term = column_sum(swap(both).astype(bf16).astype(f32))
        value_sum = term if value_sum is None else value_sum + term
    turned[:HD] = jnp.transpose(query_grads[...])[:HD].astype(bf16)
    turned[HD:] = sums[...].astype(bf16)

    @pl.when(pl.program_id(0) == 0)
    def _():
        weight_ref[...] = jnp.zeros_like(weight_ref)
        bias_ref[...] = jnp.zeros_like(bias_ref)

    weight_ref[...] = weight_ref[...] + mm(turned[...], norm_ref[0])
    bias_ref[0:1, :] = bias_ref[0:1, :] + query_sum
    bias_ref[1:2, :] = bias_ref[1:2, :] + value_sum


def project_kernel(n_context, place_ref, *refs):
    blocks = len(refs) - 5
    folded, (own_ref, far_ref, mixed_ref, part_ref, scratch) = refs[:blocks], refs[blocks:]
    y = place_ref[2]
    images, half, _ = folded[0].shape
    rows = 2 * half
    for slot in range(blocks):
        scratch[owner_of(place_ref, slot, n_context)] = folded[slot][...]
    low = low_lanes((half, LANES))
    for pair in range(blocks // 2):
        columns = slice(pair * LANES, (pair + 1) * LANES)
        for image in range(images):
            first = scratch[2 * pair, image].astype(f32)
            second = scratch[2 * pair + 1, image].astype(f32)
            start = image * rows
            mixed_ref[start : start + half, columns] = jnp.where(
                low, first, swap(second)
            ).astype(bf16)
            mixed_ref[start + half : start + rows, columns] = jnp.where(
                low, swap(first), second
            ).astype(bf16)
    size = mixed_ref.shape[1] // 2
    total = None
    for group, ref in ((y, own_ref), (1 - y, far_ref)):
        mixed = mixed_ref[:, pl.ds(pl.multiple_of(group * size, LANES), size)]
        term = mm(mixed, ref[...], NT)
        total = term if total is None else total + term
    part_ref[...] = total.astype(bf16)


def norm_kernel(place_ref, x_ref, part_ref, other_ref, vec_ref, norm_ref, half_ref):
    vec = vec_ref[...]
    branch = part_ref[...].astype(f32) + other_ref[...].astype(f32) + row(vec, B_OUT)
    middle = x_ref[...].astype(f32) + row(vec, SCALE1) * branch
    normed, _ = normalise(middle)
    norm_ref[...] = (normed * row(vec, GAIN2) + row(vec, SHIFT2)).astype(bf16)
    half = half_ref.shape[0]
    half_ref[...] = norm_ref[pl.ds(pl.multiple_of(place_ref[3] * half, 16), half), :]


def mlp_kernel(
    place_ref, own_ref, near_ref, far_ref, cot_ref, vec_ref, bup_ref, weight_ref,
    norm_ref, grad_ref, act_ref, pre_ref, gup_ref, *refs
):
    outs, sums = refs[:4], refs[4]
    y, core = place_ref[2], place_ref[3]
    tokens, half = own_ref.shape[0], near_ref.shape[0]
    images = cot_ref.shape[0]
    rows = tokens // images
    mine = pl.multiple_of(core * half, 16)
    other = pl.multiple_of((1 - core) * half, 16)
    norm_ref[:tokens] = own_ref[...]
    norm_ref[pl.ds(tokens + mine, half), :] = near_ref[...]
    norm_ref[pl.ds(tokens + other, half), :] = far_ref[...]
    scale = vec_ref[SCALE2 : SCALE2 + 1, :]
    for yr in range(2):
        first = pl.multiple_of((y if yr == 0 else 1 - y) * rows, 16)
        for image in range(images):
            start = yr * tokens + image * rows
            value = scale * cot_ref[image, pl.ds(first, rows), :].astype(f32)
            grad_ref[start : start + rows] = value.astype(bf16)
    norm_low, branch_grad = norm_ref[...], grad_ref[...]
    hidden = bup_ref.shape[1]
    first = weight_ref.shape[1] - 2 * hidden
    step = hidden // 4
    down, back = None, None
    for part in range(4):
        columns = slice(part * step, (part + 1) * step)
        up = weight_ref[:, first + part * step : first + (part + 1) * step]
        start = first + hidden + part * step
        turned = weight_ref[:, start : start + step]
        pre = mm(norm_low, up) + bup_ref[:, columns]
        erf_term = 0.5 * (1.0 + lax.erf(pre * root_half))
        act = (pre * erf_term).astype(bf16)
        act_ref[:, columns] = act
        term = mm(act, turned, NT)
        down = term if down is None else down + term
        slope = erf_term + pre * inv_root_two_pi * jnp.exp(-0.5 * pre * pre)
        pre_grad = (mm(branch_grad, turned) * slope).astype(bf16)
        pre_ref[:, columns] = pre_grad
        gup_ref[:, columns] = column_sum(pre_grad.astype(f32))
        term = mm(pre_grad, up, NT)
        back = term if back is None else back + term
    for kind, value in ((0, back), (1, down)):
        sums[...] = value.astype(bf16)
        for out, spot in ((outs[2 * kind], mine), (outs[2 * kind + 1], other)):
            out[:half] = sums[pl.ds(spot, half), :]
            out[half:] = sums[pl.ds(tokens + spot, half), :]


def mlp_weights_kernel(norm_ref, grad_ref, act_ref, pre_ref, out_ref, norm_t, grad_t):
    kind = pl.program_id(0)

    @pl.when((kind == 0) & (pl.program_id(1) == 0))
    def _():
        norm_t[...] = turn(norm_ref[...])
        grad_t[...] = turn(grad_ref[...])

    @pl.when(kind == 0)
    def _():
        out_ref[...] = mm(norm_t[...], pre_ref[...]).astype(bf16)

    @pl.when(kind == 1)
    def _():
        out_ref[...] = mm(grad_t[...], act_ref[...]).astype(bf16)


def by_core(core, near_ref, far_ref, whole):
    half = near_ref.shape[0]
    whole[pl.ds(pl.multiple_of(core * half, 16), half), :] = near_ref[...].astype(f32)
    whole[pl.ds(pl.multiple_of((1 - core) * half, 16), half), :] = far_ref[...].astype(f32)
    return whole[...]


def result_kernel(
    place_ref, x_ref, cot_ref, part_ref, other_ref, near_ref, far_ref, vec_ref,
    result_ref, sums_ref, whole,
):
    vec = vec_ref[...]
    branch = part_ref[...].astype(f32) + other_ref[...].astype(f32) + row(vec, B_OUT)
    middle = x_ref[...].astype(f32) + row(vec, SCALE1) * branch
    mlp = by_core(place_ref[3], near_ref, far_ref, whole) + row(vec, B_DOWN)
    result_ref[...] = (middle + row(vec, SCALE2) * mlp).astype(bf16)
    sums_ref[...] = jnp.zeros_like(sums_ref)
    sums_ref[0:1, :] = column_sum(cot_ref[...].astype(f32) * mlp)


def back_kernel(
    images, n_context, place_ref, x_ref, cot_ref, part_ref, other_ref, near_ref, far_ref,
    vec_ref, own_ref, distant_ref, *refs
):
    middle_grad_ref, proj_ref, sums_ref = refs[:3]
    outs, scratch, whole = refs[3:-2], refs[-2], refs[-1]
    y, core = place_ref[2], place_ref[3]
    tokens = x_ref.shape[0]
    vec = vec_ref[...]
    upstream = cot_ref[...].astype(f32)
    branch = part_ref[...].astype(f32) + other_ref[...].astype(f32) + row(vec, B_OUT)
    middle = x_ref[...].astype(f32) + row(vec, SCALE1) * branch
    normed, inv_std = normalise(middle)
    norm_grad = by_core(core, near_ref, far_ref, whole)
    middle_grad = upstream + norm_back(norm_grad * row(vec, GAIN2), normed, inv_std)
    middle_grad_ref[...] = middle_grad
    proj_wide = row(vec, SCALE1) * middle_grad
    proj = proj_wide.astype(bf16)
    proj_ref[...] = proj
    sums_ref[...] = jnp.zeros_like(sums_ref)
    for place, value in (
        (B_OUT, proj_wide),
        (B_DOWN, row(vec, SCALE2) * upstream),
        (GAIN2, norm_grad * normed),
        (SHIFT2, norm_grad),
        (SCALE1, middle_grad * branch),
    ):
        sums_ref[place : place + 1, :] = column_sum(value)
    rows = tokens // images
    half = rows // 2
    low = low_lanes((half, LANES))
    size = own_ref.shape[1]
    for group, ref in ((y, own_ref), (1 - y, distant_ref)):
        wide = mm(proj, ref[...])
        for pair in range(size // LANES):
            head = group * n_context + 2 * pair
            for image in range(images):
                block = wide[image * rows : (image + 1) * rows, pair * LANES : (pair + 1) * LANES]
                first, second = block[:half], block[half:]
                scratch[head, image] = jnp.where(low, first, swap(second)).astype(bf16)
                scratch[head + 1, image] = jnp.where(low, swap(first), second).astype(bf16)
    for slot in range(len(outs)):
        outs[slot][...] = scratch[owner_of(place_ref, slot, n_context)]


def out_weights_kernel(place_ref, proj_ref, mixed_ref, own_ref, far_ref):
    y = place_ref[2]
    columns = own_ref.shape[1]
    proj_t = turn(proj_ref[...])
    for group, ref in ((y, own_ref), (1 - y, far_ref)):
        mixed = mixed_ref[:, pl.ds(pl.multiple_of(group * columns, LANES), columns)]
        ref[...] = mm(proj_t, mixed).astype(bf16)


def qkv_back_kernel(n_context, place_ref, *refs):
    packs, (own_ref, far_ref, part_ref, scratch, grads) = refs[:-5], refs[-5:]
    y = place_ref[2]
    blocks = len(packs)
    images = packs[0].shape[0]
    rows = packs[0].shape[1] * 2 // 3
    half = rows // 2
    columns = grads.shape[3]
    for slot in range(blocks):
        scratch[owner_of(place_ref, slot, n_context)] = packs[slot][...]
    low = low_lanes((rows, LANES))
    low_half = low_lanes((half, LANES))
    total = None
    for group in range(2):
        for pair in range(columns // LANES):
            head = group * n_context + 2 * pair
            lanes = slice(pair * LANES, (pair + 1) * LANES)
            for image in range(images):
                first = scratch[head, image].astype(f32)
                second = scratch[head + 1, image].astype(f32)
                start = image * rows
                here = slice(start, start + rows)
                grads[group, 0, here, lanes] = jnp.where(
                    low, first[:rows], swap(second[:rows])
                ).astype(bf16)
                grads[group, 1, here, lanes] = jnp.where(
                    low, swap(first[:rows]), second[:rows]
                ).astype(bf16)
                grads[group, 2, start : start + half, lanes] = jnp.where(
                    low_half, first[rows:], swap(second[rows:])
                ).astype(bf16)
                grads[group, 2, start + half : start + rows, lanes] = jnp.where(
                    low_half, swap(first[rows:]), second[rows:]
                ).astype(bf16)
    for group, ref in ((y, own_ref), (1 - y, far_ref)):
        for part in range(3):
            term = mm(grads[group, part], ref[:, part * columns : (part + 1) * columns], NT)
            total = term if total is None else total + term
    part_ref[...] = total.astype(bf16)


def head_grads_kernel(place_ref, *refs):
    pieces, (out_ref, wout_ref, scratch) = refs[:-3], refs[-3:]
    z = place_ref[1]
    count = len(pieces)
    rows = out_ref.shape[0]
    for j in range(count):
        head = lax.rem(z + j, count)
        for part in range(3):
            start = pl.multiple_of(part * count * HD + head * HD, HD)
            scratch[pl.ds(start, HD), :] = pieces[j][part * HD : (part + 1) * HD].astype(f32)
    out_ref[...] = jnp.transpose(scratch[...])[:rows]
    for block in range(wout_ref.shape[0] // LANES):
        lines = slice(3 * HD + block * rows, 3 * HD + (block + 1) * rows)
        total = pieces[0][lines].astype(f32)
        for piece in pieces[1:]:
            total = total + piece[lines].astype(f32)
        wout_ref[block * LANES : (block + 1) * LANES, :] = jnp.transpose(total)


def finish_kernel(
    sizes, place_ref, x_ref, middle_grad_ref, part_ref, other_ref, vec_ref, sums_ref, extra_ref,
    gup_ref, gqv_ref, out_ref, own_ref, far_ref,
):
    n_shard, n_context, last = sizes
    x, z = place_ref[0], place_ref[1]
    width = x_ref.shape[1]
    piece_rows = width // (n_shard * n_context)
    norm_grad = part_ref[...].astype(f32) + other_ref[...].astype(f32)
    normed, inv_std = normalise(x_ref[...].astype(f32))
    gain = vec_ref[GAIN1 : GAIN1 + 1, :]
    out_ref[...] = (
        middle_grad_ref[...] + norm_back(norm_grad * gain, normed, inv_std)
    ).astype(bf16)
    line = lax.broadcasted_iota(jnp.int32, sums_ref.shape, 0)
    sums = jnp.where(line == GAIN1, column_sum(norm_grad * normed), sums_ref[...])
    sums = jnp.where(line == SHIFT1, column_sum(norm_grad), sums)
    sums = jnp.where(line == SCALE2, extra_ref[0:1, :], sums).astype(bf16)
    up = gup_ref[...]
    line = lax.broadcasted_iota(jnp.int32, (SMALL_ROWS, up.shape[1]), 0)
    column = lax.broadcasted_iota(jnp.int32, (SMALL_ROWS, up.shape[1]), 1) // HD
    up = jnp.where(column == line, up, 0.0).astype(bf16)
    line = lax.broadcasted_iota(jnp.int32, (SMALL_ROWS, LANES), 0)
    low = low_lanes((SMALL_ROWS, LANES))
    qv = jnp.where((line == z) & low, gqv_ref[0:1, :], 0.0)
    qv = (qv + jnp.where((line == n_context + z) & low, gqv_ref[1:2, :], 0.0)).astype(bf16)
    for xr in range(n_shard):
        for zr in range(n_context):
            sc = lax.rem(x - xr + n_shard, n_shard) * n_context
            sc = sc + lax.rem(z - zr + n_context, n_context)
            start = (xr * n_context + zr) * SMALL_ROWS
            lines = slice(start, start + SMALL_ROWS)
            entry = lax.broadcasted_iota(jnp.int32, (LANES, width), 0)
            column = lax.broadcasted_iota(jnp.int32, (LANES, width), 1)
            place = jnp.where(
                (entry < piece_rows) & (column == sc * piece_rows + entry), 1.0, 0.0
            ).astype(bf16)
            term = mm(sums, place, NT)
            own_ref[lines, :LANES] = term
            far_ref[lines, :] = term
            own_ref[lines, LANES : 2 * LANES] = mm(up, spread_mask(sc, last, up.shape[1]), NT)
            own_ref[lines, 2 * LANES :] = mm(qv, spread_mask(sc, last, LANES), NT)


def merge_kernel(place_ref, own_ref, near_ref, far_ref, out_ref):
    y, core, image = place_ref[2], place_ref[3], pl.program_id(0)
    half = near_ref.shape[0]
    rows = own_ref.shape[0]
    block = rows // 2
    out_ref[0, pl.ds(pl.multiple_of(y * rows, 16), rows), :] = own_ref[...].astype(f32)
    for part in range(2):
        first = image * rows + part * block
        source = first // half
        line = pl.multiple_of(first - source * half, 16)
        there = pl.multiple_of((1 - y) * rows + part * block, 16)

        @pl.when(source == core)
        def _():
            out_ref[0, pl.ds(there, block), :] = near_ref[pl.ds(line, block), :].astype(f32)

        @pl.when(source != core)
        def _():
            out_ref[0, pl.ds(there, block), :] = far_ref[pl.ds(line, block), :].astype(f32)


KERNEL_US = {
    "bundle": 3,
    "prepare": 2,
    "attend": 26,
    "project": 4,
    "norm": 4,
    "mlp": 19,
    "mlp_weights": 12,
    "back": 8,
    "out_weights": 3,
    "result": 6,
    "attend_back": 26,
    "qkv_back": 6,
    "finish": 6,
    "head_grads": 2,
    "merge": 4,
}


def cost_of(name):
    time = KERNEL_US[name]
    return pl.CostEstimate(
        flops=int(time * FLOPS), transcendentals=0, bytes_accessed=int(time * BYTES)
    )


def vmem():
    return pl.BlockSpec(memory_space=pltpu.VMEM)


def smem():
    return pl.BlockSpec(memory_space=pltpu.SMEM)


def shaped(shape, dtype):
    return jax.ShapeDtypeStruct(shape, dtype)


def call(kernel, name, out_shape, scratch, place, *operands):
    return pl.pallas_call(
        kernel,
        name=name,
        cost_estimate=cost_of(name),
        in_specs=[smem()] + [vmem()] * len(operands),
        out_specs=[vmem()] * len(out_shape),
        out_shape=out_shape,
        scratch_shapes=scratch,
    )(place, *operands)


def per_device(sizes, *args):
    (
        tokens_in,
        counts,
        w_qkv,
        b_qv,
        w_out,
        b_out,
        w_up,
        b_up,
        w_down,
        b_down,
        norm1_gain,
        norm1_bias,
        norm2_gain,
        norm2_bias,
        scale1,
        scale2,
        cotangent,
    ) = args
    n_shard, n_context, n_y = sizes
    images, row_count, width = tokens_in.shape
    piece_rows = w_qkv.shape[0]
    head_columns = w_qkv.shape[2]
    hidden = w_up.shape[1]
    last = b_up.shape[1]
    rows = row_count // n_y
    half = rows // 2
    tokens = images * rows
    x = lax.axis_index("shard")
    z = lax.axis_index("context")
    y = lax.axis_index("y")
    core = lax.axis_index("core")
    place = jnp.stack([x, z, y, core]).astype(jnp.int32)
    blocks = n_y * n_context
    everyone = ("shard", "context")

    def send(value, axis, step):
        size = {"shard": n_shard, "context": n_context}[axis]
        return lax.ppermute(value, axis, [(i, (i + step) % size) for i in range(size)])

    def across(value):
        return lax.ppermute(value, "y", [(0, 1), (1, 0)])

    def partner(value):
        return lax.ppermute(value, "core", [(0, 1), (1, 0)])

    def hand_over(values, back):
        out = [values[0]]
        for slot in range(1, blocks):
            jy, jz = slot // n_context, slot % n_context
            step = -jz if back else jz
            pairs = [
                (i * n_y + t, (i + step) % n_context * n_y + (t ^ jy))
                for i in range(n_context)
                for t in range(n_y)
            ]
            out.append(lax.ppermute(values[slot], ("context", "y"), pairs))
        return out

    flat_qkv = w_qkv.reshape(piece_rows, -1)
    attention = lax.all_gather(
        jnp.concatenate([flat_qkv, w_out.T], axis=1), everyone, axis=0, tiled=True
    )
    feed = lax.all_gather(
        jnp.concatenate([w_up, w_down.T], axis=1), everyone, axis=0, tiled=True
    )

    vectors = [b_out, b_down, norm1_gain, norm1_bias, norm2_gain, norm2_bias, scale1, scale2]

    def block_of(value):
        return jnp.pad(value, ((0, SMALL_ROWS - value.shape[0]), (0, LANES - value.shape[1])))

    small = jnp.concatenate(
        [block_of(jnp.stack(vectors)), block_of(b_up), block_of(b_qv.reshape(-1, last))], axis=0
    )
    step_rows = piece_rows + 3 * SMALL_ROWS
    quarter_rows = half
    quarter = images * quarter_rows
    block = block_rows(step_rows)
    bundles = call(
        bundle_kernel,
        "bundle",
        [shaped((block, width), bf16)]
        + [shaped((quarter + block, width), bf16)] * (n_context - 1),
        [pltpu.VMEM((n_context, block, width), bf16)],
        place,
        flat_qkv,
        small,
        tokens_in,
    )
    near = [send(bundles[j], "context", j) for j in range(1, n_context)]
    head_stack = jnp.concatenate([bundles[0]] + [value[quarter:] for value in near], axis=0)
    head_stacks = [head_stack] + [send(head_stack, "shard", j) for j in range(1, n_shard)]
    def after(value, *others):
        return lax.optimization_barrier((value, *others))[0]

    weight_head, vec, bias_head, bup = call(
        functools.partial(prepare_kernel, (n_shard, n_context, last, b_qv.shape[1])),
        "prepare",
        [
            shaped((width, 2 * LANES), bf16),
            shaped((SMALL_ROWS, width), f32),
            shaped((8, 2 * LANES), f32),
            shaped((1, hidden), f32),
        ],
        [],
        place,
        *head_stacks,
    )

    quarters = []
    for j, value in enumerate(near):
        value = value[:quarter]
        far = across(value)
        crossed = after(far, weight_head) if j + 1 == n_context // 2 else far
        quarters += [value, far, partner(value), partner(crossed)]
    wout = attention[:, 3 * head_columns :]
    wout_far = across(after(wout, *quarters))
    def own_rows(array):
        return lax.dynamic_slice_in_dim(array, y * rows, rows, 1).reshape(tokens, width)

    residual = own_rows(tokens_in)
    upstream = own_rows(cotangent)

    pack_rows = rows + half
    slot = jnp.arange(blocks)
    source = (z - slot % n_context) % n_context * row_count + (y ^ (slot // n_context)) * rows
    key_place = (source[:, None] + jnp.arange(rows)[None, :]).reshape(1, -1).astype(jnp.int32)
    length = blocks * rows
    pack_spec = pl.BlockSpec((1, pack_rows, LANES), lambda i: (i, 0, 0))
    fold_spec = pl.BlockSpec((1, half, LANES), lambda i: (i, 0, 0))
    pos_spec = pl.BlockSpec((1, length), lambda i: (0, 0))
    log_spec = pl.BlockSpec((1, length, 1), lambda i: (i, 0, 0))
    head_spec = pl.BlockSpec((1, length, LANES), lambda i: (i, 0, 0))
    norm_spec = pl.BlockSpec((1, length, width), lambda i: (i, 0, 0))

    def fixed(shape):
        return pl.BlockSpec(shape, lambda i: (0,) * len(shape))

    attended = pl.pallas_call(
        functools.partial(attend_kernel, n_context),
        name="attend",
        cost_estimate=cost_of("attend"),
        grid=(images,),
        in_specs=[smem(), smem(), pos_spec]
        + [fixed((width, 2 * LANES)), fixed((SMALL_ROWS, width)), fixed((8, 2 * LANES))]
        + [pl.BlockSpec((1, row_count, width), lambda i: (i, 0, 0))]
        + [pl.BlockSpec((quarter_rows, width), lambda i: (i, 0))] * len(quarters),
        out_specs=[fold_spec] * blocks + [log_spec, norm_spec, head_spec, head_spec],
        out_shape=[shaped((images, half, LANES), bf16)] * blocks
        + [
            shaped((images, length, 1), f32),
            shaped((images, length, width), bf16),
            shaped((images, length, LANES), bf16),
            shaped((images, length, LANES), bf16),
        ],
        scratch_shapes=[pltpu.VMEM((length, LANES), bf16), pltpu.VMEM((rows, width), bf16)],
    )(counts, place, key_place, weight_head, vec, bias_head, tokens_in, *quarters)
    mixes, (log_total, norm_all, head_qk, head_v) = attended[:blocks], attended[blocks:]
    folded = hand_over(mixes, True)

    fold_scratch = pltpu.VMEM((blocks, images, half, LANES), bf16)
    mixture, proj_part = call(
        functools.partial(project_kernel, n_context),
        "project",
        [shaped((tokens, blocks * HD), bf16), shaped((tokens, width), bf16)],
        [fold_scratch],
        place,
        *folded,
        wout,
        wout_far,
    )
    proj_other = partner(proj_part)

    core_rows = tokens // CORES
    norm_own, norm_half = call(
        norm_kernel,
        "norm",
        [shaped((tokens, width), bf16), shaped((core_rows, width), bf16)],
        [],
        place,
        residual,
        proj_part,
        proj_other,
        vec,
    )
    norm_near = across(norm_half)
    norm_far = partner(norm_near)
    wqkv = after(attention[:, : 3 * head_columns], norm_near)
    wqkv_far = across(wqkv)
    mlp_rows = n_y * tokens
    (norm_low2, branch_grad, hidden_act, pre_grad, grad_bup, *halves) = call(
        mlp_kernel,
        "mlp",
        [
            shaped((mlp_rows, width), bf16),
            shaped((mlp_rows, width), bf16),
            shaped((mlp_rows, hidden), bf16),
            shaped((mlp_rows, hidden), bf16),
            shaped((1, hidden), f32),
        ]
        + [shaped((tokens, width), bf16)] * 4,
        [pltpu.VMEM((mlp_rows, width), bf16)],
        place,
        norm_own,
        norm_near,
        norm_far,
        cotangent,
        vec,
        bup,
        feed,
    )

    def sum_cores(mine, given):
        return (mine.astype(f32) + partner(given).astype(f32)).astype(bf16)

    def sum_y(both):
        part = both[:core_rows].astype(f32) + across(both[core_rows:]).astype(f32)
        return part.astype(bf16)

    back_both = sum_cores(halves[0], halves[1])
    back_half = sum_y(back_both)
    hidden_act = after(hidden_act, back_both)
    steps = 2
    columns = hidden // steps
    whole_spec = pl.BlockSpec((mlp_rows, width), lambda i, k: (0, 0))
    feed_grad = pl.pallas_call(
        mlp_weights_kernel,
        name="mlp_weights",
        cost_estimate=cost_of("mlp_weights"),
        grid=(2, steps),
        in_specs=[
            whole_spec,
            whole_spec,
            pl.BlockSpec((mlp_rows, columns), lambda i, k: (0, i * k)),
            pl.BlockSpec((mlp_rows, columns), lambda i, k: (0, (1 - i) * k + i * (steps - 1))),
        ],
        out_specs=pl.BlockSpec((width, columns), lambda i, k: (0, i * steps + k)),
        out_shape=shaped((width, 2 * hidden), bf16),
        scratch_shapes=[pltpu.VMEM((width, mlp_rows), bf16)] * 2,
    )(norm_low2, branch_grad, hidden_act, pre_grad)
    back_half, feed_grad = lax.optimization_barrier((back_half, feed_grad))
    back_far = partner(back_half)
    feed_grad = lax.psum_scatter(feed_grad, everyone, scatter_dimension=0, tiled=True)

    back = call(
        functools.partial(back_kernel, images, n_context),
        "back",
        [
            shaped((tokens, width), f32),
            shaped((tokens, width), bf16),
            shaped((SMALL_ROWS, width), f32),
        ]
        + [shaped((images, half, LANES), bf16)] * blocks,
        [fold_scratch, pltpu.VMEM((tokens, width), f32)],
        place,
        residual,
        upstream,
        proj_part,
        proj_other,
        back_half,
        back_far,
        vec,
        wout,
        wout_far,
    )
    middle_grad, proj_grad, sums = back[:3]
    mix_grads = hand_over(back[3:], False)
    out_own, out_far = call(
        out_weights_kernel,
        "out_weights",
        [shaped((width, head_columns), bf16)] * 2,
        [],
        place,
        proj_grad,
        mixture,
    )

    down_half = sum_y(sum_cores(after(halves[2], back_half), halves[3]))
    down_half = after(down_half, proj_grad)
    result, extra = call(
        result_kernel,
        "result",
        [shaped((tokens, width), bf16), shaped((8, width), f32)],
        [pltpu.VMEM((tokens, width), f32)],
        place,
        residual,
        upstream,
        proj_part,
        proj_other,
        down_half,
        partner(down_half),
        vec,
    )

    mix_grads = lax.optimization_barrier((out_own, out_far, result, extra, *mix_grads))
    out_own, out_far, result, extra = mix_grads[:4]
    mix_grads = mix_grads[4:]
    attended_back = pl.pallas_call(
        attend_back_kernel,
        name="attend_back",
        cost_estimate=cost_of("attend_back"),
        grid=(images,),
        in_specs=[smem(), pos_spec, log_spec, norm_spec, head_spec, head_spec]
        + [fold_spec] * (2 * blocks),
        out_specs=[pack_spec] * blocks + [fixed((3 * HD, width)), fixed((8, LANES))],
        out_shape=[shaped((images, pack_rows, LANES), bf16)] * blocks
        + [shaped((3 * HD, width), f32), shaped((8, LANES), f32)],
        scratch_shapes=[
            pltpu.VMEM((length, LANES), bf16),
            pltpu.VMEM((2 * HD, length), f32),
            pltpu.VMEM((length, LANES), f32),
            pltpu.VMEM((3 * HD, length), bf16),
        ],
    )(counts, key_place, log_total, norm_all, head_qk, head_v, *mixes, *mix_grads)
    grad_head, grad_qv = attended_back[blocks:]
    pack_grads = hand_over(attended_back[:blocks], True)

    part_rows = n_context * piece_rows
    def whole_rows(value):
        mine = lax.dynamic_slice_in_dim(value, core * (tokens // 2), tokens // 2, 0)
        near = across(mine)
        far = partner(near)
        half_spec = pl.BlockSpec((tokens // 2, width), lambda i: (0, 0))
        return pl.pallas_call(
            merge_kernel,
            name="merge",
        cost_estimate=cost_of("merge"),
            grid=(images,),
            in_specs=[smem(), pl.BlockSpec((rows, width), lambda i: (i, 0)), half_spec, half_spec],
            out_specs=pl.BlockSpec((1, row_count, width), lambda i: (i, 0, 0)),
            out_shape=shaped((images, row_count, width), f32),
        )(place, value, near, far)

    pack_grads = lax.optimization_barrier(
        (
            feed_grad[:, :hidden].astype(f32),
            feed_grad[:, hidden:].astype(f32).T,
            *pack_grads,
        )
    )
    grad_wup, grad_wdown = pack_grads[:2]
    pack_grads = pack_grads[2:]
    (norm1_part,) = call(
        functools.partial(qkv_back_kernel, n_context),
        "qkv_back",
        [shaped((tokens, width), bf16)],
        [
            pltpu.VMEM((blocks, images, pack_rows, LANES), bf16),
            pltpu.VMEM((n_y, 3, tokens, head_columns), bf16),
        ],
        place,
        *pack_grads,
        wqkv,
        wqkv_far,
    )
    norm1_other = partner(norm1_part)

    input_grad, own, far = call(
        functools.partial(finish_kernel, (n_shard, n_context, last)),
        "finish",
        [shaped((tokens, width), bf16)]
        + [
            shaped((n_shard * n_context * SMALL_ROWS, SMALL_LANES), f32),
            shaped((n_shard * n_context * SMALL_ROWS, LANES), f32),
        ],
        [],
        place,
        residual,
        middle_grad,
        norm1_part,
        norm1_other,
        vec,
        sums,
        extra,
        grad_bup,
        grad_qv,
    )
    far = jnp.pad(across(far), ((0, 0), (0, SMALL_LANES - LANES)))
    total = (own + far).reshape(n_shard, -1, SMALL_LANES)
    over_shard = total[0]
    for j in range(1, n_shard):
        over_shard = over_shard + send(total[j], "shard", -j)
    over_shard = over_shard.reshape(n_context, SMALL_ROWS, SMALL_LANES)
    small_grad = over_shard[0]
    for j in range(1, n_context):
        small_grad = small_grad + send(over_shard[j], "context", -j)

    out_sum = (out_own.astype(f32) + across(out_far).astype(f32)).astype(bf16)
    grad_head, out_sum = lax.optimization_barrier(
        (grad_head, out_sum, norm1_part)
    )[:2]

    def shard_part(j):
        start = lax.rem(x - j + n_shard, n_shard) * part_rows
        head = lax.dynamic_slice_in_dim(grad_head, start, part_rows, 1).astype(bf16)
        rest = lax.dynamic_slice_in_dim(out_sum, start, part_rows, 0)
        wide = part_rows // head_columns
        if wide > 1:
            rest = jnp.concatenate(jnp.split(rest, wide, axis=0), axis=1)
        else:
            rest = jnp.concatenate(jnp.split(rest, head_columns // part_rows, axis=1), axis=0)
        return jnp.concatenate([head, rest], axis=0)

    both = shard_part(0).astype(f32)
    for j in range(1, n_shard):
        both = both + send(shard_part(j), "shard", -j).astype(f32)
    both = after(both.astype(bf16), input_grad)
    head_sum, out_sum = both[: 3 * HD], both[3 * HD :]
    if part_rows > head_columns:
        out_sum = jnp.concatenate(jnp.split(out_sum, part_rows // head_columns, axis=1), axis=0)
    else:
        out_sum = jnp.concatenate(jnp.split(out_sum, head_columns // part_rows, axis=0), axis=1)
    lane_pad = -piece_rows % LANES

    def context_part(j):
        start = lax.rem(z - j + n_context, n_context) * piece_rows
        head = lax.dynamic_slice_in_dim(head_sum, start, piece_rows, 1)
        rest = lax.dynamic_slice_in_dim(out_sum, start, piece_rows, 0)
        rest = jnp.concatenate(jnp.split(rest, head_columns // LANES, axis=1), axis=0)
        return jnp.concatenate([jnp.pad(head, ((0, 0), (0, lane_pad))), rest], axis=0)

    parts = [context_part(0)]
    for j in range(1, n_context):
        parts.append(send(context_part(j), "context", -j))
    grad_wqkv, grad_wout = call(
        head_grads_kernel,
        "head_grads",
        [shaped((piece_rows, 3 * head_columns), f32), shaped((head_columns, piece_rows), f32)],
        [pltpu.VMEM((3 * head_columns, piece_rows + lane_pad), f32)],
        place,
        *parts,
    )
    vec_grad = small_grad[: len(vectors), :piece_rows]
    return (
        whole_rows(result),
        whole_rows(input_grad),
        grad_wqkv.reshape(piece_rows, 3, head_columns),
        small_grad[: b_qv.shape[0] * b_qv.shape[1], 2 * LANES : 2 * LANES + last].reshape(
            b_qv.shape
        ),
        grad_wout,
        vec_grad[B_OUT],
        grad_wup,
        small_grad[: b_up.shape[0], LANES : LANES + last],
        grad_wdown,
        vec_grad[B_DOWN],
        vec_grad[GAIN1],
        vec_grad[SHIFT1],
        vec_grad[GAIN2],
        vec_grad[SHIFT2],
        vec_grad[SCALE1],
        vec_grad[SCALE2],
    )


def solution(mesh):
    pair = ("y", "core")
    both = ("shard", "context")
    tokens = P("shard", "context", None)
    vector = P(both)
    in_specs = (
        tokens,
        P("shard"),
        P(both, None, pair),
        P(None, pair, both),
        P(pair, both),
        vector,
        P(both, pair),
        P(pair, both),
        P(pair, both),
    ) + (vector,) * 7
    in_specs = in_specs + (tokens,)
    out_specs = (
        tokens,
        tokens,
        P(both, None, pair),
        P(None, pair, both),
        P(pair, both),
        vector,
        P(both, pair),
        P(pair, both),
        P(pair, both),
    ) + (vector,) * 7
    sizes = tuple(mesh.shape[name] for name in ("shard", "context", "tensor"))
    split = Mesh(
        mesh.devices.reshape(sizes[0], sizes[1], sizes[2] // CORES, CORES),
        ("shard", "context", "y", "core"),
    )
    return jax.shard_map(
        functools.partial(per_device, split.devices.shape[:3]),
        mesh=split,
        in_specs=in_specs,
        out_specs=out_specs,
        check_vma=False,
    )
```

time: 580 us -> 467 us (0.81)
  starting transfers between devices: 144 us -> 69.8 us
  waiting for transfers between devices: 247 us -> 204 us
    ppermute x28 -> x21, starting transfers between devices: 98.5 us -> 35.8 us  [hand_over(): out.append(lax.ppermute(values[slot], ('context', 'y'), pairs))]
    ppermute x28 -> x21, waiting for transfers between devices: 105 us -> 49.1 us  [hand_over(): out.append(lax.ppermute(values[slot], ('context', 'y'), pairs))]
    ppermute x19 -> x12, waiting for transfers between devices: 67.3 us -> 102 us  [send(): lax.ppermute(value, axis, [(i, (i + step) % size) for i in range(size)])]
    ppermute x9 -> x12, waiting for transfers between devices: 69.4 us -> 42.5 us  [across(): return lax.ppermute(value, 'y', [(0, 1), (1, 0)])]
    ppermute x19 -> x12, starting transfers between devices: 37.4 us -> 18.8 us  [send(): lax.ppermute(value, axis, [(i, (i + step) % size) for i in range(size)])]
    ppermute x9 -> x12, starting transfers between devices: 8.05 us -> 13.7 us  [across(): return lax.ppermute(value, 'y', [(0, 1), (1, 0)])]
    pallas_call x13 -> x16, Pallas kernels: 134 us -> 137 us  [the longest x11 64.5 us: call(): pl.pallas_call(kernel, name=name, cost_estimate=cost_of(name), in_specs=[...]
    unnamed x148 -> x149, local copies, waits for them, and re-layouts: 15.6 us -> 13.6 us
  transfers between devices with their start and end apart: 63 -> 63, of which waited for: 29 -> 24; matrix products, arithmetic and copies ran while one was open for 2% -> 4% of each run, Pallas kernels for 16% -> 24%
where the time goes in v3:
time: 467 us; the launch traced here: 459 us
  waiting for transfers between devices  204 us (44%)
  Pallas kernels  137 us (29%)
  starting transfers between devices  69.8 us (15%)
  local copies, waits for them, and re-layouts  23.8 us (5%)
  between operations  15.2 us (3%)
  other arithmetic  9.2 us (2%)
    ppermute x12, waiting for transfers between devices, send(): lax.ppermute(value, axis, [(i, (i + step) % size) for i in range(size)])  102 us
    pallas_call x11, Pallas kernels, call(): pl.pallas_call(kernel, name=name, cost_estimate=cost_of(name), in_specs=[...  64.5 us
    ppermute x21, waiting for transfers between devices, hand_over(): out.append(lax.ppermute(values[slot], ('context', 'y'), pairs))  49.1 us
    ppermute x12, waiting for transfers between devices, across(): return lax.ppermute(value, 'y', [(0, 1), (1, 0)])  42.5 us
    ppermute x21, starting transfers between devices, hand_over(): out.append(lax.ppermute(values[slot], ('context', 'y'), pairs))  35.8 us
    pallas_call x1, Pallas kernels, per_device(): pl.pallas_call(functools.partial(attend_kernel, n_context), name='attend'...  26.3 us
    pallas_call x1, Pallas kernels, per_device(): pl.pallas_call(attend_back_kernel, name='attend_back', cost_estimate=cost...  26.1 us
    ppermute x12, starting transfers between devices, send(): lax.ppermute(value, axis, [(i, (i + step) % size) for i in range(size)])  18.8 us
  transfers between devices with their start and end apart: 63, of which 24 were waited for; matrix products, arithmetic and copies ran while one was open for 4% of the time, Pallas kernels for 24%

profile of v3, /device:TPU:0, one launch (start us, length us, event | category | flops | bytes accessed | tf_op | source)
XLA Modules:
  0.0 458.7 jit_solution(5781525145132059008)
XLA Ops:
  11.9 3.4 bundle.1
  15.3 5.1 %collective-permute-start.2 = (bf16[336,1024]{1,0:T(8,128)(2,1)}, bf16[336,1024]{1,0:T(8,128)(2,1)S(1)}, u32[]{:S(2)}, u32[]{:S(2)}) collective-permute-start(bf16[336,1024]{1,0:T(8,128)(2,1)} %get-tuple-element.115), channel_id=1, source_target_pairs={{0,12},{4,0},{8,4},{12,8},{1,13},{5,1},{9,5},{13,9},{2,14},{6,2},{... | collective-permute-start | bytes 2064392 | tf_op jit(solution)/shard_map/ppermute | solution.py:693
  22.5 22.5 %collective-permute-done.2 = bf16[336,1024]{1,0:T(8,128)(2,1)S(1)} collective-permute-done((bf16[336,1024]{1,0:T(8,128)(2,1)}, bf16[336,1024]{1,0:T(8,128)(2,1)S(1)}, u32[]{:S(2)}, u32[]{:S(2)}) %collective-permute-start.2) | collective-permute-done | bytes 688160 | tf_op jit(solution)/shard_map/ppermute | solution.py:693
  45.0 1.6 collective-permute-start.10
  46.6 58.1 %collective-permute-done.1 = bf16[336,1024]{1,0:T(8,128)(2,1)S(1)} collective-permute-done((bf16[336,1024]{1,0:T(8,128)(2,1)}, bf16[336,1024]{1,0:T(8,128)(2,1)S(1)}, u32[]{:S(2)}, u32[]{:S(2)}) %collective-permute-start.1) | collective-permute-done | bytes 688160 | tf_op jit(solution)/shard_map/ppermute | solution.py:693
  104.8 1.6 collective-permute-start.7
  107.8 1.6 collective-permute-start.3
  109.4 13.6 %collective-permute-done.3.refs_1_ = bf16[192,1024]{1,0:T(8,128)(2,1)S(1)} collective-permute-done((bf16[192,1024]{1,0:T(8,128)(2,1)S(1)}, bf16[192,1024]{1,0:T(8,128)(2,1)S(1)}, u32[]{:S(2)}, u32[]{:S(2)}) %collective-permute-start.3) | collective-permute-done | bytes 393248 | tf_op jit(solution)/shard_map/ppermute | solution.py:693
  123.7 2.3 prepare.1
  126.6 5.2 %collective-permute-done.4.refs_1_ = bf16[288,1024]{1,0:T(8,128)(2,1)} collective-permute-done((bf16[288,1024]{1,0:T(8,128)(2,1)}, bf16[288,1024]{1,0:T(8,128)(2,1)}, u32[]{:S(2)}, u32[]{:S(2)}) %collective-permute-start.4) | collective-permute-done | bytes 589856 | tf_op jit(solution)/shard_map/ppermute | solution.py:696
  134.9 1.5 collective-permute-start.20
  136.4 26.3 %attend.1 = (bf16[3,96,128]{2,1,0:T(8,128)(2,1)}, bf16[3,96,128]{2,1,0:T(8,128)(2,1)}, bf16[3,96,128]{2,1,0:T(8,128)(2,1)}, bf16[3,96,128]{2,1,0:T(8,128)(2,1)},...) custom-call(s32[3]{0:T(128)} %count_ref.3, ...), custom_call_target="tpu_custom_call" | custom-call | flops 25999998976 | bytes 78000000 | tf_op jit(solution)/shard_map/attend/pallas_call | solution.py:794
  162.9 1.9 collective-permute-start.15
  166.0 5.4 %collective-permute-done.13.refs_1_ = bf16[3,96,128]{2,1,0:T(8,128)(2,1)S(1)} collective-permute-done((bf16[3,96,128]{2,1,0:T(8,128)(2,1)}, bf16[3,96,128]{2,1,0:T(8,128)(2,1)S(1)}, u32[]{:S(2)}, u32[]{:S(2)}) %collective-permute-start.13) | collective-permute-done | bytes 73760 | tf_op jit(solution)/shard_map/ppermute | solution.py:711
  172.1 3.9 collective-permute-done.14.refs_2_
  176.0 7.0 %collective-permute-start.19 = (bf16[3,96,128]{2,1,0:T(8,128)(2,1)}, bf16[3,96,128]{2,1,0:T(8,128)(2,1)S(1)}, u32[]{:S(2)}, u32[]{:S(2)}) collective-permute-start(bf16[3,96,128]{2,1,0:T(8,128)(2,1)} %get-tuple-element.127.refs_7_), channel_id=1, source_target_pairs={{0,6},{2,4},{4,10},{6,8},{8,14},{10,12},{12,2},{14,0},{1,7},{3,5},... | collective-permute-start | bytes 221192 | tf_op jit(solution)/shard_map/ppermute | solution.py:711
  183.0 4.6 %collective-permute-done.18.refs_6_ = bf16[3,96,128]{2,1,0:T(8,128)(2,1)S(1)} collective-permute-done((bf16[3,96,128]{2,1,0:T(8,128)(2,1)}, bf16[3,96,128]{2,1,0:T(8,128)(2,1)S(1)}, u32[]{:S(2)}, u32[]{:S(2)}) %collective-permute-start.18) | collective-permute-done | bytes 73760 | tf_op jit(solution)/shard_map/ppermute | solution.py:711
  189.1 3.7 project.1
  193.9 1.9 collective-permute-done.21.other_ref
  196.9 4.4 norm.1
  202.3 14.6 %collective-permute-done.22.near_ref = bf16[288,1024]{1,0:T(8,128)(2,1)S(1)} collective-permute-done((bf16[288,1024]{1,0:T(8,128)(2,1)}, bf16[288,1024]{1,0:T(8,128)(2,1)S(1)}, u32[]{:S(2)}, u32[]{:S(2)}) %collective-permute-start.22) | collective-permute-done | bytes 589856 | tf_op jit(solution)/shard_map/ppermute | solution.py:696
  216.9 2.0 collective-permute-done.23.far_ref
  219.7 18.7 %mlp.1 = (bf16[1152,1024]{1,0:T(8,128)(2,1)}, bf16[1152,1024]{1,0:T(8,128)(2,1)}, bf16[1152,1024]{1,0:T(8,128)(2,1)}, bf16[1152,1024]{1,0:T(8,128)(2,1)}, f32[1,...) custom-call(s32[4]{0:T(128)} %pad_add_fusion.1.place_ref, ...), custom_call_target="tpu_custom_call" | custom-call | flops 19000000512 | bytes 57000000 | tf_op jit(solution)/shard_map/mlp/pallas_call | solution.py:643
  238.6 2.9 collective-permute-done.24
  241.5 1.7 add_convert_fusion.1
  244.3 11.7 %mlp_weights.1 = bf16[1024,2048]{1,0:T(8,128)(2,1)} custom-call(bf16[1152,1024]{1,0:T(8,128)(2,1)} %get-tuple-element.135.norm_ref, bf16[1152,1024]{1,0:T(8,128)(2,1)} %get-tuple-element.136.grad_ref, bf16[1152,1024]{1,0:T(8,128)(2,1)} %get-tuple-element.138.act_ref, bf16[1152,1024]{1,0:T(8,128)(2,1)} %get-tuple-element.139.pre_ref), custom_call_target="tpu_custom_call" | custom-call | flops 12000000000 | bytes 36000000 | tf_op jit(solution)/shard_map/mlp_weights/pallas_call | solution.py:881
  256.0 2.7 collective-permute-done.25
  259.0 1.4 copy-done.30
  260.4 2.8 collective-permute-done.27
  266.0 13.2 %collective-permute-done.28 = bf16[288,1024]{1,0:T(8,128)(2,1)S(1)} collective-permute-done((bf16[288,1024]{1,0:T(8,128)(2,1)S(1)}, bf16[288,1024]{1,0:T(8,128)(2,1)S(1)}, u32[]{:S(2)}, u32[]{:S(2)}) %collective-permute-start.28) | collective-permute-done | bytes 589856 | tf_op jit(solution)/shard_map/ppermute | solution.py:696
  280.3 8.3 %back.1 = (f32[576,1024]{1,0:T(8,128)}, bf16[576,1024]{1,0:T(8,128)(2,1)}, f32[16,1024]{1,0:T(8,128)}, bf16[3,96,128]{2,1,0:T(8,128)(2,1)}, bf16[3,96,128]{2,1,0...) custom-call(s32[4]{0:T(128)} %pad_add_fusion.1.place_ref, ...), custom_call_target="tpu_custom_call" | custom-call | flops 8000000000 | bytes 24000000 | tf_op jit(solution)/shard_map/back/pallas_call | solution.py:643
  290.3 2.8 collective-permute-start.31
  293.2 3.5 out_weights.1
  296.7 2.0 collective-permute-start.32
  300.9 2.5 collective-permute-done.31.refs_10_
  304.6 6.7 %collective-permute-start.36 = (bf16[3,96,128]{2,1,0:T(8,128)(2,1)S(1)}, bf16[3,96,128]{2,1,0:T(8,128)(2,1)S(1)}, u32[]{:S(2)}, u32[]{:S(2)}) collective-permute-start(bf16[3,96,128]{2,1,0:T(8,128)(2,1)S(1)} %copy-done.52), channel_id=1, source_target_pairs={{0,14},{2,12},{4,2},{6,0},{8,6},{10,4},{12,10},{14,8},{1,15},{3,13... | collective-permute-start | bytes 221192 | tf_op jit(solution)/shard_map/ppermute | solution.py:711
  311.3 5.6 %result.1 = (bf16[576,1024]{1,0:T(8,128)(2,1)}, f32[8,1024]{1,0:T(8,128)}) custom-call(s32[4]{0:T(128)} %pad_add_fusion.1.place_ref, bf16[576,1024]{1,0:T(8,128)(2,1)} %bitcast.41, bf16[576,1024]{1,0:T(8,128)(2,1)} %bitcast.44, bf16[576,1024]{1,0:T(8,128)(2,1)} %get-tuple-element.129.part_ref, bf16[576,1024]{1,0:T(8,128)(2,1)} %copy-done.29, ...), custom_call_target="tpu_custom_call" | custom-call | flops 6000000000 | bytes 18000000 | tf_op jit(solution)/shard_map/result/pallas_call | solution.py:643
  317.8 26.1 %attend_back.1 = (bf16[3,288,128]{2,1,0:T(8,128)(2,1)}, bf16[3,288,128]{2,1,0:T(8,128)(2,1)}, bf16[3,288,128]{2,1,0:T(8,128)(2,1)}, bf16[3,288,128]{2,1,0:T(8,12...) custom-call(s32[3]{0:T(128)} %count_ref.3, ...), custom_call_target="tpu_custom_call" | custom-call | flops 25999998976 | bytes 78000000 | tf_op jit(solution)/shard_map/attend_back/pallas_call | solution.py:953
  343.8 1.4 collective-permute-start.39
  347.2 2.4 collective-permute-start.40
  350.5 6.7 %collective-permute-done.39.refs_1_ = bf16[3,288,128]{2,1,0:T(8,128)(2,1)S(1)} collective-permute-done((bf16[3,288,128]{2,1,0:T(8,128)(2,1)}, bf16[3,288,128]{2,1,0:T(8,128)(2,1)S(1)}, u32[]{:S(2)}, u32[]{:S(2)}) %collective-permute-start.39) | collective-permute-done | bytes 221216 | tf_op jit(solution)/shard_map/ppermute | solution.py:711
  357.2 1.5 collective-permute-start.42
  358.7 13.7 %collective-permute-done.40.refs_2_ = bf16[3,288,128]{2,1,0:T(8,128)(2,1)S(1)} collective-permute-done((bf16[3,288,128]{2,1,0:T(8,128)(2,1)}, bf16[3,288,128]{2,1,0:T(8,128)(2,1)S(1)}, u32[]{:S(2)}, u32[]{:S(2)}) %collective-permute-start.40) | collective-permute-done | bytes 221216 | tf_op jit(solution)/shard_map/ppermute | solution.py:711
  372.4 1.4 collective-permute-start.44
  373.8 2.3 collective-permute-start.45
  376.1 1.9 convert_bitcast_fusion
  378.0 3.7 collective-permute-done.43.refs_5_
  381.7 2.3 collective-permute-start.50
  384.0 8.6 %collective-permute-done.44.refs_6_ = bf16[3,288,128]{2,1,0:T(8,128)(2,1)} collective-permute-done((bf16[3,288,128]{2,1,0:T(8,128)(2,1)}, bf16[3,288,128]{2,1,0:T(8,128)(2,1)}, u32[]{:S(2)}, u32[]{:S(2)}) %collective-permute-start.44) | collective-permute-done | bytes 221216 | tf_op jit(solution)/shard_map/ppermute | solution.py:711
  392.6 6.3 %qkv_back.1.part_ref = bf16[576,1024]{1,0:T(8,128)(2,1)} custom-call(s32[4]{0:T(128)} %pad_add_fusion.1.place_ref, bf16[3,288,128]{2,1,0:T(8,128)(2,1)} %get-tuple-element.182.refs_0_, bf16[3,288,128]{2,1,0:T(8,128)(2,1)} %copy-done.43, bf16[3,288,128]{2,1,0:T(8,128)(2,1)} %copy-done.45, bf16[3,288,128]{2,1,0:T(8,128)(2,1)} %copy-done.46, ...), custom_call_target="tpu_custom_call" | custom-call | flops 6000000000 | bytes 18000000 | tf_op jit(solution)/shard_map/qkv_back/pallas_call | solution.py:643
  398.9 4.1 collective-permute-done.50
  403.3 1.5 collective-permute-start.51
  404.8 4.1 merge.2
  409.9 5.3 %collective-permute-done.51 = bf16[448,512]{1,0:T(8,128)(2,1)S(1)} collective-permute-done((bf16[448,512]{1,0:T(8,128)(2,1)S(1)}, bf16[448,512]{1,0:T(8,128)(2,1)S(1)}, u32[]{:S(2)}, u32[]{:S(2)}) %collective-permute-start.51) | collective-permute-done | bytes 458784 | tf_op jit(solution)/shard_map/ppermute | solution.py:693
  415.3 6.1 %finish.1 = (bf16[576,1024]{1,0:T(8,128)(2,1)}, f32[128,384]{1,0:T(8,128)}, f32[128,128]{1,0:T(8,128)}) custom-call(s32[4]{0:T(128)} %pad_add_fusion.1.place_ref, bf16[576,1024]{1,0:T(8,128)(2,1)} %bitcast.42, f32[576,1024]{1,0:T(8,128)} %get-tuple-element.160.middle_grad_ref, bf16[576,1024]{1,0:T(8,128)(2,1)} %qkv_back.1.part_ref, ...), custom_call_target="tpu_custom_call" | custom-call | flops 6000000000 | bytes 18000000 | tf_op jit(solution)/shard_map/finish/pallas_call | solution.py:643
  424.3 2.6 collective-permute-start.52
  427.0 1.6 collective-permute-start.48
  428.6 1.5 collective-permute-start.56
  430.7 2.5 collective-permute-done.56
  433.9 1.5 collective-permute-start.58
  435.5 1.9 collective-permute-start.59
  437.4 2.7 collective-permute-done.48.near_ref
  440.8 2.1 head_grads.1
  447.7 4.1 merge.3
  (283 shorter events, 44.7 us)
Async XLA Ops:
  7.3 125.8 %all-gather.3.cloned.1.call-start = ((), (), s32[]{:S(2)}) async-start(), calls=%async_computation.1 | async-start | bytes 2359296 | tf_op jit(solution)/shard_map/all_gather | solution.py:715
  10.4 208.5 %all-gather.5.cloned.1.call-start = ((), (), s32[]{:S(2)}) async-start(), calls=%async_computation.2 | async-start | bytes 4718592 | tf_op jit(solution)/shard_map/all_gather | solution.py:718
  15.3 29.6 %collective-permute-start.2 = (bf16[336,1024]{1,0:T(8,128)(2,1)}, bf16[336,1024]{1,0:T(8,128)(2,1)S(1)}, u32[]{:S(2)}, u32[]{:S(2)}) collective-permute-start(bf16[336,1024]{1,0:T(8,128)(2,1)} %get-tuple-element.115), channel_id=1, source_target_pairs={{0,12},{4,0},{8,4},{12,8},{1,13},{5,1},{9,5},{13,9},{2,14},{6,2},{... | collective-permute-start | bytes 2064392 | tf_op jit(solution)/shard_map/ppermute | solution.py:693
  20.4 84.3 %collective-permute-start.1 = (bf16[336,1024]{1,0:T(8,128)(2,1)}, bf16[336,1024]{1,0:T(8,128)(2,1)S(1)}, u32[]{:S(2)}, u32[]{:S(2)}) collective-permute-start(bf16[336,1024]{1,0:T(8,128)(2,1)} %get-tuple-element.114), channel_id=1, source_target_pairs={{0,8},{4,12},{8,0},{12,4},{1,9},{5,13},{9,1},{13,5},{2,10},{6,14},... | collective-permute-start | bytes 2064392 | tf_op jit(solution)/shard_map/ppermute | solution.py:693
  20.4 86.0 %collective-permute-start = (bf16[336,1024]{1,0:T(8,128)(2,1)}, bf16[336,1024]{1,0:T(8,128)(2,1)S(1)}, u32[]{:S(2)}, u32[]{:S(2)}) collective-permute-start(bf16[336,1024]{1,0:T(8,128)(2,1)} %get-tuple-element.113), channel_id=1, source_target_pairs={{0,4},{4,8},{8,12},{12,0},{1,5},{5,9},{9,13},{13,1},{2,6},{6,10},{... | collective-permute-start | bytes 2064392 | tf_op jit(solution)/shard_map/ppermute | solution.py:693
  22.5 353.6 %reduce-scatter.2.cloned.1.call-start = ((), (), s32[]{:S(2)}) async-start(), calls=%async_computation.3 | async-start | bytes 4718592 | tf_op jit(solution)/shard_map/reduce_scatter | solution.py:898
  45.0 62.2 %copy-start.8 = (bf16[288,1024]{1,0:T(8,128)(2,1)}, bf16[288,1024]{1,0:T(8,128)(2,1)S(1)}, u32[]{:S(2)}) copy-start(bf16[288,1024]{1,0:T(8,128)(2,1)S(1)} %slice.147.refs_8_) | copy-start | bytes 1769476
  45.0 81.1 %collective-permute-start.10 = (bf16[288,1024]{1,0:T(8,128)(2,1)S(1)}, bf16[288,1024]{1,0:T(8,128)(2,1)}, u32[]{:S(2)}, u32[]{:S(2)}) collective-permute-start(bf16[288,1024]{1,0:T(8,128)(2,1)S(1)} %slice.147.refs_8_), channel_id=1, source_target_pairs={{0,2},{2,0},{1,3},{3,1},{4,6},{6,4},{5,7},{7,5},{8,10},{10,8},{9,1... | collective-permute-start | bytes 1769480 | tf_op jit(solution)/shard_map/ppermute | solution.py:696
  46.6 85.2 %collective-permute-start.11 = (bf16[288,1024]{1,0:T(8,128)(2,1)S(1)}, bf16[288,1024]{1,0:T(8,128)(2,1)}, u32[]{:S(2)}, u32[]{:S(2)}) collective-permute-start(bf16[288,1024]{1,0:T(8,128)(2,1)S(1)} %slice.147.refs_8_), channel_id=1, source_target_pairs={{0,1},{1,0},{2,3},{3,2},{4,5},{5,4},{6,7},{7,6},{8,9},{9,8},{10,11... | collective-permute-start | bytes 1769480 | tf_op jit(solution)/shard_map/ppermute | solution.py:699
  104.8 21.2 %collective-permute-start.7 = (bf16[288,1024]{1,0:T(8,128)(2,1)S(1)}, bf16[288,1024]{1,0:T(8,128)(2,1)}, u32[]{:S(2)}, u32[]{:S(2)}) collective-permute-start(bf16[288,1024]{1,0:T(8,128)(2,1)S(1)} %slice.146.refs_4_), channel_id=1, source_target_pairs={{0,2},{2,0},{1,3},{3,1},{4,6},{6,4},{5,7},{7,5},{8,10},{10,8},{9,1... | collective-permute-start | bytes 1769480 | tf_op jit(solution)/shard_map/ppermute | solution.py:696
  107.2 24.6 %collective-permute-start.4 = (bf16[288,1024]{1,0:T(8,128)(2,1)}, bf16[288,1024]{1,0:T(8,128)(2,1)}, u32[]{:S(2)}, u32[]{:S(2)}) collective-permute-start(bf16[288,1024]{1,0:T(8,128)(2,1)} %slice.145.refs_0_), channel_id=1, source_target_pairs={{0,2},{2,0},{1,3},{3,1},{4,6},{6,4},{5,7},{7,5},{8,10},{10,8},{9,1... | collective-permute-start | bytes 1769480 | tf_op jit(solution)/shard_map/ppermute | solution.py:696
  107.8 15.1 %collective-permute-start.3 = (bf16[192,1024]{1,0:T(8,128)(2,1)S(1)}, bf16[192,1024]{1,0:T(8,128)(2,1)S(1)}, u32[]{:S(2)}, u32[]{:S(2)}) collective-permute-start(bf16[192,1024]{1,0:T(8,128)(2,1)S(1)} %pad_maximum_fusion.1.refs_0_), channel_id=1, source_target_pairs={{0,16},{16,0},{1,17},{17,1},{2,18},{18,2},{3,19},{19,3},{4,20},{20... | collective-permute-start | bytes 1179656 | tf_op jit(solution)/shard_map/ppermute | solution.py:693
  123.0 11.2 %collective-permute-start.5 = (bf16[288,1024]{1,0:T(8,128)(2,1)}, bf16[288,1024]{1,0:T(8,128)(2,1)S(1)}, u32[]{:S(2)}, u32[]{:S(2)}) collective-permute-start(bf16[288,1024]{1,0:T(8,128)(2,1)} %slice.145.refs_0_), channel_id=1, source_target_pairs={{0,1},{1,0},{2,3},{3,2},{4,5},{5,4},{6,7},{7,6},{8,9},{9,8},{10,11... | collective-permute-start | bytes 1769480 | tf_op jit(solution)/shard_map/ppermute | solution.py:699
  126.0 8.2 %collective-permute-start.8 = (bf16[288,1024]{1,0:T(8,128)(2,1)S(1)}, bf16[288,1024]{1,0:T(8,128)(2,1)S(1)}, u32[]{:S(2)}, u32[]{:S(2)}) collective-permute-start(bf16[288,1024]{1,0:T(8,128)(2,1)S(1)} %slice.146.refs_4_), channel_id=1, source_target_pairs={{0,1},{1,0},{2,3},{3,2},{4,5},{5,4},{6,7},{7,6},{8,9},{9,8},{10,11... | collective-permute-start | bytes 1769480 | tf_op jit(solution)/shard_map/ppermute | solution.py:699
  126.1 8.1 %collective-permute-start.9 = (bf16[288,1024]{1,0:T(8,128)(2,1)}, bf16[288,1024]{1,0:T(8,128)(2,1)}, u32[]{:S(2)}, u32[]{:S(2)}) collective-permute-start(bf16[288,1024]{1,0:T(8,128)(2,1)} %collective-permute-done.7.refs_5_), channel_id=1, source_target_pairs={{0,1},{1,0},{2,3},{3,2},{4,5},{5,4},{6,7},{7,6},{8,9},{9,8},{10,11... | collective-permute-start | bytes 1769480 | tf_op jit(solution)/shard_map/ppermute | solution.py:699
  131.8 2.4 collective-permute-start.12
  131.8 3.1 collective-permute-start.6
  134.9 52.8 %collective-permute-start.20 = (bf16[1024,256]{1,0:T(8,128)(2,1)S(1)}, bf16[1024,256]{1,0:T(8,128)(2,1)S(1)}, u32[]{:S(2)}, u32[]{:S(2)}) collective-permute-start(bf16[1024,256]{1,0:T(8,128)(2,1)S(1)} %slice.148.refs_8_.own_ref), channel_id=1, source_target_pairs={{0,2},{2,0},{1,3},{3,1},{4,6},{6,4},{5,7},{7,5},{8,10},{10,8},{9,1... | collective-permute-start | bytes 1572872 | tf_op jit(solution)/shard_map/ppermute | solution.py:696
  162.7 8.7 %collective-permute-start.13 = (bf16[3,96,128]{2,1,0:T(8,128)(2,1)}, bf16[3,96,128]{2,1,0:T(8,128)(2,1)S(1)}, u32[]{:S(2)}, u32[]{:S(2)}) collective-permute-start(bf16[3,96,128]{2,1,0:T(8,128)(2,1)} %get-tuple-element.121.refs_1_), channel_id=1, source_target_pairs={{0,12},{2,14},{4,0},{6,2},{8,4},{10,6},{12,8},{14,10},{1,13},{3,15... | collective-permute-start | bytes 221192 | tf_op jit(solution)/shard_map/ppermute | solution.py:711
  162.8 13.2 %collective-permute-start.14 = (bf16[3,96,128]{2,1,0:T(8,128)(2,1)}, bf16[3,96,128]{2,1,0:T(8,128)(2,1)S(1)}, u32[]{:S(2)}, u32[]{:S(2)}) collective-permute-start(bf16[3,96,128]{2,1,0:T(8,128)(2,1)} %get-tuple-element.122.refs_2_), channel_id=1, source_target_pairs={{0,8},{2,10},{4,12},{6,14},{8,0},{10,2},{12,4},{14,6},{1,9},{3,11}... | collective-permute-start | bytes 221192 | tf_op jit(solution)/shard_map/ppermute | solution.py:711
  162.9 13.1 %collective-permute-start.15 = (bf16[3,96,128]{2,1,0:T(8,128)(2,1)}, bf16[3,96,128]{2,1,0:T(8,128)(2,1)S(1)}, u32[]{:S(2)}, u32[]{:S(2)}) collective-permute-start(bf16[3,96,128]{2,1,0:T(8,128)(2,1)} %get-tuple-element.123.refs_3_), channel_id=1, source_target_pairs={{0,4},{2,6},{4,8},{6,10},{8,12},{10,14},{12,0},{14,2},{1,5},{3,7},... | collective-permute-start | bytes 221192 | tf_op jit(solution)/shard_map/ppermute | solution.py:711
  164.8 18.2 %collective-permute-start.16 = (bf16[3,96,128]{2,1,0:T(8,128)(2,1)}, bf16[3,96,128]{2,1,0:T(8,128)(2,1)S(1)}, u32[]{:S(2)}, u32[]{:S(2)}) collective-permute-start(bf16[3,96,128]{2,1,0:T(8,128)(2,1)} %get-tuple-element.124.refs_4_), channel_id=1, source_target_pairs={{0,2},{2,0},{4,6},{6,4},{8,10},{10,8},{12,14},{14,12},{1,3},{3,1},... | collective-permute-start | bytes 221192 | tf_op jit(solution)/shard_map/ppermute | solution.py:711
  171.4 11.6 %collective-permute-start.17 = (bf16[3,96,128]{2,1,0:T(8,128)(2,1)}, bf16[3,96,128]{2,1,0:T(8,128)(2,1)S(1)}, u32[]{:S(2)}, u32[]{:S(2)}) collective-permute-start(bf16[3,96,128]{2,1,0:T(8,128)(2,1)} %get-tuple-element.125.refs_5_), channel_id=1, source_target_pairs={{0,14},{2,12},{4,2},{6,0},{8,6},{10,4},{12,10},{14,8},{1,15},{3,13... | collective-permute-start | bytes 221192 | tf_op jit(solution)/shard_map/ppermute | solution.py:711
  176.0 11.7 %collective-permute-start.18 = (bf16[3,96,128]{2,1,0:T(8,128)(2,1)}, bf16[3,96,128]{2,1,0:T(8,128)(2,1)S(1)}, u32[]{:S(2)}, u32[]{:S(2)}) collective-permute-start(bf16[3,96,128]{2,1,0:T(8,128)(2,1)} %get-tuple-element.126.refs_6_), channel_id=1, source_target_pairs={{0,10},{2,8},{4,14},{6,12},{8,2},{10,0},{12,6},{14,4},{1,11},{3,9}... | collective-permute-start | bytes 221192 | tf_op jit(solution)/shard_map/ppermute | solution.py:711
  176.0 11.7 %collective-permute-start.19 = (bf16[3,96,128]{2,1,0:T(8,128)(2,1)}, bf16[3,96,128]{2,1,0:T(8,128)(2,1)S(1)}, u32[]{:S(2)}, u32[]{:S(2)}) collective-permute-start(bf16[3,96,128]{2,1,0:T(8,128)(2,1)} %get-tuple-element.127.refs_7_), channel_id=1, source_target_pairs={{0,6},{2,4},{4,10},{6,8},{8,14},{10,12},{12,2},{14,0},{1,7},{3,5},... | collective-permute-start | bytes 221192 | tf_op jit(solution)/shard_map/ppermute | solution.py:711
  192.8 3.1 collective-permute-start.21
  201.3 15.6 %collective-permute-start.22 = (bf16[288,1024]{1,0:T(8,128)(2,1)}, bf16[288,1024]{1,0:T(8,128)(2,1)S(1)}, u32[]{:S(2)}, u32[]{:S(2)}) collective-permute-start(bf16[288,1024]{1,0:T(8,128)(2,1)} %get-tuple-element.131), channel_id=1, source_target_pairs={{0,2},{2,0},{1,3},{3,1},{4,6},{6,4},{5,7},{7,5},{8,10},{10,8},{9,1... | collective-permute-start | bytes 1769480 | tf_op jit(solution)/shard_map/ppermute | solution.py:696
  216.9 2.0 collective-permute-start.23
  238.4 3.1 collective-permute-start.24
  243.3 15.4 %collective-permute-start.25 = (bf16[288,1024]{1,0:T(8,128)(2,1)S(1)}, bf16[288,1024]{1,0:T(8,128)(2,1)S(1)}, u32[]{:S(2)}, u32[]{:S(2)}) collective-permute-start(bf16[288,1024]{1,0:T(8,128)(2,1)S(1)} %slice.150), channel_id=1, source_target_pairs={{0,2},{2,0},{1,3},{3,1},{4,6},{6,4},{5,7},{7,5},{8,10},{10,8},{9,1... | collective-permute-start | bytes 1769480 | tf_op jit(solution)/shard_map/ppermute | solution.py:696
  260.4 2.8 collective-permute-start.27
  263.8 15.4 %collective-permute-start.28 = (bf16[288,1024]{1,0:T(8,128)(2,1)S(1)}, bf16[288,1024]{1,0:T(8,128)(2,1)S(1)}, u32[]{:S(2)}, u32[]{:S(2)}) collective-permute-start(bf16[288,1024]{1,0:T(8,128)(2,1)S(1)} %slice.152), channel_id=1, source_target_pairs={{0,2},{2,0},{1,3},{3,1},{4,6},{6,4},{5,7},{7,5},{8,10},{10,8},{9,1... | collective-permute-start | bytes 1769480 | tf_op jit(solution)/shard_map/ppermute | solution.py:696
  264.8 14.6 %collective-permute-start.26 = (bf16[288,1024]{1,0:T(8,128)(2,1)S(1)}, bf16[288,1024]{1,0:T(8,128)(2,1)S(1)}, u32[]{:S(2)}, u32[]{:S(2)}) collective-permute-start(bf16[288,1024]{1,0:T(8,128)(2,1)S(1)} %add_convert_fusion.3.near_ref), channel_id=1, source_target_pairs={{0,1},{1,0},{2,3},{3,2},{4,5},{5,4},{6,7},{7,6},{8,9},{9,8},{10,11... | collective-permute-start | bytes 1769480 | tf_op jit(solution)/shard_map/ppermute | solution.py:699
  288.7 15.9 %collective-permute-start.29 = (bf16[288,1024]{1,0:T(8,128)(2,1)S(1)}, bf16[288,1024]{1,0:T(8,128)(2,1)S(1)}, u32[]{:S(2)}, u32[]{:S(2)}) collective-permute-start(bf16[288,1024]{1,0:T(8,128)(2,1)S(1)} %add_convert_fusion.2.near_ref), channel_id=1, source_target_pairs={{0,1},{1,0},{2,3},{3,2},{4,5},{5,4},{6,7},{7,6},{8,9},{9,8},{10,11... | collective-permute-start | bytes 1769480 | tf_op jit(solution)/shard_map/ppermute | solution.py:699
  290.1 10.0 %collective-permute-start.30 = (bf16[3,96,128]{2,1,0:T(8,128)(2,1)S(1)}, bf16[3,96,128]{2,1,0:T(8,128)(2,1)S(1)}, u32[]{:S(2)}, u32[]{:S(2)}) collective-permute-start(bf16[3,96,128]{2,1,0:T(8,128)(2,1)S(1)} %copy-done.63), channel_id=1, source_target_pairs={{0,4},{2,6},{4,8},{6,10},{8,12},{10,14},{12,0},{14,2},{1,5},{3,7},... | collective-permute-start | bytes 221192 | tf_op jit(solution)/shard_map/ppermute | solution.py:711
  290.3 13.1 %collective-permute-start.31 = (bf16[3,96,128]{2,1,0:T(8,128)(2,1)S(1)}, bf16[3,96,128]{2,1,0:T(8,128)(2,1)S(1)}, u32[]{:S(2)}, u32[]{:S(2)}) collective-permute-start(bf16[3,96,128]{2,1,0:T(8,128)(2,1)S(1)} %copy-done.62), channel_id=1, source_target_pairs={{0,8},{2,10},{4,12},{6,14},{8,0},{10,2},{12,4},{14,6},{1,9},{3,11}... | collective-permute-start | bytes 221192 | tf_op jit(solution)/shard_map/ppermute | solution.py:711
  296.7 20.2 %collective-permute-start.32 = (bf16[3,96,128]{2,1,0:T(8,128)(2,1)S(1)}, bf16[3,96,128]{2,1,0:T(8,128)(2,1)S(1)}, u32[]{:S(2)}, u32[]{:S(2)}) collective-permute-start(bf16[3,96,128]{2,1,0:T(8,128)(2,1)S(1)} %copy-done.58), channel_id=1, source_target_pairs={{0,12},{2,14},{4,0},{6,2},{8,4},{10,6},{12,8},{14,10},{1,13},{3,15... | collective-permute-start | bytes 221192 | tf_op jit(solution)/shard_map/ppermute | solution.py:711
  298.7 18.3 %collective-permute-start.33 = (bf16[3,96,128]{2,1,0:T(8,128)(2,1)S(1)}, bf16[3,96,128]{2,1,0:T(8,128)(2,1)S(1)}, u32[]{:S(2)}, u32[]{:S(2)}) collective-permute-start(bf16[3,96,128]{2,1,0:T(8,128)(2,1)S(1)} %copy-done.56), channel_id=1, source_target_pairs={{0,2},{2,0},{4,6},{6,4},{8,10},{10,8},{12,14},{14,12},{1,3},{3,1},... | collective-permute-start | bytes 221192 | tf_op jit(solution)/shard_map/ppermute | solution.py:711
  300.0 17.0 %collective-permute-start.34 = (bf16[3,96,128]{2,1,0:T(8,128)(2,1)S(1)}, bf16[3,96,128]{2,1,0:T(8,128)(2,1)S(1)}, u32[]{:S(2)}, u32[]{:S(2)}) collective-permute-start(bf16[3,96,128]{2,1,0:T(8,128)(2,1)S(1)} %copy-done.54), channel_id=1, source_target_pairs={{0,6},{2,4},{4,10},{6,8},{8,14},{10,12},{12,2},{14,0},{1,7},{3,5},... | collective-permute-start | bytes 221192 | tf_op jit(solution)/shard_map/ppermute | solution.py:711
  303.4 13.6 %collective-permute-start.35 = (bf16[3,96,128]{2,1,0:T(8,128)(2,1)S(1)}, bf16[3,96,128]{2,1,0:T(8,128)(2,1)S(1)}, u32[]{:S(2)}, u32[]{:S(2)}) collective-permute-start(bf16[3,96,128]{2,1,0:T(8,128)(2,1)S(1)} %copy-done.53), channel_id=1, source_target_pairs={{0,10},{2,8},{4,14},{6,12},{8,2},{10,0},{12,6},{14,4},{1,11},{3,9}... | collective-permute-start | bytes 221192 | tf_op jit(solution)/shard_map/ppermute | solution.py:711
  304.6 12.5 %collective-permute-start.36 = (bf16[3,96,128]{2,1,0:T(8,128)(2,1)S(1)}, bf16[3,96,128]{2,1,0:T(8,128)(2,1)S(1)}, u32[]{:S(2)}, u32[]{:S(2)}) collective-permute-start(bf16[3,96,128]{2,1,0:T(8,128)(2,1)S(1)} %copy-done.52), channel_id=1, source_target_pairs={{0,14},{2,12},{4,2},{6,0},{8,6},{10,4},{12,10},{14,8},{1,15},{3,13... | collective-permute-start | bytes 221192 | tf_op jit(solution)/shard_map/ppermute | solution.py:711
  316.9 75.7 %collective-permute-start.46 = (bf16[1024,768]{1,0:T(8,128)(2,1)S(1)}, bf16[1024,768]{1,0:T(8,128)(2,1)}, u32[]{:S(2)}, u32[]{:S(2)}) collective-permute-start(bf16[1024,768]{1,0:T(8,128)(2,1)S(1)} %copy-done.1), channel_id=1, source_target_pairs={{0,2},{2,0},{1,3},{3,1},{4,6},{6,4},{5,7},{7,5},{8,10},{10,8},{9,1... | collective-permute-start | bytes 4718600 | tf_op jit(solution)/shard_map/ppermute | solution.py:696
  343.8 13.4 %collective-permute-start.39 = (bf16[3,288,128]{2,1,0:T(8,128)(2,1)}, bf16[3,288,128]{2,1,0:T(8,128)(2,1)S(1)}, u32[]{:S(2)}, u32[]{:S(2)}) collective-permute-start(bf16[3,288,128]{2,1,0:T(8,128)(2,1)} %get-tuple-element.175), channel_id=1, source_target_pairs={{0,12},{2,14},{4,0},{6,2},{8,4},{10,6},{12,8},{14,10},{1,13},{3,15... | collective-permute-start | bytes 663560 | tf_op jit(solution)/shard_map/ppermute | solution.py:711
  346.3 37.7 %collective-permute-start.37 = (bf16[288,1024]{1,0:T(8,128)(2,1)S(1)}, bf16[288,1024]{1,0:T(8,128)(2,1)}, u32[]{:S(2)}, u32[]{:S(2)}) collective-permute-start(bf16[288,1024]{1,0:T(8,128)(2,1)S(1)} %constant_dynamic-slice_fusion.9), channel_id=1, source_target_pairs={{0,2},{2,0},{1,3},{3,1},{4,6},{6,4},{5,7},{7,5},{8,10},{10,8},{9,1... | collective-permute-start | bytes 1769480 | tf_op jit(solution)/shard_map/ppermute | solution.py:696
  347.2 25.1 %collective-permute-start.40 = (bf16[3,288,128]{2,1,0:T(8,128)(2,1)}, bf16[3,288,128]{2,1,0:T(8,128)(2,1)S(1)}, u32[]{:S(2)}, u32[]{:S(2)}) collective-permute-start(bf16[3,288,128]{2,1,0:T(8,128)(2,1)} %get-tuple-element.176), channel_id=1, source_target_pairs={{0,8},{2,10},{4,12},{6,14},{8,0},{10,2},{12,4},{14,6},{1,9},{3,11}... | collective-permute-start | bytes 663560 | tf_op jit(solution)/shard_map/ppermute | solution.py:711
  349.7 22.7 %collective-permute-start.41 = (bf16[3,288,128]{2,1,0:T(8,128)(2,1)}, bf16[3,288,128]{2,1,0:T(8,128)(2,1)S(1)}, u32[]{:S(2)}, u32[]{:S(2)}) collective-permute-start(bf16[3,288,128]{2,1,0:T(8,128)(2,1)} %get-tuple-element.177), channel_id=1, source_target_pairs={{0,4},{2,6},{4,8},{6,10},{8,12},{10,14},{12,0},{14,2},{1,5},{3,7},... | collective-permute-start | bytes 663560 | tf_op jit(solution)/shard_map/ppermute | solution.py:711
  357.2 16.6 %collective-permute-start.42 = (bf16[3,288,128]{2,1,0:T(8,128)(2,1)}, bf16[3,288,128]{2,1,0:T(8,128)(2,1)}, u32[]{:S(2)}, u32[]{:S(2)}) collective-permute-start(bf16[3,288,128]{2,1,0:T(8,128)(2,1)} %get-tuple-element.178), channel_id=1, source_target_pairs={{0,2},{2,0},{4,6},{6,4},{8,10},{10,8},{12,14},{14,12},{1,3},{3,1},... | collective-permute-start | bytes 663560 | tf_op jit(solution)/shard_map/ppermute | solution.py:711
  372.4 9.3 %collective-permute-start.43 = (bf16[3,288,128]{2,1,0:T(8,128)(2,1)S(1)}, bf16[3,288,128]{2,1,0:T(8,128)(2,1)}, u32[]{:S(2)}, u32[]{:S(2)}) collective-permute-start(bf16[3,288,128]{2,1,0:T(8,128)(2,1)S(1)} %copy-done.44), channel_id=1, source_target_pairs={{0,14},{2,12},{4,2},{6,0},{8,6},{10,4},{12,10},{14,8},{1,15},{3,13... | collective-permute-start | bytes 663560 | tf_op jit(solution)/shard_map/ppermute | solution.py:711
  372.4 20.2 %collective-permute-start.44 = (bf16[3,288,128]{2,1,0:T(8,128)(2,1)}, bf16[3,288,128]{2,1,0:T(8,128)(2,1)}, u32[]{:S(2)}, u32[]{:S(2)}) collective-permute-start(bf16[3,288,128]{2,1,0:T(8,128)(2,1)} %get-tuple-element.180), channel_id=1, source_target_pairs={{0,10},{2,8},{4,14},{6,12},{8,2},{10,0},{12,6},{14,4},{1,11},{3,9}... | collective-permute-start | bytes 663560 | tf_op jit(solution)/shard_map/ppermute | solution.py:711
  373.8 18.8 %collective-permute-start.45 = (bf16[3,288,128]{2,1,0:T(8,128)(2,1)S(1)}, bf16[3,288,128]{2,1,0:T(8,128)(2,1)}, u32[]{:S(2)}, u32[]{:S(2)}) collective-permute-start(bf16[3,288,128]{2,1,0:T(8,128)(2,1)S(1)} %copy-done.42), channel_id=1, source_target_pairs={{0,6},{2,4},{4,10},{6,8},{8,14},{10,12},{12,2},{14,0},{1,7},{3,5},... | collective-permute-start | bytes 663560 | tf_op jit(solution)/shard_map/ppermute | solution.py:711
  381.7 21.3 %collective-permute-start.50 = (bf16[1024,256]{1,0:T(8,128)(2,1)}, bf16[1024,256]{1,0:T(8,128)(2,1)S(1)}, u32[]{:S(2)}, u32[]{:S(2)}) collective-permute-start(bf16[1024,256]{1,0:T(8,128)(2,1)} %get-tuple-element.198), channel_id=1, source_target_pairs={{0,2},{2,0},{1,3},{3,1},{4,6},{6,4},{5,7},{7,5},{8,10},{10,8},{9,1... | collective-permute-start | bytes 1572872 | tf_op jit(solution)/shard_map/ppermute | solution.py:696
  384.0 20.8 %collective-permute-start.38 = (bf16[288,1024]{1,0:T(8,128)(2,1)}, bf16[288,1024]{1,0:T(8,128)(2,1)}, u32[]{:S(2)}, u32[]{:S(2)}) collective-permute-start(bf16[288,1024]{1,0:T(8,128)(2,1)} %collective-permute-done.37.near_ref), channel_id=1, source_target_pairs={{0,1},{1,0},{2,3},{3,2},{4,5},{5,4},{6,7},{7,6},{8,9},{9,8},{10,11... | collective-permute-start | bytes 1769480 | tf_op jit(solution)/shard_map/ppermute | solution.py:699
  398.9 16.4 %collective-permute-start.47 = (bf16[576,1024]{1,0:T(8,128)(2,1)}, bf16[576,1024]{1,0:T(8,128)(2,1)}, u32[]{:S(2)}, u32[]{:S(2)}) collective-permute-start(bf16[576,1024]{1,0:T(8,128)(2,1)} %qkv_back.1.part_ref), channel_id=1, source_target_pairs={{0,1},{1,0},{2,3},{3,2},{4,5},{5,4},{6,7},{7,6},{8,9},{9,8},{10,11... | collective-permute-start | bytes 3538952 | tf_op jit(solution)/shard_map/ppermute | solution.py:699
  403.3 11.9 %collective-permute-start.51 = (bf16[448,512]{1,0:T(8,128)(2,1)S(1)}, bf16[448,512]{1,0:T(8,128)(2,1)S(1)}, u32[]{:S(2)}, u32[]{:S(2)}) collective-permute-start(bf16[448,512]{1,0:T(8,128)(2,1)S(1)} %maximum_maximum_fusion), channel_id=1, source_target_pairs={{0,16},{16,0},{1,17},{17,1},{2,18},{18,2},{3,19},{19,3},{4,20},{20... | collective-permute-start | bytes 1376264 | tf_op jit(solution)/shard_map/ppermute | solution.py:693
  421.5 7.1 %collective-permute-start.55 = (f32[128,128]{1,0:T(8,128)}, f32[128,128]{1,0:T(8,128)S(1)}, u32[]{:S(2)}, u32[]{:S(2)}) collective-permute-start(f32[128,128]{1,0:T(8,128)} %get-tuple-element.204), channel_id=1, source_target_pairs={{0,2},{2,0},{1,3},{3,1},{4,6},{6,4},{5,7},{7,5},{8,10},{10,8},{9,1... | collective-permute-start | bytes 196616 | tf_op jit(solution)/shard_map/ppermute | solution.py:696
  422.9 11.1 %collective-permute-start.54 = (bf16[448,128]{1,0:T(8,128)(2,1)S(1)}, bf16[448,128]{1,0:T(8,128)(2,1)S(1)}, u32[]{:S(2)}, u32[]{:S(2)}) collective-permute-start(bf16[448,128]{1,0:T(8,128)(2,1)S(1)} %pad_maximum_fusion.6), channel_id=1, source_target_pairs={{0,4},{4,8},{8,12},{12,0},{1,5},{5,9},{9,13},{13,1},{2,6},{6,10},{... | collective-permute-start | bytes 344072 | tf_op jit(solution)/shard_map/ppermute | solution.py:693
  422.9 12.5 %collective-permute-start.53 = (bf16[448,128]{1,0:T(8,128)(2,1)S(1)}, bf16[448,128]{1,0:T(8,128)(2,1)S(1)}, u32[]{:S(2)}, u32[]{:S(2)}) collective-permute-start(bf16[448,128]{1,0:T(8,128)(2,1)S(1)} %pad_maximum_fusion.5), channel_id=1, source_target_pairs={{0,8},{4,12},{8,0},{12,4},{1,9},{5,13},{9,1},{13,5},{2,10},{6,14},... | collective-permute-start | bytes 344072 | tf_op jit(solution)/shard_map/ppermute | solution.py:693
  424.3 15.8 %collective-permute-start.52 = (bf16[448,128]{1,0:T(8,128)(2,1)S(1)}, bf16[448,128]{1,0:T(8,128)(2,1)S(1)}, u32[]{:S(2)}, u32[]{:S(2)}) collective-permute-start(bf16[448,128]{1,0:T(8,128)(2,1)S(1)} %pad_maximum_fusion.4), channel_id=1, source_target_pairs={{0,12},{4,0},{8,4},{12,8},{1,13},{5,1},{9,5},{13,9},{2,14},{6,2},{... | collective-permute-start | bytes 344072 | tf_op jit(solution)/shard_map/ppermute | solution.py:693
  427.0 13.1 %collective-permute-start.48 = (bf16[288,1024]{1,0:T(8,128)(2,1)S(1)}, bf16[288,1024]{1,0:T(8,128)(2,1)S(1)}, u32[]{:S(2)}, u32[]{:S(2)}) collective-permute-start(bf16[288,1024]{1,0:T(8,128)(2,1)S(1)} %constant_dynamic-slice_fusion.8), channel_id=1, source_target_pairs={{0,2},{2,0},{1,3},{3,1},{4,6},{6,4},{5,7},{7,5},{8,10},{10,8},{9,1... | collective-permute-start | bytes 1769480 | tf_op jit(solution)/shard_map/ppermute | solution.py:696
  428.6 4.7 %collective-permute-start.56 = (f32[64,384]{1,0:T(8,128)S(1)}, f32[64,384]{1,0:T(8,128)S(1)}, u32[]{:S(2)}, u32[]{:S(2)}) collective-permute-start(f32[64,384]{1,0:T(8,128)S(1)} %slice.157), channel_id=1, source_target_pairs={{0,16},{16,0},{1,17},{17,1},{2,18},{18,2},{3,19},{19,3},{4,20},{20... | collective-permute-start | bytes 294920 | tf_op jit(solution)/shard_map/ppermute | solution.py:693
  433.3 11.7 %collective-permute-start.57 = (f32[16,384]{1,0:T(8,128)S(1)}, f32[16,384]{1,0:T(8,128)S(1)}, u32[]{:S(2)}, u32[]{:S(2)}) collective-permute-start(f32[16,384]{1,0:T(8,128)S(1)} %get-tuple-element.258), channel_id=1, source_target_pairs={{0,12},{4,0},{8,4},{12,8},{1,13},{5,1},{9,5},{13,9},{2,14},{6,2},{... | collective-permute-start | bytes 73736 | tf_op jit(solution)/shard_map/ppermute | solution.py:693
  433.9 11.1 %collective-permute-start.58 = (f32[16,384]{1,0:T(8,128)S(1)}, f32[16,384]{1,0:T(8,128)S(1)}, u32[]{:S(2)}, u32[]{:S(2)}) collective-permute-start(f32[16,384]{1,0:T(8,128)S(1)} %get-tuple-element.260), channel_id=1, source_target_pairs={{0,8},{4,12},{8,0},{12,4},{1,9},{5,13},{9,1},{13,5},{2,10},{6,14},... | collective-permute-start | bytes 73736 | tf_op jit(solution)/shard_map/ppermute | solution.py:693
  435.5 9.5 %collective-permute-start.59 = (f32[16,384]{1,0:T(8,128)S(1)}, f32[16,384]{1,0:T(8,128)S(1)}, u32[]{:S(2)}, u32[]{:S(2)}) collective-permute-start(f32[16,384]{1,0:T(8,128)S(1)} %get-tuple-element.259), channel_id=1, source_target_pairs={{0,4},{4,8},{8,12},{12,0},{1,5},{5,9},{9,13},{13,1},{2,6},{6,10},{... | collective-permute-start | bytes 73736 | tf_op jit(solution)/shard_map/ppermute | solution.py:693
  440.1 6.7 %collective-permute-start.49 = (bf16[288,1024]{1,0:T(8,128)(2,1)S(1)}, bf16[288,1024]{1,0:T(8,128)(2,1)S(1)}, u32[]{:S(2)}, u32[]{:S(2)}) collective-permute-start(bf16[288,1024]{1,0:T(8,128)(2,1)S(1)} %collective-permute-done.48.near_ref), channel_id=1, source_target_pairs={{0,1},{1,0},{2,3},{3,2},{4,5},{5,4},{6,7},{7,6},{8,9},{9,8},{10,11... | collective-permute-start | bytes 1769480 | tf_op jit(solution)/shard_map/ppermute | solution.py:699
  (70 other events, 443.2 us)
Sparse Core Ops, SparseCore 0:
  10.5 89.3 all-gather.2
  102.0 85.5 all-gather.4
  259.1 98.2 reduce-scatter.1

commit v4 on v3

--- a/solution.py
+++ b/solution.py
@@ -762,10 +762,15 @@
         *head_stacks,
     )
 
+    fars = {}
+    for j in sorted(range(n_context - 1), key=lambda j: min(j, n_context - 2 - j)):
+        value = near[j][:quarter]
+        if min(j, n_context - 2 - j):
+            value = after(value, *fars.values())
+        fars[j] = across(value)
     quarters = []
     for j, value in enumerate(near):
-        value = value[:quarter]
-        far = across(value)
+        value, far = value[:quarter], fars[j]
         crossed = after(far, weight_head) if j + 1 == n_context // 2 else far
         quarters += [value, far, partner(value), partner(crossed)]
     wout = attention[:, 3 * head_columns :]

time: 467 us -> 466 us (level)
  waiting for transfers between devices: 204 us -> 198 us
    unnamed x149 -> x145, local copies, waits for them, and re-layouts: 13.6 us -> 15 us
  transfers between devices with their start and end apart: 63 -> 63, of which waited for: 24 -> 25; matrix products, arithmetic and copies ran while one was open for 4% -> 4% of each run, Pallas kernels for 24% -> 24%
where the time goes in v4:
time: 466 us; the launch traced here: 458 us
  waiting for transfers between devices  198 us (42%)
  Pallas kernels  137 us (29%)
  starting transfers between devices  73.3 us (16%)
  local copies, waits for them, and re-layouts  24.5 us (5%)
  between operations  15.2 us (3%)
  other arithmetic  10 us (2%)
    ppermute x12, waiting for transfers between devices, send(): lax.ppermute(value, axis, [(i, (i + step) % size) for i in range(size)])  99.8 us
    pallas_call x11, Pallas kernels, call(): pl.pallas_call(kernel, name=name, cost_estimate=cost_of(name), in_specs=[...  64.5 us
    ppermute x21, waiting for transfers between devices, hand_over(): out.append(lax.ppermute(values[slot], ('context', 'y'), pairs))  48.3 us
    ppermute x12, waiting for transfers between devices, across(): return lax.ppermute(value, 'y', [(0, 1), (1, 0)])  38.3 us
    ppermute x21, starting transfers between devices, hand_over(): out.append(lax.ppermute(values[slot], ('context', 'y'), pairs))  38 us
    pallas_call x1, Pallas kernels, per_device(): pl.pallas_call(functools.partial(attend_kernel, n_context), name='attend'...  26.2 us
    pallas_call x1, Pallas kernels, per_device(): pl.pallas_call(attend_back_kernel, name='attend_back', cost_estimate=cost...  26.1 us
    ppermute x12, starting transfers between devices, send(): lax.ppermute(value, axis, [(i, (i + step) % size) for i in range(size)])  18.7 us
  transfers between devices with their start and end apart: 63, of which 25 were waited for; matrix products, arithmetic and copies ran while one was open for 4% of the time, Pallas kernels for 24%

profile of v4, /device:TPU:0, one launch (start us, length us, event | category | flops | bytes accessed | tf_op | source)
XLA Modules:
  0.0 457.5 jit_solution(11779468214038663592)
XLA Ops:
  11.8 3.4 bundle.1
  15.2 3.1 collective-permute-start
  18.2 2.0 collective-permute-start.2
  21.3 23.9 %collective-permute-done = bf16[336,1024]{1,0:T(8,128)(2,1)S(1)} collective-permute-done((bf16[336,1024]{1,0:T(8,128)(2,1)}, bf16[336,1024]{1,0:T(8,128)(2,1)S(1)}, u32[]{:S(2)}, u32[]{:S(2)}) %collective-permute-start) | collective-permute-done | bytes 688160 | tf_op jit(solution)/shard_map/ppermute | solution.py:693
  45.3 1.8 collective-permute-start.4
  47.1 16.0 %collective-permute-done.2 = bf16[336,1024]{1,0:T(8,128)(2,1)S(1)} collective-permute-done((bf16[336,1024]{1,0:T(8,128)(2,1)}, bf16[336,1024]{1,0:T(8,128)(2,1)S(1)}, u32[]{:S(2)}, u32[]{:S(2)}) %collective-permute-start.2) | collective-permute-done | bytes 688160 | tf_op jit(solution)/shard_map/ppermute | solution.py:693
  63.1 1.7 collective-permute-start.7
  65.9 1.8 pad_maximum_fusion
  67.9 37.5 %collective-permute-done.1 = bf16[336,1024]{1,0:T(8,128)(2,1)S(1)} collective-permute-done((bf16[336,1024]{1,0:T(8,128)(2,1)}, bf16[336,1024]{1,0:T(8,128)(2,1)S(1)}, u32[]{:S(2)}, u32[]{:S(2)}) %collective-permute-start.1) | collective-permute-done | bytes 688160 | tf_op jit(solution)/shard_map/ppermute | solution.py:693
  105.5 1.6 collective-permute-start.8
  107.1 1.6 collective-permute-start.3
  109.2 14.4 %collective-permute-done.3.refs_1_ = bf16[192,1024]{1,0:T(8,128)(2,1)S(1)} collective-permute-done((bf16[192,1024]{1,0:T(8,128)(2,1)S(1)}, bf16[192,1024]{1,0:T(8,128)(2,1)S(1)}, u32[]{:S(2)}, u32[]{:S(2)}) %collective-permute-start.3) | collective-permute-done | bytes 393248 | tf_op jit(solution)/shard_map/ppermute | solution.py:693
  124.3 2.3 prepare.1
  131.2 26.2 %attend.1 = (bf16[3,96,128]{2,1,0:T(8,128)(2,1)}, bf16[3,96,128]{2,1,0:T(8,128)(2,1)}, bf16[3,96,128]{2,1,0:T(8,128)(2,1)}, bf16[3,96,128]{2,1,0:T(8,128)(2,1)},...) custom-call(s32[3]{0:T(128)} %count_ref.3, ...), custom_call_target="tpu_custom_call" | custom-call | flops 25999998976 | bytes 78000000 | tf_op jit(solution)/shard_map/attend/pallas_call | solution.py:799
  157.7 1.9 collective-permute-start.15
  159.5 1.5 collective-permute-start.16
  162.4 4.0 collective-permute-start.17
  166.3 3.7 collective-permute-done.14.refs_2_
  170.4 7.5 %collective-permute-start.19 = (bf16[3,96,128]{2,1,0:T(8,128)(2,1)}, bf16[3,96,128]{2,1,0:T(8,128)(2,1)S(1)}, u32[]{:S(2)}, u32[]{:S(2)}) collective-permute-start(bf16[3,96,128]{2,1,0:T(8,128)(2,1)} %get-tuple-element.129.refs_7_), channel_id=1, source_target_pairs={{0,6},{2,4},{4,10},{6,8},{8,14},{10,12},{12,2},{14,0},{1,7},{3,5},... | collective-permute-start | bytes 221192 | tf_op jit(solution)/shard_map/ppermute | solution.py:711
  177.9 6.8 %collective-permute-done.18.refs_6_ = bf16[3,96,128]{2,1,0:T(8,128)(2,1)S(1)} collective-permute-done((bf16[3,96,128]{2,1,0:T(8,128)(2,1)}, bf16[3,96,128]{2,1,0:T(8,128)(2,1)S(1)}, u32[]{:S(2)}, u32[]{:S(2)}) %collective-permute-start.18) | collective-permute-done | bytes 73760 | tf_op jit(solution)/shard_map/ppermute | solution.py:711
  186.1 3.7 project.1
  190.9 1.9 collective-permute-done.21.other_ref
  193.9 4.4 norm.1
  198.8 15.0 %collective-permute-done.22.near_ref = bf16[288,1024]{1,0:T(8,128)(2,1)S(1)} collective-permute-done((bf16[288,1024]{1,0:T(8,128)(2,1)}, bf16[288,1024]{1,0:T(8,128)(2,1)S(1)}, u32[]{:S(2)}, u32[]{:S(2)}) %collective-permute-start.22) | collective-permute-done | bytes 589856 | tf_op jit(solution)/shard_map/ppermute | solution.py:696
  213.9 2.0 collective-permute-done.23.far_ref
  216.7 18.7 %mlp.1 = (bf16[1152,1024]{1,0:T(8,128)(2,1)}, bf16[1152,1024]{1,0:T(8,128)(2,1)}, bf16[1152,1024]{1,0:T(8,128)(2,1)}, bf16[1152,1024]{1,0:T(8,128)(2,1)}, f32[1,...) custom-call(s32[4]{0:T(128)} %pad_add_fusion.1.place_ref, ...), custom_call_target="tpu_custom_call" | custom-call | flops 19000000512 | bytes 57000000 | tf_op jit(solution)/shard_map/mlp/pallas_call | solution.py:643
  235.5 2.9 collective-permute-done.24
  238.5 1.7 add_convert_fusion.1
  240.8 11.7 %mlp_weights.1 = bf16[1024,2048]{1,0:T(8,128)(2,1)} custom-call(bf16[1152,1024]{1,0:T(8,128)(2,1)} %get-tuple-element.137.norm_ref, bf16[1152,1024]{1,0:T(8,128)(2,1)} %get-tuple-element.138.grad_ref, bf16[1152,1024]{1,0:T(8,128)(2,1)} %get-tuple-element.140.act_ref, bf16[1152,1024]{1,0:T(8,128)(2,1)} %get-tuple-element.141.pre_ref), custom_call_target="tpu_custom_call" | custom-call | flops 12000000000 | bytes 36000000 | tf_op jit(solution)/shard_map/mlp_weights/pallas_call | solution.py:886
  252.5 3.2 collective-permute-done.25
  257.4 2.8 collective-permute-done.27
  263.0 13.2 %collective-permute-done.28 = bf16[288,1024]{1,0:T(8,128)(2,1)S(1)} collective-permute-done((bf16[288,1024]{1,0:T(8,128)(2,1)S(1)}, bf16[288,1024]{1,0:T(8,128)(2,1)S(1)}, u32[]{:S(2)}, u32[]{:S(2)}) %collective-permute-start.28) | collective-permute-done | bytes 589856 | tf_op jit(solution)/shard_map/ppermute | solution.py:696
  277.3 8.3 %back.1 = (f32[576,1024]{1,0:T(8,128)}, bf16[576,1024]{1,0:T(8,128)(2,1)}, f32[16,1024]{1,0:T(8,128)}, bf16[3,96,128]{2,1,0:T(8,128)(2,1)}, bf16[3,96,128]{2,1,0...) custom-call(s32[4]{0:T(128)} %pad_add_fusion.1.place_ref, ...), custom_call_target="tpu_custom_call" | custom-call | flops 8000000000 | bytes 24000000 | tf_op jit(solution)/shard_map/back/pallas_call | solution.py:643
  287.2 3.3 collective-permute-start.31
  290.5 3.5 out_weights.1
  294.1 1.5 collective-permute-start.32
  297.6 3.1 collective-permute-done.31.refs_10_
  300.8 6.2 %collective-permute-start.36 = (bf16[3,96,128]{2,1,0:T(8,128)(2,1)S(1)}, bf16[3,96,128]{2,1,0:T(8,128)(2,1)S(1)}, u32[]{:S(2)}, u32[]{:S(2)}) collective-permute-start(bf16[3,96,128]{2,1,0:T(8,128)(2,1)S(1)} %copy-done.52), channel_id=1, source_target_pairs={{0,14},{2,12},{4,2},{6,0},{8,6},{10,4},{12,10},{14,8},{1,15},{3,13... | collective-permute-start | bytes 221192 | tf_op jit(solution)/shard_map/ppermute | solution.py:711
  307.0 5.7 %result.1 = (bf16[576,1024]{1,0:T(8,128)(2,1)}, f32[8,1024]{1,0:T(8,128)}) custom-call(s32[4]{0:T(128)} %pad_add_fusion.1.place_ref, bf16[576,1024]{1,0:T(8,128)(2,1)} %bitcast.41, bf16[576,1024]{1,0:T(8,128)(2,1)} %bitcast.44, bf16[576,1024]{1,0:T(8,128)(2,1)} %get-tuple-element.131.part_ref, bf16[576,1024]{1,0:T(8,128)(2,1)} %copy-done.30, ...), custom_call_target="tpu_custom_call" | custom-call | flops 6000000000 | bytes 18000000 | tf_op jit(solution)/shard_map/result/pallas_call | solution.py:643
  312.7 1.8 collective-permute-start.46
  315.2 26.1 %attend_back.1 = (bf16[3,288,128]{2,1,0:T(8,128)(2,1)}, bf16[3,288,128]{2,1,0:T(8,128)(2,1)}, bf16[3,288,128]{2,1,0:T(8,128)(2,1)}, bf16[3,288,128]{2,1,0:T(8,12...) custom-call(s32[3]{0:T(128)} %count_ref.3, ...), custom_call_target="tpu_custom_call" | custom-call | flops 25999998976 | bytes 78000000 | tf_op jit(solution)/shard_map/attend_back/pallas_call | solution.py:958
  343.8 2.3 collective-permute-start.40
  346.1 1.9 collective-permute-start.41
  348.0 7.6 %collective-permute-done.39.refs_1_ = bf16[3,288,128]{2,1,0:T(8,128)(2,1)S(1)} collective-permute-done((bf16[3,288,128]{2,1,0:T(8,128)(2,1)}, bf16[3,288,128]{2,1,0:T(8,128)(2,1)S(1)}, u32[]{:S(2)}, u32[]{:S(2)}) %collective-permute-start.39) | collective-permute-done | bytes 221216 | tf_op jit(solution)/shard_map/ppermute | solution.py:711
  357.0 13.7 %collective-permute-done.40.refs_2_ = bf16[3,288,128]{2,1,0:T(8,128)(2,1)S(1)} collective-permute-done((bf16[3,288,128]{2,1,0:T(8,128)(2,1)}, bf16[3,288,128]{2,1,0:T(8,128)(2,1)S(1)}, u32[]{:S(2)}, u32[]{:S(2)}) %collective-permute-start.40) | collective-permute-done | bytes 221216 | tf_op jit(solution)/shard_map/ppermute | solution.py:711
  372.1 2.3 collective-permute-start.45
  374.5 1.9 convert_bitcast_fusion
  376.4 3.6 collective-permute-done.43.refs_5_
  380.0 2.6 collective-permute-start.50
  382.6 8.5 %collective-permute-done.44.refs_6_ = bf16[3,288,128]{2,1,0:T(8,128)(2,1)} collective-permute-done((bf16[3,288,128]{2,1,0:T(8,128)(2,1)}, bf16[3,288,128]{2,1,0:T(8,128)(2,1)}, u32[]{:S(2)}, u32[]{:S(2)}) %collective-permute-start.44) | collective-permute-done | bytes 221216 | tf_op jit(solution)/shard_map/ppermute | solution.py:711
  391.1 6.3 %qkv_back.1.part_ref = bf16[576,1024]{1,0:T(8,128)(2,1)} custom-call(s32[4]{0:T(128)} %pad_add_fusion.1.place_ref, bf16[3,288,128]{2,1,0:T(8,128)(2,1)} %get-tuple-element.184.refs_0_, bf16[3,288,128]{2,1,0:T(8,128)(2,1)} %copy-done.43, bf16[3,288,128]{2,1,0:T(8,128)(2,1)} %copy-done.45, bf16[3,288,128]{2,1,0:T(8,128)(2,1)} %copy-done.46, ...), custom_call_target="tpu_custom_call" | custom-call | flops 6000000000 | bytes 18000000 | tf_op jit(solution)/shard_map/qkv_back/pallas_call | solution.py:643
  397.4 4.3 collective-permute-done.50
  402.0 1.5 collective-permute-start.51
  403.5 4.1 merge.2
  408.6 5.4 %collective-permute-done.51 = bf16[448,512]{1,0:T(8,128)(2,1)S(1)} collective-permute-done((bf16[448,512]{1,0:T(8,128)(2,1)S(1)}, bf16[448,512]{1,0:T(8,128)(2,1)S(1)}, u32[]{:S(2)}, u32[]{:S(2)}) %collective-permute-start.51) | collective-permute-done | bytes 458784 | tf_op jit(solution)/shard_map/ppermute | solution.py:693
  414.2 6.1 %finish.1 = (bf16[576,1024]{1,0:T(8,128)(2,1)}, f32[128,384]{1,0:T(8,128)}, f32[128,128]{1,0:T(8,128)}) custom-call(s32[4]{0:T(128)} %pad_add_fusion.1.place_ref, bf16[576,1024]{1,0:T(8,128)(2,1)} %bitcast.42, f32[576,1024]{1,0:T(8,128)} %get-tuple-element.162.middle_grad_ref, bf16[576,1024]{1,0:T(8,128)(2,1)} %qkv_back.1.part_ref, ...), custom_call_target="tpu_custom_call" | custom-call | flops 6000000000 | bytes 18000000 | tf_op jit(solution)/shard_map/finish/pallas_call | solution.py:643
  422.7 2.9 collective-permute-start.52
  425.7 1.7 collective-permute-start.48
  429.6 2.5 collective-permute-done.56
  432.8 1.5 collective-permute-start.58
  434.3 1.9 collective-permute-start.59
  436.3 2.6 collective-permute-done.48.near_ref
  439.6 2.1 head_grads.1
  446.4 4.1 merge.3
  (281 shorter events, 47.4 us)
Async XLA Ops:
  7.3 120.7 %all-gather.3.cloned.1.call-start = ((), (), s32[]{:S(2)}) async-start(), calls=%async_computation.1 | async-start | bytes 2359296 | tf_op jit(solution)/shard_map/all_gather | solution.py:715
  10.4 205.5 %all-gather.5.cloned.1.call-start = ((), (), s32[]{:S(2)}) async-start(), calls=%async_computation.2 | async-start | bytes 4718592 | tf_op jit(solution)/shard_map/all_gather | solution.py:718
  15.2 30.0 %collective-permute-start = (bf16[336,1024]{1,0:T(8,128)(2,1)}, bf16[336,1024]{1,0:T(8,128)(2,1)S(1)}, u32[]{:S(2)}, u32[]{:S(2)}) collective-permute-start(bf16[336,1024]{1,0:T(8,128)(2,1)} %get-tuple-element.114), channel_id=1, source_target_pairs={{0,4},{4,8},{8,12},{12,0},{1,5},{5,9},{9,13},{13,1},{2,6},{6,10},{... | collective-permute-start | bytes 2064392 | tf_op jit(solution)/shard_map/ppermute | solution.py:693
  18.2 44.8 %collective-permute-start.2 = (bf16[336,1024]{1,0:T(8,128)(2,1)}, bf16[336,1024]{1,0:T(8,128)(2,1)S(1)}, u32[]{:S(2)}, u32[]{:S(2)}) collective-permute-start(bf16[336,1024]{1,0:T(8,128)(2,1)} %get-tuple-element.116), channel_id=1, source_target_pairs={{0,12},{4,0},{8,4},{12,8},{1,13},{5,1},{9,5},{13,9},{2,14},{6,2},{... | collective-permute-start | bytes 2064392 | tf_op jit(solution)/shard_map/ppermute | solution.py:693
  20.3 85.2 %collective-permute-start.1 = (bf16[336,1024]{1,0:T(8,128)(2,1)}, bf16[336,1024]{1,0:T(8,128)(2,1)S(1)}, u32[]{:S(2)}, u32[]{:S(2)}) collective-permute-start(bf16[336,1024]{1,0:T(8,128)(2,1)} %get-tuple-element.115), channel_id=1, source_target_pairs={{0,8},{4,12},{8,0},{12,4},{1,9},{5,13},{9,1},{13,5},{2,10},{6,14},... | collective-permute-start | bytes 2064392 | tf_op jit(solution)/shard_map/ppermute | solution.py:693
  45.3 63.4 %copy-start.10 = (bf16[288,1024]{1,0:T(8,128)(2,1)}, bf16[288,1024]{1,0:T(8,128)(2,1)S(1)}, u32[]{:S(2)}) copy-start(bf16[288,1024]{1,0:T(8,128)(2,1)S(1)} %slice.148.refs_0_) | copy-start | bytes 1769476
  45.3 60.2 %collective-permute-start.4 = (bf16[288,1024]{1,0:T(8,128)(2,1)S(1)}, bf16[288,1024]{1,0:T(8,128)(2,1)}, u32[]{:S(2)}, u32[]{:S(2)}) collective-permute-start(bf16[288,1024]{1,0:T(8,128)(2,1)S(1)} %slice.148.refs_0_), channel_id=1, source_target_pairs={{0,2},{2,0},{1,3},{3,1},{4,6},{6,4},{5,7},{7,5},{8,10},{10,8},{9,1... | collective-permute-start | bytes 1769480 | tf_op jit(solution)/shard_map/ppermute | solution.py:696
  63.1 42.4 %collective-permute-start.7 = (bf16[288,1024]{1,0:T(8,128)(2,1)S(1)}, bf16[288,1024]{1,0:T(8,128)(2,1)}, u32[]{:S(2)}, u32[]{:S(2)}) collective-permute-start(bf16[288,1024]{1,0:T(8,128)(2,1)S(1)} %slice.150.refs_8_), channel_id=1, source_target_pairs={{0,2},{2,0},{1,3},{3,1},{4,6},{6,4},{5,7},{7,5},{8,10},{10,8},{9,1... | collective-permute-start | bytes 1769480 | tf_op jit(solution)/shard_map/ppermute | solution.py:696
  67.7 306.8 %reduce-scatter.2.cloned.1.call-start = ((), (), s32[]{:S(2)}) async-start(), calls=%async_computation.3 | async-start | bytes 4718592 | tf_op jit(solution)/shard_map/reduce_scatter | solution.py:903
  67.7 59.4 %collective-permute-start.11 = (bf16[288,1024]{1,0:T(8,128)(2,1)S(1)}, bf16[288,1024]{1,0:T(8,128)(2,1)}, u32[]{:S(2)}, u32[]{:S(2)}) collective-permute-start(bf16[288,1024]{1,0:T(8,128)(2,1)S(1)} %slice.150.refs_8_), channel_id=1, source_target_pairs={{0,1},{1,0},{2,3},{3,2},{4,5},{5,4},{6,7},{7,6},{8,9},{9,8},{10,11... | collective-permute-start | bytes 1769480 | tf_op jit(solution)/shard_map/ppermute | solution.py:699
  105.5 21.2 %collective-permute-start.8 = (bf16[288,1024]{1,0:T(8,128)(2,1)S(1)}, bf16[288,1024]{1,0:T(8,128)(2,1)S(1)}, u32[]{:S(2)}, u32[]{:S(2)}) collective-permute-start(bf16[288,1024]{1,0:T(8,128)(2,1)S(1)} %slice.149.refs_4_), channel_id=1, source_target_pairs={{0,2},{2,0},{1,3},{3,1},{4,6},{6,4},{5,7},{7,5},{8,10},{10,8},{9,1... | collective-permute-start | bytes 1769480 | tf_op jit(solution)/shard_map/ppermute | solution.py:696
  107.1 16.4 %collective-permute-start.3 = (bf16[192,1024]{1,0:T(8,128)(2,1)S(1)}, bf16[192,1024]{1,0:T(8,128)(2,1)S(1)}, u32[]{:S(2)}, u32[]{:S(2)}) collective-permute-start(bf16[192,1024]{1,0:T(8,128)(2,1)S(1)} %pad_maximum_fusion.1.refs_0_), channel_id=1, source_target_pairs={{0,16},{16,0},{1,17},{17,1},{2,18},{18,2},{3,19},{19,3},{4,20},{20... | collective-permute-start | bytes 1179656 | tf_op jit(solution)/shard_map/ppermute | solution.py:693
  108.7 20.4 %collective-permute-start.5 = (bf16[288,1024]{1,0:T(8,128)(2,1)S(1)}, bf16[288,1024]{1,0:T(8,128)(2,1)}, u32[]{:S(2)}, u32[]{:S(2)}) collective-permute-start(bf16[288,1024]{1,0:T(8,128)(2,1)S(1)} %slice.148.refs_0_), channel_id=1, source_target_pairs={{0,1},{1,0},{2,3},{3,2},{4,5},{5,4},{6,7},{7,6},{8,9},{9,8},{10,11... | collective-permute-start | bytes 1769480 | tf_op jit(solution)/shard_map/ppermute | solution.py:699
  108.7 20.4 %collective-permute-start.9 = (bf16[288,1024]{1,0:T(8,128)(2,1)S(1)}, bf16[288,1024]{1,0:T(8,128)(2,1)}, u32[]{:S(2)}, u32[]{:S(2)}) collective-permute-start(bf16[288,1024]{1,0:T(8,128)(2,1)S(1)} %slice.149.refs_4_), channel_id=1, source_target_pairs={{0,1},{1,0},{2,3},{3,2},{4,5},{5,4},{6,7},{7,6},{8,9},{9,8},{10,11... | collective-permute-start | bytes 1769480 | tf_op jit(solution)/shard_map/ppermute | solution.py:699
  126.6 2.5 collective-permute-start.12
  126.7 3.2 collective-permute-start.6
  127.2 3.5 collective-permute-start.10
  130.7 54.0 %collective-permute-start.20 = (bf16[1024,256]{1,0:T(8,128)(2,1)S(1)}, bf16[1024,256]{1,0:T(8,128)(2,1)S(1)}, u32[]{:S(2)}, u32[]{:S(2)}) collective-permute-start(bf16[1024,256]{1,0:T(8,128)(2,1)S(1)} %slice.151.refs_8_.own_ref), channel_id=1, source_target_pairs={{0,2},{2,0},{1,3},{3,1},{4,6},{6,4},{5,7},{7,5},{8,10},{10,8},{9,1... | collective-permute-start | bytes 1572872 | tf_op jit(solution)/shard_map/ppermute | solution.py:696
  157.4 4.9 %collective-permute-start.13 = (bf16[3,96,128]{2,1,0:T(8,128)(2,1)}, bf16[3,96,128]{2,1,0:T(8,128)(2,1)S(1)}, u32[]{:S(2)}, u32[]{:S(2)}) collective-permute-start(bf16[3,96,128]{2,1,0:T(8,128)(2,1)} %get-tuple-element.123.refs_1_), channel_id=1, source_target_pairs={{0,12},{2,14},{4,0},{6,2},{8,4},{10,6},{12,8},{14,10},{1,13},{3,15... | collective-permute-start | bytes 221192 | tf_op jit(solution)/shard_map/ppermute | solution.py:711
  157.7 12.4 %collective-permute-start.14 = (bf16[3,96,128]{2,1,0:T(8,128)(2,1)}, bf16[3,96,128]{2,1,0:T(8,128)(2,1)S(1)}, u32[]{:S(2)}, u32[]{:S(2)}) collective-permute-start(bf16[3,96,128]{2,1,0:T(8,128)(2,1)} %get-tuple-element.124.refs_2_), channel_id=1, source_target_pairs={{0,8},{2,10},{4,12},{6,14},{8,0},{10,2},{12,4},{14,6},{1,9},{3,11}... | collective-permute-start | bytes 221192 | tf_op jit(solution)/shard_map/ppermute | solution.py:711
  157.7 12.8 %collective-permute-start.15 = (bf16[3,96,128]{2,1,0:T(8,128)(2,1)}, bf16[3,96,128]{2,1,0:T(8,128)(2,1)S(1)}, u32[]{:S(2)}, u32[]{:S(2)}) collective-permute-start(bf16[3,96,128]{2,1,0:T(8,128)(2,1)} %get-tuple-element.125.refs_3_), channel_id=1, source_target_pairs={{0,4},{2,6},{4,8},{6,10},{8,12},{10,14},{12,0},{14,2},{1,5},{3,7},... | collective-permute-start | bytes 221192 | tf_op jit(solution)/shard_map/ppermute | solution.py:711
  159.5 18.4 %collective-permute-start.16 = (bf16[3,96,128]{2,1,0:T(8,128)(2,1)}, bf16[3,96,128]{2,1,0:T(8,128)(2,1)S(1)}, u32[]{:S(2)}, u32[]{:S(2)}) collective-permute-start(bf16[3,96,128]{2,1,0:T(8,128)(2,1)} %get-tuple-element.126.refs_4_), channel_id=1, source_target_pairs={{0,2},{2,0},{4,6},{6,4},{8,10},{10,8},{12,14},{14,12},{1,3},{3,1},... | collective-permute-start | bytes 221192 | tf_op jit(solution)/shard_map/ppermute | solution.py:711
  162.4 15.5 %collective-permute-start.17 = (bf16[3,96,128]{2,1,0:T(8,128)(2,1)}, bf16[3,96,128]{2,1,0:T(8,128)(2,1)S(1)}, u32[]{:S(2)}, u32[]{:S(2)}) collective-permute-start(bf16[3,96,128]{2,1,0:T(8,128)(2,1)} %get-tuple-element.127.refs_5_), channel_id=1, source_target_pairs={{0,14},{2,12},{4,2},{6,0},{8,6},{10,4},{12,10},{14,8},{1,15},{3,13... | collective-permute-start | bytes 221192 | tf_op jit(solution)/shard_map/ppermute | solution.py:711
  170.1 14.6 %collective-permute-start.18 = (bf16[3,96,128]{2,1,0:T(8,128)(2,1)}, bf16[3,96,128]{2,1,0:T(8,128)(2,1)S(1)}, u32[]{:S(2)}, u32[]{:S(2)}) collective-permute-start(bf16[3,96,128]{2,1,0:T(8,128)(2,1)} %get-tuple-element.128.refs_6_), channel_id=1, source_target_pairs={{0,10},{2,8},{4,14},{6,12},{8,2},{10,0},{12,6},{14,4},{1,11},{3,9}... | collective-permute-start | bytes 221192 | tf_op jit(solution)/shard_map/ppermute | solution.py:711
  170.4 14.2 %collective-permute-start.19 = (bf16[3,96,128]{2,1,0:T(8,128)(2,1)}, bf16[3,96,128]{2,1,0:T(8,128)(2,1)S(1)}, u32[]{:S(2)}, u32[]{:S(2)}) collective-permute-start(bf16[3,96,128]{2,1,0:T(8,128)(2,1)} %get-tuple-element.129.refs_7_), channel_id=1, source_target_pairs={{0,6},{2,4},{4,10},{6,8},{8,14},{10,12},{12,2},{14,0},{1,7},{3,5},... | collective-permute-start | bytes 221192 | tf_op jit(solution)/shard_map/ppermute | solution.py:711
  189.8 3.1 collective-permute-start.21
  198.3 15.6 %collective-permute-start.22 = (bf16[288,1024]{1,0:T(8,128)(2,1)}, bf16[288,1024]{1,0:T(8,128)(2,1)S(1)}, u32[]{:S(2)}, u32[]{:S(2)}) collective-permute-start(bf16[288,1024]{1,0:T(8,128)(2,1)} %get-tuple-element.133), channel_id=1, source_target_pairs={{0,2},{2,0},{1,3},{3,1},{4,6},{6,4},{5,7},{7,5},{8,10},{10,8},{9,1... | collective-permute-start | bytes 1769480 | tf_op jit(solution)/shard_map/ppermute | solution.py:696
  213.9 2.0 collective-permute-start.23
  235.4 3.1 collective-permute-start.24
  240.2 15.4 %collective-permute-start.25 = (bf16[288,1024]{1,0:T(8,128)(2,1)S(1)}, bf16[288,1024]{1,0:T(8,128)(2,1)S(1)}, u32[]{:S(2)}, u32[]{:S(2)}) collective-permute-start(bf16[288,1024]{1,0:T(8,128)(2,1)S(1)} %slice.153), channel_id=1, source_target_pairs={{0,2},{2,0},{1,3},{3,1},{4,6},{6,4},{5,7},{7,5},{8,10},{10,8},{9,1... | collective-permute-start | bytes 1769480 | tf_op jit(solution)/shard_map/ppermute | solution.py:696
  257.4 2.8 collective-permute-start.27
  260.8 15.4 %collective-permute-start.28 = (bf16[288,1024]{1,0:T(8,128)(2,1)S(1)}, bf16[288,1024]{1,0:T(8,128)(2,1)S(1)}, u32[]{:S(2)}, u32[]{:S(2)}) collective-permute-start(bf16[288,1024]{1,0:T(8,128)(2,1)S(1)} %slice.155), channel_id=1, source_target_pairs={{0,2},{2,0},{1,3},{3,1},{4,6},{6,4},{5,7},{7,5},{8,10},{10,8},{9,1... | collective-permute-start | bytes 1769480 | tf_op jit(solution)/shard_map/ppermute | solution.py:696
  261.4 15.1 %collective-permute-start.26 = (bf16[288,1024]{1,0:T(8,128)(2,1)S(1)}, bf16[288,1024]{1,0:T(8,128)(2,1)S(1)}, u32[]{:S(2)}, u32[]{:S(2)}) collective-permute-start(bf16[288,1024]{1,0:T(8,128)(2,1)S(1)} %add_convert_fusion.3.near_ref), channel_id=1, source_target_pairs={{0,1},{1,0},{2,3},{3,2},{4,5},{5,4},{6,7},{7,6},{8,9},{9,8},{10,11... | collective-permute-start | bytes 1769480 | tf_op jit(solution)/shard_map/ppermute | solution.py:699
  285.6 15.1 %collective-permute-start.29 = (bf16[288,1024]{1,0:T(8,128)(2,1)S(1)}, bf16[288,1024]{1,0:T(8,128)(2,1)S(1)}, u32[]{:S(2)}, u32[]{:S(2)}) collective-permute-start(bf16[288,1024]{1,0:T(8,128)(2,1)S(1)} %add_convert_fusion.2.near_ref), channel_id=1, source_target_pairs={{0,1},{1,0},{2,3},{3,2},{4,5},{5,4},{6,7},{7,6},{8,9},{9,8},{10,11... | collective-permute-start | bytes 1769480 | tf_op jit(solution)/shard_map/ppermute | solution.py:699
  287.0 9.3 %collective-permute-start.30 = (bf16[3,96,128]{2,1,0:T(8,128)(2,1)S(1)}, bf16[3,96,128]{2,1,0:T(8,128)(2,1)S(1)}, u32[]{:S(2)}, u32[]{:S(2)}) collective-permute-start(bf16[3,96,128]{2,1,0:T(8,128)(2,1)S(1)} %copy-done.61), channel_id=1, source_target_pairs={{0,4},{2,6},{4,8},{6,10},{8,12},{10,14},{12,0},{14,2},{1,5},{3,7},... | collective-permute-start | bytes 221192 | tf_op jit(solution)/shard_map/ppermute | solution.py:711
  287.2 13.5 %collective-permute-start.31 = (bf16[3,96,128]{2,1,0:T(8,128)(2,1)}, bf16[3,96,128]{2,1,0:T(8,128)(2,1)S(1)}, u32[]{:S(2)}, u32[]{:S(2)}) collective-permute-start(bf16[3,96,128]{2,1,0:T(8,128)(2,1)} %get-tuple-element.155), channel_id=1, source_target_pairs={{0,8},{2,10},{4,12},{6,14},{8,0},{10,2},{12,4},{14,6},{1,9},{3,11}... | collective-permute-start | bytes 221192 | tf_op jit(solution)/shard_map/ppermute | solution.py:711
  294.1 18.6 %collective-permute-start.32 = (bf16[3,96,128]{2,1,0:T(8,128)(2,1)S(1)}, bf16[3,96,128]{2,1,0:T(8,128)(2,1)S(1)}, u32[]{:S(2)}, u32[]{:S(2)}) collective-permute-start(bf16[3,96,128]{2,1,0:T(8,128)(2,1)S(1)} %copy-done.58), channel_id=1, source_target_pairs={{0,12},{2,14},{4,0},{6,2},{8,4},{10,6},{12,8},{14,10},{1,13},{3,15... | collective-permute-start | bytes 221192 | tf_op jit(solution)/shard_map/ppermute | solution.py:711
  295.6 18.9 %collective-permute-start.33 = (bf16[3,96,128]{2,1,0:T(8,128)(2,1)S(1)}, bf16[3,96,128]{2,1,0:T(8,128)(2,1)S(1)}, u32[]{:S(2)}, u32[]{:S(2)}) collective-permute-start(bf16[3,96,128]{2,1,0:T(8,128)(2,1)S(1)} %copy-done.56), channel_id=1, source_target_pairs={{0,2},{2,0},{4,6},{6,4},{8,10},{10,8},{12,14},{14,12},{1,3},{3,1},... | collective-permute-start | bytes 221192 | tf_op jit(solution)/shard_map/ppermute | solution.py:711
  296.3 18.2 %collective-permute-start.34 = (bf16[3,96,128]{2,1,0:T(8,128)(2,1)S(1)}, bf16[3,96,128]{2,1,0:T(8,128)(2,1)S(1)}, u32[]{:S(2)}, u32[]{:S(2)}) collective-permute-start(bf16[3,96,128]{2,1,0:T(8,128)(2,1)S(1)} %copy-done.54), channel_id=1, source_target_pairs={{0,6},{2,4},{4,10},{6,8},{8,14},{10,12},{12,2},{14,0},{1,7},{3,5},... | collective-permute-start | bytes 221192 | tf_op jit(solution)/shard_map/ppermute | solution.py:711
  300.7 13.8 %collective-permute-start.35 = (bf16[3,96,128]{2,1,0:T(8,128)(2,1)S(1)}, bf16[3,96,128]{2,1,0:T(8,128)(2,1)}, u32[]{:S(2)}, u32[]{:S(2)}) collective-permute-start(bf16[3,96,128]{2,1,0:T(8,128)(2,1)S(1)} %copy-done.53), channel_id=1, source_target_pairs={{0,10},{2,8},{4,14},{6,12},{8,2},{10,0},{12,6},{14,4},{1,11},{3,9}... | collective-permute-start | bytes 221192 | tf_op jit(solution)/shard_map/ppermute | solution.py:711
  300.8 13.8 %collective-permute-start.36 = (bf16[3,96,128]{2,1,0:T(8,128)(2,1)S(1)}, bf16[3,96,128]{2,1,0:T(8,128)(2,1)S(1)}, u32[]{:S(2)}, u32[]{:S(2)}) collective-permute-start(bf16[3,96,128]{2,1,0:T(8,128)(2,1)S(1)} %copy-done.52), channel_id=1, source_target_pairs={{0,14},{2,12},{4,2},{6,0},{8,6},{10,4},{12,10},{14,8},{1,15},{3,13... | collective-permute-start | bytes 221192 | tf_op jit(solution)/shard_map/ppermute | solution.py:711
  312.7 78.4 %collective-permute-start.46 = (bf16[1024,768]{1,0:T(8,128)(2,1)S(1)}, bf16[1024,768]{1,0:T(8,128)(2,1)}, u32[]{:S(2)}, u32[]{:S(2)}) collective-permute-start(bf16[1024,768]{1,0:T(8,128)(2,1)S(1)} %copy-done.1), channel_id=1, source_target_pairs={{0,2},{2,0},{1,3},{3,1},{4,6},{6,4},{5,7},{7,5},{8,10},{10,8},{9,1... | collective-permute-start | bytes 4718600 | tf_op jit(solution)/shard_map/ppermute | solution.py:696
  341.3 14.3 %collective-permute-start.39 = (bf16[3,288,128]{2,1,0:T(8,128)(2,1)}, bf16[3,288,128]{2,1,0:T(8,128)(2,1)S(1)}, u32[]{:S(2)}, u32[]{:S(2)}) collective-permute-start(bf16[3,288,128]{2,1,0:T(8,128)(2,1)} %get-tuple-element.177), channel_id=1, source_target_pairs={{0,12},{2,14},{4,0},{6,2},{8,4},{10,6},{12,8},{14,10},{1,13},{3,15... | collective-permute-start | bytes 663560 | tf_op jit(solution)/shard_map/ppermute | solution.py:711
  342.6 40.0 %collective-permute-start.37 = (bf16[288,1024]{1,0:T(8,128)(2,1)S(1)}, bf16[288,1024]{1,0:T(8,128)(2,1)}, u32[]{:S(2)}, u32[]{:S(2)}) collective-permute-start(bf16[288,1024]{1,0:T(8,128)(2,1)S(1)} %constant_dynamic-slice_fusion.9), channel_id=1, source_target_pairs={{0,2},{2,0},{1,3},{3,1},{4,6},{6,4},{5,7},{7,5},{8,10},{10,8},{9,1... | collective-permute-start | bytes 1769480 | tf_op jit(solution)/shard_map/ppermute | solution.py:696
  343.8 26.9 %collective-permute-start.40 = (bf16[3,288,128]{2,1,0:T(8,128)(2,1)}, bf16[3,288,128]{2,1,0:T(8,128)(2,1)S(1)}, u32[]{:S(2)}, u32[]{:S(2)}) collective-permute-start(bf16[3,288,128]{2,1,0:T(8,128)(2,1)} %get-tuple-element.178), channel_id=1, source_target_pairs={{0,8},{2,10},{4,12},{6,14},{8,0},{10,2},{12,4},{14,6},{1,9},{3,11}... | collective-permute-start | bytes 663560 | tf_op jit(solution)/shard_map/ppermute | solution.py:711
  346.1 24.6 %collective-permute-start.41 = (bf16[3,288,128]{2,1,0:T(8,128)(2,1)}, bf16[3,288,128]{2,1,0:T(8,128)(2,1)S(1)}, u32[]{:S(2)}, u32[]{:S(2)}) collective-permute-start(bf16[3,288,128]{2,1,0:T(8,128)(2,1)} %get-tuple-element.179), channel_id=1, source_target_pairs={{0,4},{2,6},{4,8},{6,10},{8,12},{10,14},{12,0},{14,2},{1,5},{3,7},... | collective-permute-start | bytes 663560 | tf_op jit(solution)/shard_map/ppermute | solution.py:711
  355.6 16.5 %collective-permute-start.42 = (bf16[3,288,128]{2,1,0:T(8,128)(2,1)}, bf16[3,288,128]{2,1,0:T(8,128)(2,1)}, u32[]{:S(2)}, u32[]{:S(2)}) collective-permute-start(bf16[3,288,128]{2,1,0:T(8,128)(2,1)} %get-tuple-element.180), channel_id=1, source_target_pairs={{0,2},{2,0},{4,6},{6,4},{8,10},{10,8},{12,14},{14,12},{1,3},{3,1},... | collective-permute-start | bytes 663560 | tf_op jit(solution)/shard_map/ppermute | solution.py:711
  370.7 9.3 %collective-permute-start.43 = (bf16[3,288,128]{2,1,0:T(8,128)(2,1)S(1)}, bf16[3,288,128]{2,1,0:T(8,128)(2,1)}, u32[]{:S(2)}, u32[]{:S(2)}) collective-permute-start(bf16[3,288,128]{2,1,0:T(8,128)(2,1)S(1)} %copy-done.44), channel_id=1, source_target_pairs={{0,14},{2,12},{4,2},{6,0},{8,6},{10,4},{12,10},{14,8},{1,15},{3,13... | collective-permute-start | bytes 663560 | tf_op jit(solution)/shard_map/ppermute | solution.py:711
  370.7 20.4 %collective-permute-start.44 = (bf16[3,288,128]{2,1,0:T(8,128)(2,1)}, bf16[3,288,128]{2,1,0:T(8,128)(2,1)}, u32[]{:S(2)}, u32[]{:S(2)}) collective-permute-start(bf16[3,288,128]{2,1,0:T(8,128)(2,1)} %get-tuple-element.182), channel_id=1, source_target_pairs={{0,10},{2,8},{4,14},{6,12},{8,2},{10,0},{12,6},{14,4},{1,11},{3,9}... | collective-permute-start | bytes 663560 | tf_op jit(solution)/shard_map/ppermute | solution.py:711
  372.1 19.0 %collective-permute-start.45 = (bf16[3,288,128]{2,1,0:T(8,128)(2,1)S(1)}, bf16[3,288,128]{2,1,0:T(8,128)(2,1)}, u32[]{:S(2)}, u32[]{:S(2)}) collective-permute-start(bf16[3,288,128]{2,1,0:T(8,128)(2,1)S(1)} %copy-done.42), channel_id=1, source_target_pairs={{0,6},{2,4},{4,10},{6,8},{8,14},{10,12},{12,2},{14,0},{1,7},{3,5},... | collective-permute-start | bytes 663560 | tf_op jit(solution)/shard_map/ppermute | solution.py:711
  380.0 21.7 %collective-permute-start.50 = (bf16[1024,256]{1,0:T(8,128)(2,1)}, bf16[1024,256]{1,0:T(8,128)(2,1)S(1)}, u32[]{:S(2)}, u32[]{:S(2)}) collective-permute-start(bf16[1024,256]{1,0:T(8,128)(2,1)} %get-tuple-element.200), channel_id=1, source_target_pairs={{0,2},{2,0},{1,3},{3,1},{4,6},{6,4},{5,7},{7,5},{8,10},{10,8},{9,1... | collective-permute-start | bytes 1572872 | tf_op jit(solution)/shard_map/ppermute | solution.py:696
  382.6 20.9 %collective-permute-start.38 = (bf16[288,1024]{1,0:T(8,128)(2,1)}, bf16[288,1024]{1,0:T(8,128)(2,1)}, u32[]{:S(2)}, u32[]{:S(2)}) collective-permute-start(bf16[288,1024]{1,0:T(8,128)(2,1)} %collective-permute-done.37.near_ref), channel_id=1, source_target_pairs={{0,1},{1,0},{2,3},{3,2},{4,5},{5,4},{6,7},{7,6},{8,9},{9,8},{10,11... | collective-permute-start | bytes 1769480 | tf_op jit(solution)/shard_map/ppermute | solution.py:699
  397.4 16.8 %collective-permute-start.47 = (bf16[576,1024]{1,0:T(8,128)(2,1)}, bf16[576,1024]{1,0:T(8,128)(2,1)}, u32[]{:S(2)}, u32[]{:S(2)}) collective-permute-start(bf16[576,1024]{1,0:T(8,128)(2,1)} %qkv_back.1.part_ref), channel_id=1, source_target_pairs={{0,1},{1,0},{2,3},{3,2},{4,5},{5,4},{6,7},{7,6},{8,9},{9,8},{10,11... | collective-permute-start | bytes 3538952 | tf_op jit(solution)/shard_map/ppermute | solution.py:699
  402.0 12.1 %collective-permute-start.51 = (bf16[448,512]{1,0:T(8,128)(2,1)S(1)}, bf16[448,512]{1,0:T(8,128)(2,1)S(1)}, u32[]{:S(2)}, u32[]{:S(2)}) collective-permute-start(bf16[448,512]{1,0:T(8,128)(2,1)S(1)} %maximum_maximum_fusion), channel_id=1, source_target_pairs={{0,16},{16,0},{1,17},{17,1},{2,18},{18,2},{3,19},{19,3},{4,20},{20... | collective-permute-start | bytes 1376264 | tf_op jit(solution)/shard_map/ppermute | solution.py:693
  420.4 7.1 %collective-permute-start.55 = (f32[128,128]{1,0:T(8,128)}, f32[128,128]{1,0:T(8,128)S(1)}, u32[]{:S(2)}, u32[]{:S(2)}) collective-permute-start(f32[128,128]{1,0:T(8,128)} %get-tuple-element.206), channel_id=1, source_target_pairs={{0,2},{2,0},{1,3},{3,1},{4,6},{6,4},{5,7},{7,5},{8,10},{10,8},{9,1... | collective-permute-start | bytes 196616 | tf_op jit(solution)/shard_map/ppermute | solution.py:696
  421.6 11.2 %collective-permute-start.54 = (bf16[448,128]{1,0:T(8,128)(2,1)S(1)}, bf16[448,128]{1,0:T(8,128)(2,1)S(1)}, u32[]{:S(2)}, u32[]{:S(2)}) collective-permute-start(bf16[448,128]{1,0:T(8,128)(2,1)S(1)} %pad_maximum_fusion.6), channel_id=1, source_target_pairs={{0,4},{4,8},{8,12},{12,0},{1,5},{5,9},{9,13},{13,1},{2,6},{6,10},{... | collective-permute-start | bytes 344072 | tf_op jit(solution)/shard_map/ppermute | solution.py:693
  421.7 12.6 %collective-permute-start.53 = (bf16[448,128]{1,0:T(8,128)(2,1)S(1)}, bf16[448,128]{1,0:T(8,128)(2,1)S(1)}, u32[]{:S(2)}, u32[]{:S(2)}) collective-permute-start(bf16[448,128]{1,0:T(8,128)(2,1)S(1)} %pad_maximum_fusion.5), channel_id=1, source_target_pairs={{0,8},{4,12},{8,0},{12,4},{1,9},{5,13},{9,1},{13,5},{2,10},{6,14},... | collective-permute-start | bytes 344072 | tf_op jit(solution)/shard_map/ppermute | solution.py:693
  422.7 16.1 %collective-permute-start.52 = (bf16[448,128]{1,0:T(8,128)(2,1)S(1)}, bf16[448,128]{1,0:T(8,128)(2,1)S(1)}, u32[]{:S(2)}, u32[]{:S(2)}) collective-permute-start(bf16[448,128]{1,0:T(8,128)(2,1)S(1)} %pad_maximum_fusion.4), channel_id=1, source_target_pairs={{0,12},{4,0},{8,4},{12,8},{1,13},{5,1},{9,5},{13,9},{2,14},{6,2},{... | collective-permute-start | bytes 344072 | tf_op jit(solution)/shard_map/ppermute | solution.py:693
  425.7 13.1 %collective-permute-start.48 = (bf16[288,1024]{1,0:T(8,128)(2,1)S(1)}, bf16[288,1024]{1,0:T(8,128)(2,1)S(1)}, u32[]{:S(2)}, u32[]{:S(2)}) collective-permute-start(bf16[288,1024]{1,0:T(8,128)(2,1)S(1)} %constant_dynamic-slice_fusion.8), channel_id=1, source_target_pairs={{0,2},{2,0},{1,3},{3,1},{4,6},{6,4},{5,7},{7,5},{8,10},{10,8},{9,1... | collective-permute-start | bytes 1769480 | tf_op jit(solution)/shard_map/ppermute | solution.py:696
  427.4 4.7 %collective-permute-start.56 = (f32[64,384]{1,0:T(8,128)S(1)}, f32[64,384]{1,0:T(8,128)S(1)}, u32[]{:S(2)}, u32[]{:S(2)}) collective-permute-start(f32[64,384]{1,0:T(8,128)S(1)} %slice.160), channel_id=1, source_target_pairs={{0,16},{16,0},{1,17},{17,1},{2,18},{18,2},{3,19},{19,3},{4,20},{20... | collective-permute-start | bytes 294920 | tf_op jit(solution)/shard_map/ppermute | solution.py:693
  432.2 11.6 %collective-permute-start.57 = (f32[16,384]{1,0:T(8,128)S(1)}, f32[16,384]{1,0:T(8,128)S(1)}, u32[]{:S(2)}, u32[]{:S(2)}) collective-permute-start(f32[16,384]{1,0:T(8,128)S(1)} %get-tuple-element.260), channel_id=1, source_target_pairs={{0,12},{4,0},{8,4},{12,8},{1,13},{5,1},{9,5},{13,9},{2,14},{6,2},{... | collective-permute-start | bytes 73736 | tf_op jit(solution)/shard_map/ppermute | solution.py:693
  432.8 11.0 %collective-permute-start.58 = (f32[16,384]{1,0:T(8,128)S(1)}, f32[16,384]{1,0:T(8,128)S(1)}, u32[]{:S(2)}, u32[]{:S(2)}) collective-permute-start(f32[16,384]{1,0:T(8,128)S(1)} %get-tuple-element.262), channel_id=1, source_target_pairs={{0,8},{4,12},{8,0},{12,4},{1,9},{5,13},{9,1},{13,5},{2,10},{6,14},... | collective-permute-start | bytes 73736 | tf_op jit(solution)/shard_map/ppermute | solution.py:693
  434.3 9.5 %collective-permute-start.59 = (f32[16,384]{1,0:T(8,128)S(1)}, f32[16,384]{1,0:T(8,128)S(1)}, u32[]{:S(2)}, u32[]{:S(2)}) collective-permute-start(f32[16,384]{1,0:T(8,128)S(1)} %get-tuple-element.261), channel_id=1, source_target_pairs={{0,4},{4,8},{8,12},{12,0},{1,5},{5,9},{9,13},{13,1},{2,6},{6,10},{... | collective-permute-start | bytes 73736 | tf_op jit(solution)/shard_map/ppermute | solution.py:693
  438.9 6.7 %collective-permute-start.49 = (bf16[288,1024]{1,0:T(8,128)(2,1)S(1)}, bf16[288,1024]{1,0:T(8,128)(2,1)S(1)}, u32[]{:S(2)}, u32[]{:S(2)}) collective-permute-start(bf16[288,1024]{1,0:T(8,128)(2,1)S(1)} %collective-permute-done.48.near_ref), channel_id=1, source_target_pairs={{0,1},{1,0},{2,3},{3,2},{4,5},{5,4},{6,7},{7,6},{8,9},{9,8},{10,11... | collective-permute-start | bytes 1769480 | tf_op jit(solution)/shard_map/ppermute | solution.py:699
  (70 other events, 582.8 us)
Sparse Core Ops, SparseCore 0:
  10.5 87.1 all-gather.2
  99.8 85.7 all-gather.4
  256.1 101.3 reduce-scatter.1
